TPU v7x, 32 devices: a whole 2x2x4 slice. The times are simulated.
32 devices in a mesh: dp: 4 (over z), ctx: 4 (over y, core), tensor: 2 (over x).
Axes of the slice: x: 2, y: 2, z: 4, core: 2. Of those that a mesh axis runs over, the one named last changes fastest.
Arguments:
- tokens: bfloat16 [4096, 1536], P(('dp', 'ctx'), 'tensor'), may hold values from -6 to 6
- segments: int32 [4, 1024], P('dp'), may hold values from 0 to 1, never falling along the last dimension, each value on 1 to 768 neighbouring positions
- order: int32 [4, 1024], P('dp'), may hold values from 0 to 1023, each once within a row
- routes: int32 [4096, 8], P('dp'), may hold values from 0 to 39, all different within a row
- gain_one: float32 [1536], P('tensor'), may hold values from 0.5 to 1.5
- w_query: bfloat16 [1536, 1536], P('dp', 'tensor'), may hold values from -0.15625 to 0.15625
- w_key: bfloat16 [1536, 512], P('dp', 'tensor'), may hold values from -0.15625 to 0.15625
- w_value: bfloat16 [1536, 512], P('dp', 'tensor'), may hold values from -0.15625 to 0.15625
- w_output: bfloat16 [1536, 1536], P('dp', 'tensor'), may hold values from -1.25 to 1.25
- gain_two: float32 [1536], P('tensor'), may hold values from 0.5 to 1.5
- w_router: bfloat16 [1536, 40], P('dp'), may hold values from -0.06982422 to 0.06982422
- w_expert_in: bfloat16 [1536, 40, 1024], P('dp', 'tensor'), may hold values from -0.15625 to 0.15625
- w_expert_out: bfloat16 [1536, 40, 512], P('dp', 'tensor'), may hold values from -0.75 to 0.75
- cotangent: bfloat16 [4096, 1536], P(('dp', 'ctx'), 'tensor'), may hold values from -6 to 6
Outputs:
- output: bfloat16 [4096, 1536], P(('dp', 'ctx'), 'tensor')
- grad_tokens: float32 [4096, 1536], P(('dp', 'ctx'), 'tensor')
- grad_gain_one: float32 [1536], P('tensor')
- grad_query: float32 [1536, 1536], P('dp', 'tensor')
- grad_key: float32 [1536, 512], P('dp', 'tensor')
- grad_value: float32 [1536, 512], P('dp', 'tensor')
- grad_output: float32 [1536, 1536], P('dp', 'tensor')
- grad_gain_two: float32 [1536], P('tensor')
- grad_router: float32 [1536, 40], P('dp')
- grad_expert_in: float32 [1536, 40, 1024], P('dp', 'tensor')
- grad_expert_out: float32 [1536, 40, 512], P('dp', 'tensor')
Inputs may be any that keep to these rules, and one draw needn't show every extreme that they name: `routes`: each row names 8 different experts. `segments`: in each pack the document numbers never fall and each of the 2 documents has at least one token; no document has more than 768 tokens. `order`: each row names every position of its pack once.
All inputs are finite; a program needn't handle non-finite values.
Results may differ from a plain program's by a relative error of at most 0.015.
Values may be sent and summed in bfloat16 or wider, within the bound.
A program may use at most 640 MiB of HBM per device.

v0:
```python
import jax
import jax.numpy as jnp
from jax import lax
from jax.sharding import PartitionSpec as P

D = 1536
HEAD_DIM = 64
EXPERTS = 40
TOP_K = 8
FF = 512


EPS = 1e-06
THETA = 10000.0
NEG = -1e30


def positions(segment_row):
    length = segment_row.shape[0]
    places = jnp.arange(length, dtype=jnp.int32)
    change = jnp.concatenate([jnp.ones((1,), jnp.bool_), segment_row[1:] != segment_row[:-1]])
    starts = lax.cummax(jnp.where(change, places, 0), axis=0)
    return (places - starts).astype(jnp.float32)


def rope_tables(position):
    halves = HEAD_DIM // 2
    frequency = THETA ** (-2.0 * jnp.arange(halves, dtype=jnp.float32) / HEAD_DIM)
    angles = position[:, None] * frequency[None, :]
    return (jnp.cos(angles)[:, None, :], jnp.sin(angles)[:, None, :])


def rotate(values, cosine_table, sine_table):
    halves = values.shape[-1] // 2
    first_half, second_half = (values[..., :halves], values[..., halves:])
    return jnp.concatenate(
        [
            first_half * cosine_table - second_half * sine_table,
            second_half * cosine_table + first_half * sine_table,
        ],
        axis=-1,
    )


def rotate_back(values, cosine_table, sine_table):
    halves = values.shape[-1] // 2
    first_half, second_half = (values[..., :halves], values[..., halves:])
    return jnp.concatenate(
        [
            first_half * cosine_table + second_half * sine_table,
            second_half * cosine_table - first_half * sine_table,
        ],
        axis=-1,
    )


def dispatch(route_rows, first_expert, local_count, capacity):
    flat_routes = route_rows.reshape(-1)
    pairs_total = flat_routes.shape[0]
    experts_all = jnp.arange(EXPERTS, dtype=jnp.int32)
    onehot = (flat_routes[:, None] == experts_all[None, :]).astype(jnp.int32)
    ranking = jnp.sum((jnp.cumsum(onehot, axis=0) - 1) * onehot, axis=1)
    local_expert = flat_routes - first_expert
    usable = (ranking < capacity) & (local_expert >= 0) & (local_expert < local_count)
    pair_slot = jnp.where(usable, local_expert * capacity + ranking, local_count * capacity)
    pair_index = jnp.arange(pairs_total, dtype=jnp.int32)
    slot_pair = (
        jnp.full((local_count * capacity + 1,), pairs_total, jnp.int32)
        .at[pair_slot]
        .set(pair_index)[:-1]
    )
    return (pair_slot, slot_pair)


def full_rows(columns):
    return lax.all_gather(columns, "tensor", axis=1, tiled=True)


def column_share(partial_value):
    return lax.psum_scatter(partial_value, "tensor", scatter_dimension=1, tiled=True)


def row_total(partial_value):
    return lax.psum(partial_value, "tensor")


def norm_forward(columns, gain_part, full_width):
    inverse = lax.rsqrt(row_total(jnp.sum(columns * columns, axis=1)) / full_width + EPS)
    return (inverse, (columns * inverse[:, None] * gain_part[None, :]).astype(jnp.bfloat16))


def norm_backward(columns, gain_part, inverse, grad_normed, full_width):
    weighted = grad_normed * gain_part[None, :]
    inner_sum = row_total(jnp.sum(weighted * columns, axis=1))
    grad_input = (
        weighted * inverse[:, None]
        - columns * (inverse * inverse * inverse * inner_sum / full_width)[:, None]
    )
    grad_gain = jnp.sum(grad_normed * columns * inverse[:, None], axis=0)
    return (grad_input, grad_gain)


def expert_forward(inputs_slot, upper_w, lower_w):
    hidden_pre = jnp.einsum(
        "ecd,def->ecf", inputs_slot, upper_w, preferred_element_type=jnp.float32
    )
    active = (jax.nn.silu(hidden_pre[..., :FF]) * hidden_pre[..., FF:]).astype(jnp.bfloat16)
    output = jnp.einsum("ecf,def->ecd", active, lower_w, preferred_element_type=jnp.float32)
    return (hidden_pre, active, output)


def on_device(
    tokens,
    segments,
    order,
    routes,
    gain_one,
    w_query,
    w_key,
    w_value,
    w_output,
    gain_two,
    w_router,
    w_expert_in,
    w_expert_out,
    cotangent,
):
    n_rows, part_width = tokens.shape
    tensor_at = lax.axis_index("tensor")
    ctx_at = lax.axis_index("ctx")
    order_row = order[0]
    pack_len = order_row.shape[0]
    order_local = lax.dynamic_slice_in_dim(order_row, ctx_at * n_rows, n_rows)
    pack_tokens, pack_cot = (
        lax.all_gather(tokens, "ctx", axis=0, tiled=True),
        lax.all_gather(cotangent, "ctx", axis=0, tiled=True),
    )
    tokens_dealt = pack_tokens[order_local]
    cot_dealt = pack_cot[order_local]
    route_rows = routes[order_local]
    query_w, key_w, value_w, output_w, router_w, upper_w, lower_w = (
        lax.all_gather(w_query, "dp", axis=0, tiled=True),
        lax.all_gather(w_key, "dp", axis=0, tiled=True),
        lax.all_gather(w_value, "dp", axis=0, tiled=True),
        lax.all_gather(w_output, "dp", axis=0, tiled=True),
        lax.all_gather(w_router, "dp", axis=0, tiled=True),
        lax.all_gather(w_expert_in, "dp", axis=0, tiled=True),
        lax.all_gather(w_expert_out, "dp", axis=0, tiled=True),
    )
    q_heads = query_w.shape[1] // HEAD_DIM
    kv_heads = key_w.shape[1] // HEAD_DIM
    group_size = q_heads // kv_heads
    score_scale = HEAD_DIM ** (-0.5)
    segment_row = segments[0]
    place_all = positions(segment_row)
    local_place = place_all[order_local]
    local_segs = segment_row[order_local]
    key_segs = segment_row[order_row]
    cosine_table, sine_table = rope_tables(local_place)
    tokens_f = tokens_dealt.astype(jnp.float32)
    inverse_one, normed_one = norm_forward(tokens_f, gain_one, D)
    h_one = full_rows(normed_one)
    queries = rotate(
        jnp.dot(h_one, query_w, preferred_element_type=jnp.float32).reshape(
            n_rows, q_heads, HEAD_DIM
        ),
        cosine_table,
        sine_table,
    ).astype(jnp.bfloat16)
    key_rows = (
        rotate(
            jnp.dot(h_one, key_w, preferred_element_type=jnp.float32).reshape(
                n_rows, kv_heads, HEAD_DIM
            ),
            cosine_table,
            sine_table,
        )
        .astype(jnp.bfloat16)
        .reshape(n_rows, kv_heads * HEAD_DIM)
    )
    value_rows = jnp.dot(h_one, value_w, preferred_element_type=jnp.float32).astype(jnp.bfloat16)
    key_all, value_all = (
        lax.all_gather(key_rows, "ctx", axis=0, tiled=True),
        lax.all_gather(value_rows, "ctx", axis=0, tiled=True),
    )
    key_heads = key_all.reshape(pack_len, kv_heads, HEAD_DIM)
    value_heads = value_all.reshape(pack_len, kv_heads, HEAD_DIM)
    block_len = min(512, n_rows)
    n_blocks = n_rows // block_len
    query_blocks = queries.reshape(n_blocks, block_len, kv_heads, group_size, HEAD_DIM)
    seg_blocks = local_segs.reshape(n_blocks, block_len)
    index_blocks = order_local.reshape(n_blocks, block_len)

    def block_scores(query_block, seg_block, index_block):
        allowed = (seg_block[:, None] == key_segs[None, :]) & (
            index_block[:, None] >= order_row[None, :]
        )
        scores = score_scale * jnp.einsum(
            "bagd,pad->agbp", query_block, key_heads, preferred_element_type=jnp.float32
        )
        return jnp.where(allowed[None, None], scores, NEG)

    def forward_block(operands):
        query_block, seg_block, index_block = operands
        scores = block_scores(query_block, seg_block, index_block)
        highest = jnp.max(scores, axis=-1, keepdims=True)
        weights = jnp.exp(scores - highest)
        totals = jnp.sum(weights, axis=-1, keepdims=True)
        shares = (weights / totals).astype(jnp.bfloat16)
        blended = jnp.einsum(
            "agbp,pad->bagd", shares, value_heads, preferred_element_type=jnp.float32
        )
        return (blended.astype(jnp.bfloat16), (highest + jnp.log(totals))[..., 0])

    blended_all, log_totals = lax.map(forward_block, (query_blocks, seg_blocks, index_blocks))
    attended = blended_all.reshape(n_rows, q_heads * HEAD_DIM)
    middle = tokens_f + column_share(
        jnp.einsum("nc,dc->nd", attended, output_w, preferred_element_type=jnp.float32)
    )
    inverse_two, normed_two = norm_forward(middle, gain_two, D)
    h_two = full_rows(normed_two)
    logits = jnp.dot(h_two, router_w, preferred_element_type=jnp.float32)
    selector = (
        route_rows[:, :, None] == jnp.arange(EXPERTS, dtype=jnp.int32)[None, None, :]
    ).astype(jnp.float32)
    gate_probs = jax.nn.softmax(jnp.sum(selector * logits[:, None, :], axis=2), axis=-1)
    local_count = upper_w.shape[1]
    capacity = n_rows * 3 // 8
    pair_slot, slot_pair = dispatch(route_rows, tensor_at * local_count, local_count, capacity)
    token_of = slot_pair // TOP_K
    h_pad = jnp.concatenate([h_two, jnp.zeros((1, D), jnp.bfloat16)])
    inputs_slot = h_pad[token_of].reshape(local_count, capacity, D)
    gate_pad = jnp.concatenate([gate_probs.reshape(-1), jnp.zeros((1,), jnp.float32)])
    slot_gate = gate_pad[slot_pair].reshape(local_count, capacity)
    hidden_pre, active, output = expert_forward(inputs_slot, upper_w, lower_w)
    weighted = (slot_gate[:, :, None] * output).reshape(-1, D)
    mixed_rows = jnp.zeros((n_rows + 1, D), jnp.float32).at[token_of].add(weighted)[:n_rows]
    result = (middle + column_share(mixed_rows)).astype(jnp.bfloat16)
    grad_out = cot_dealt.astype(jnp.float32)
    grad_full = full_rows(cot_dealt)
    grad_pad = jnp.concatenate([grad_full, jnp.zeros((1, D), jnp.bfloat16)])
    grad_slots = grad_pad[token_of].reshape(local_count, capacity, D).astype(jnp.float32)
    grad_out_slots = (slot_gate[:, :, None] * grad_slots).astype(jnp.bfloat16)
    gate_grad_slots = jnp.sum(grad_slots * output, axis=-1).reshape(-1)
    grad_active = jnp.einsum(
        "ecd,def->ecf", grad_out_slots, lower_w, preferred_element_type=jnp.float32
    )
    gate_part = hidden_pre[..., :FF]
    up_part = hidden_pre[..., FF:]
    sigmoid_gate = jax.nn.sigmoid(gate_part)
    grad_hidden = jnp.concatenate(
        [
            grad_active * up_part * sigmoid_gate * (1.0 + gate_part * (1.0 - sigmoid_gate)),
            grad_active * gate_part * sigmoid_gate,
        ],
        axis=-1,
    ).astype(jnp.bfloat16)
    grad_lower = jnp.einsum(
        "ecd,ecf->def", grad_out_slots, active, preferred_element_type=jnp.float32
    )
    grad_upper = jnp.einsum(
        "ecd,ecf->def", inputs_slot, grad_hidden, preferred_element_type=jnp.float32
    )
    grad_inputs = jnp.einsum(
        "ecf,def->ecd", grad_hidden, upper_w, preferred_element_type=jnp.float32
    ).reshape(-1, D)
    grad_h_two = jnp.zeros((n_rows + 1, D), jnp.float32).at[token_of].add(grad_inputs)[:n_rows]
    pair_grads = (
        jnp.zeros((n_rows * TOP_K + 1,), jnp.float32)
        .at[slot_pair]
        .add(gate_grad_slots)[:-1]
        .reshape(n_rows, TOP_K)
    )
    gate_grads = row_total(pair_grads)
    chosen_grads = gate_probs * (
        gate_grads - jnp.sum(gate_probs * gate_grads, axis=1, keepdims=True)
    )
    logit_grads = jnp.sum(selector * chosen_grads[:, :, None], axis=1).astype(jnp.bfloat16)
    grad_router = jnp.einsum("nd,ne->de", h_two, logit_grads, preferred_element_type=jnp.float32)
    router_rows = lax.dynamic_slice_in_dim(router_w, tensor_at * part_width, part_width, 0)
    grad_norm_two = column_share(grad_h_two) + jnp.einsum(
        "ne,de->nd", logit_grads, router_rows, preferred_element_type=jnp.float32
    )
    grad_middle, grad_gain_two = norm_backward(middle, gain_two, inverse_two, grad_norm_two, D)
    grad_middle = grad_middle + grad_out
    grad_attn = full_rows(grad_middle.astype(jnp.bfloat16))
    grad_output_w = jnp.einsum("nd,nc->dc", grad_attn, attended, preferred_element_type=jnp.float32)
    grad_blended = jnp.einsum(
        "nd,dc->nc", grad_attn, output_w, preferred_element_type=jnp.float32
    ).astype(jnp.bfloat16)
    grad_blended = grad_blended.reshape(n_blocks, block_len, kv_heads, group_size, HEAD_DIM)

    def backward_block(running, operands):
        grad_keys, grad_values = running
        query_block, seg_block, index_block, log_block, grad_block = operands
        scores = block_scores(query_block, seg_block, index_block)
        shares = jnp.exp(scores - log_block[..., None])
        grad_shares = jnp.einsum(
            "bagd,pad->agbp", grad_block, value_heads, preferred_element_type=jnp.float32
        )
        inner_sum = jnp.sum(shares * grad_shares, axis=-1, keepdims=True)
        grad_scores = (shares * (grad_shares - inner_sum)).astype(jnp.bfloat16)
        grad_query = score_scale * jnp.einsum(
            "agbp,pad->bagd", grad_scores, key_heads, preferred_element_type=jnp.float32
        )
        grad_keys = grad_keys + score_scale * jnp.einsum(
            "agbp,bagd->pad", grad_scores, query_block, preferred_element_type=jnp.float32
        )
        grad_values = grad_values + jnp.einsum(
            "agbp,bagd->pad",
            shares.astype(jnp.bfloat16),
            grad_block,
            preferred_element_type=jnp.float32,
        )
        return ((grad_keys, grad_values), grad_query)

    zero_rows = jnp.zeros((pack_len, kv_heads, HEAD_DIM), jnp.float32)
    (grad_keys, grad_values), grad_queries = lax.scan(
        backward_block,
        (zero_rows, zero_rows),
        (query_blocks, seg_blocks, index_blocks, log_totals, grad_blended),
    )
    grad_key_rows, grad_value_rows = (
        lax.psum_scatter(
            grad_keys.reshape(pack_len, kv_heads * HEAD_DIM), "ctx", scatter_dimension=0, tiled=True
        ),
        lax.psum_scatter(
            grad_values.reshape(pack_len, kv_heads * HEAD_DIM),
            "ctx",
            scatter_dimension=0,
            tiled=True,
        ),
    )
    grad_q = (
        rotate_back(grad_queries.reshape(n_rows, q_heads, HEAD_DIM), cosine_table, sine_table)
        .astype(jnp.bfloat16)
        .reshape(n_rows, q_heads * HEAD_DIM)
    )
    grad_k = (
        rotate_back(grad_key_rows.reshape(n_rows, kv_heads, HEAD_DIM), cosine_table, sine_table)
        .astype(jnp.bfloat16)
        .reshape(n_rows, kv_heads * HEAD_DIM)
    )
    grad_v = grad_value_rows.astype(jnp.bfloat16)
    grad_query_w = jnp.einsum("nd,nc->dc", h_one, grad_q, preferred_element_type=jnp.float32)
    grad_key_w = jnp.einsum("nd,nc->dc", h_one, grad_k, preferred_element_type=jnp.float32)
    grad_value_w = jnp.einsum("nd,nc->dc", h_one, grad_v, preferred_element_type=jnp.float32)
    grad_h_one = jnp.einsum("nc,dc->nd", grad_q, query_w, preferred_element_type=jnp.float32)
    grad_h_one = grad_h_one + jnp.einsum(
        "nc,dc->nd", grad_k, key_w, preferred_element_type=jnp.float32
    )
    grad_h_one = grad_h_one + jnp.einsum(
        "nc,dc->nd", grad_v, value_w, preferred_element_type=jnp.float32
    )
    grad_tokens, grad_gain_one = norm_backward(
        tokens_f, gain_one, inverse_one, column_share(grad_h_one), D
    )
    grad_tokens = grad_tokens + grad_middle
    inverse_order = (
        jnp.zeros((pack_len,), jnp.int32).at[order_row].set(jnp.arange(pack_len, dtype=jnp.int32))
    )
    own_rows = lax.dynamic_slice_in_dim(inverse_order, ctx_at * n_rows, n_rows)
    result_pack = lax.all_gather(result, "ctx", axis=0, tiled=True)
    grad_pack = lax.all_gather(grad_tokens, "ctx", axis=0, tiled=True)
    result_out = result_pack[own_rows]
    grad_tokens_out = grad_pack[own_rows]
    gain_one_out, gain_two_out = lax.psum((grad_gain_one, grad_gain_two), ("dp", "ctx"))
    weight_grads = (
        grad_query_w,
        grad_key_w,
        grad_value_w,
        grad_output_w,
        grad_router,
        grad_upper,
        grad_lower,
    )
    shares_out = (
        lax.psum_scatter(weight_grads[0], ("dp", "ctx"), scatter_dimension=0, tiled=True),
        lax.psum_scatter(weight_grads[1], ("dp", "ctx"), scatter_dimension=0, tiled=True),
        lax.psum_scatter(weight_grads[2], ("dp", "ctx"), scatter_dimension=0, tiled=True),
        lax.psum_scatter(weight_grads[3], ("dp", "ctx"), scatter_dimension=0, tiled=True),
        lax.psum_scatter(weight_grads[4], ("dp", "ctx"), scatter_dimension=0, tiled=True),
        lax.psum_scatter(weight_grads[5], ("dp", "ctx"), scatter_dimension=0, tiled=True),
        lax.psum_scatter(weight_grads[6], ("dp", "ctx"), scatter_dimension=0, tiled=True),
    )
    summed = (
        lax.all_gather(shares_out[0], "ctx", axis=0, tiled=True),
        lax.all_gather(shares_out[1], "ctx", axis=0, tiled=True),
        lax.all_gather(shares_out[2], "ctx", axis=0, tiled=True),
        lax.all_gather(shares_out[3], "ctx", axis=0, tiled=True),
        lax.all_gather(shares_out[4], "ctx", axis=0, tiled=True),
        lax.all_gather(shares_out[5], "ctx", axis=0, tiled=True),
        lax.all_gather(shares_out[6], "ctx", axis=0, tiled=True),
    )
    return (
        result_out,
        grad_tokens_out,
        gain_one_out,
        summed[0],
        summed[1],
        summed[2],
        summed[3],
        gain_two_out,
        summed[4],
        summed[5],
        summed[6],
    )


def solution(mesh):
    return jax.shard_map(
        on_device,
        mesh=mesh,
        in_specs=(
            P(("dp", "ctx"), "tensor"),
            P("dp", None),
            P("dp", None),
            P("dp", None),
            P("tensor"),
            P("dp", "tensor"),
            P("dp", "tensor"),
            P("dp", "tensor"),
            P("dp", "tensor"),
            P("tensor"),
            P("dp", None),
            P("dp", "tensor", None),
            P("dp", "tensor", None),
            P(("dp", "ctx"), "tensor"),
        ),
        out_specs=(
            P(("dp", "ctx"), "tensor"),
            P(("dp", "ctx"), "tensor"),
            P("tensor"),
            P("dp", "tensor"),
            P("dp", "tensor"),
            P("dp", "tensor"),
            P("dp", "tensor"),
            P("tensor"),
            P("dp", None),
            P("dp", "tensor", None),
            P("dp", "tensor", None),
        ),
        check_vma=False,
    )
```

profile of v0, /device:TPU:0, one launch (start us, length us, event | category | flops | bytes accessed | tf_op | source)
XLA Modules:
  0.0 4928.3 jit_solution(7062412815779929809)
XLA Ops:
  11.5 21.5 all_gather.76
  37.8 4.5 gather_fusion.2
  42.4 28.5 all_gather.74
  74.7 5.0 psum.49
  79.9 8.4 all_gather.73
  88.8 7.1 all_gather.77
  96.3 8.2 all_gather.75
  119.4 26.7 all-gather.19.cloned.1.call-done
  153.1 11.3 reduce-window.19
  165.7 8.0 scatter_custom_fusion
  173.8 13.6 all_gather.81
  191.2 10.6 all-gather
  201.9 7.8 gather_fusion.9
  211.3 4.9 psum.50
  217.0 8.6 all_gather.80
  225.6 8.0 gather_fusion.6
  234.1 1006.7 %all-gather.21.cloned.1.call-done = bf16[1536,20,1024]{2,0,1:T(8,128)(2,1)} async-done(((bf16[384,20,1024]{2,0,1:T(8,128)(2,1)}), bf16[1536,20,1024]{2,0,1:T(8,128)(2,1)}) %all-gather.21.cloned.1.call-update) | async-done | bytes 62914576 | tf_op jit(solution)/shard_map/all_gather | solution.py:147
  1240.8 34.9 fusion.71
  1275.7 5.9 multiply_convert_fusion.2
  1281.6 486.1 %all-gather.23.cloned.1.call-done = bf16[1536,20,512]{2,0,1:T(8,128)(2,1)} async-done(((bf16[384,20,512]{2,0,1:T(8,128)(2,1)}), bf16[1536,20,512]{2,0,1:T(8,128)(2,1)}) %all-gather.23.cloned.1.call-update) | async-done | bytes 31457296 | tf_op jit(solution)/shard_map/all_gather | solution.py:148
  1767.7 21.1 fusion.4
  1788.9 14.4 scatter_custom_fusion.4
  1803.5 5.2 psum.51
  1808.9 10.4 gather_fusion.5
  1819.4 19.1 multiply_convert_fusion.1
  1838.5 30.8 fusion.15
  1869.3 22.8 scatter_custom_fusion.3
  1895.5 23.8 reduce-scatter.20.cloned.1.call-done
  1921.5 5.4 psum.52
  1927.8 10.2 all_gather.87
  1940.6 6.9 fusion
  1949.0 4.9 fusion.2
  1953.9 5.8 fusion.16
  1959.8 8.7 fusion.7
  1968.6 4.1 convolution_multiply_fusion
  1974.9 9.8 reduce-scatter.22.cloned.1.call-done
  1988.8 23.7 reduce-scatter.24.cloned.1.call-done
  2015.8 9.7 broadcast_multiply_fusion
  2025.5 22.7 scatter_custom_fusion.1
  2057.3 24.6 convolution_bitcast_fusion.1
  2081.9 70.4 %copy.89 = f32[1536,20,512]{2,1,0:T(8,128)} copy(f32[1536,20,512]{0,2,1:T(8,128)} %convolution_bitcast_fusion.1) | data formatting | bytes 125829120 | tf_op jit(solution)/shard_map/ecd,ecf->def/transpose | solution.py:258
  2153.8 47.7 convolution_bitcast_fusion
  2201.5 147.5 %copy.87 = f32[1536,20,1024]{2,1,0:T(8,128)} copy(f32[1536,20,1024]{0,2,1:T(8,128)} %convolution_bitcast_fusion) | data formatting | bytes 251658240 | tf_op jit(solution)/shard_map/ecd,ecf->def/transpose | solution.py:261
  2359.0 4.9 psum.53
  2369.7 570.1 %reduce-scatter.38.cloned.1.call-done = f32[96,20,512]{2,1,0:T(8,128)} async-done(((f32[1536,20,512]{2,1,0:T(8,128)}), f32[96,20,512]{2,1,0:T(8,128)}) %reduce-scatter.38.cloned.1.call-update) | async-done | bytes 3932176 | tf_op jit(solution)/shard_map/reduce_scatter | solution.py:384
  2939.8 6.5 copy.90
  2946.6 1365.9 %reduce-scatter.36.cloned.1.call-done = f32[96,20,1024]{2,1,0:T(8,128)} async-done(((f32[1536,20,1024]{2,1,0:T(8,128)}), f32[96,20,1024]{2,1,0:T(8,128)}) %reduce-scatter.36.cloned.1.call-update) | async-done | bytes 7864336 | tf_op jit(solution)/shard_map/reduce_scatter | solution.py:383
  4312.5 11.5 copy.88
  4324.0 4.4 scatter_custom_fusion.2
  4328.6 44.6 reduce-scatter.40.cloned.1.call-done
  4374.1 5.3 all-gather.1
  4380.1 55.2 %reduce-scatter.30.cloned.1.call-done = f32[96,256]{1,0:T(8,128)} async-done(((f32[1536,256]{1,0:T(8,128)}), f32[96,256]{1,0:T(8,128)}) %reduce-scatter.30.cloned.1.call-update) | async-done | bytes 98320 | tf_op jit(solution)/shard_map/reduce_scatter | solution.py:379
  4435.3 6.3 all_gather.90
  4441.6 55.9 %reduce-scatter.32.cloned.1.call-done = f32[96,256]{1,0:T(8,128)} async-done(((f32[1536,256]{1,0:T(8,128)}), f32[96,256]{1,0:T(8,128)}) %reduce-scatter.32.cloned.1.call-update) | async-done | bytes 98320 | tf_op jit(solution)/shard_map/reduce_scatter | solution.py:380
  4497.5 6.3 all_gather.91
  4503.9 33.4 all-reduce.2
  4537.3 3.8 gather_fusion.7
  4541.0 15.9 all-gather.33.cloned.1.call-done
  4556.9 30.7 all-gather.29.cloned.1.call-done
  4587.6 4.2 gather_fusion.10
  4591.7 97.8 %all-gather.37.cloned.1.call-done = f32[384,20,512]{2,0,1:T(8,128)} async-done(((f32[96,20,512]{2,0,1:T(8,128)}), f32[384,20,512]{2,0,1:T(8,128)}) %all-gather.37.cloned.1.call-update) | async-done | bytes 15728656 | tf_op jit(solution)/shard_map/all_gather | solution.py:393
  4689.5 191.8 %all-gather.35.cloned.1.call-done = f32[384,20,1024]{2,0,1:T(8,128)} async-done(((f32[96,20,1024]{2,0,1:T(8,128)}), f32[384,20,1024]{2,0,1:T(8,128)}) %all-gather.35.cloned.1.call-update) | async-done | bytes 31457296 | tf_op jit(solution)/shard_map/all_gather | solution.py:392
  4884.8 22.6 copy.115
  4907.4 14.0 copy.116
  (317 shorter events, 95.5 us)
Async XLA Ops:
  7.2 64.0 %copy-start.62 = (s32[1,1024]{1,0:T(1,128)S(1)}, s32[1,1024]{1,0:T(1,128)}, u32[]{:S(2)}) copy-start(s32[1,1024]{1,0:T(1,128)} %param.16) | copy-start | bytes 12292
  7.2 30.7 copy-start
  7.2 35.2 copy-start.41
  7.2 64.3 %all-gather.15.cloned.1.call-start = ((), (), s32[]{:S(2)}) async-start(), calls=%async_computation.13 | async-start | bytes 1966080 | tf_op jit(solution)/shard_map/all_gather | solution.py:135
  7.9 97.9 %all-gather.17.cloned.1.call-start = ((), (), s32[]{:S(2)}) async-start(), calls=%async_computation.14 | async-start | bytes 2949120 | tf_op jit(solution)/shard_map/all_gather | solution.py:142
  8.7 137.4 %all-gather.19.cloned.1.call-start = ((), (), s32[]{:S(2)}) async-start(), calls=%async_computation.15 | async-start | bytes 2949120 | tf_op jit(solution)/shard_map/all_gather | solution.py:145
  9.4 178.6 %all-gather.27.cloned.1.call-start = ((), (), s32[]{:S(2)}) async-start(), calls=%async_computation.21 | async-start | bytes 1966080 | tf_op jit(solution)/shard_map/all_gather | solution.py:136
  10.0 199.6 %reduce-scatter.16.cloned.1.call-start = ((), (), s32[]{:S(2)}) async-start(), calls=%async_computation.16 | async-start | bytes 2359296 | tf_op jit(solution)/shard_map/reduce_scatter | solution.py:80
  10.8 63.8 %copy-start.67 = (s32[1024,1]{0,1:T(1,128)}, s32[1024,1]{0,1:T(1,128)S(1)}, u32[]{:S(2)}) copy-start(s32[1024,1]{0,1:T(1,128)S(1)} %compare_select_fusion.1) | copy-start | bytes 12292
  11.5 139.9 %copy-start.63 = (s32[1024]{0:T(1024)}, s32[1024]{0:T(1024)S(1)}, u32[]{:S(2)}) copy-start(s32[1024]{0:T(1024)S(1)} %pad_clamp_fusion.3) | copy-start | bytes 12292
  33.0 55.3 %copy-start.15 = (bf16[1536,256]{1,0:T(8,128)(2,1)}, bf16[1536,256]{1,0:T(8,128)(2,1)S(1)}, u32[]{:S(2)}) copy-start(bf16[1536,256]{1,0:T(8,128)(2,1)S(1)} %all_gather.76) | copy-start | bytes 2359300
  33.0 46.7 copy-start.52
  70.9 33.6 copy-start.13
  71.1 37.6 copy-start.34
  71.1 37.6 copy-start.36
  74.5 135.1 %copy-start.8 = (bf16[256,768]{1,0:T(8,128)(2,1)}, bf16[256,768]{1,0:T(8,128)(2,1)S(1)}, u32[]{:S(2)}) copy-start(bf16[256,768]{1,0:T(8,128)(2,1)S(1)} %gather_fusion) | copy-start | bytes 1179652
  79.7 29.0 copy-start.69
  79.7 29.0 copy-start.64
  88.3 20.5 copy-start.2
  119.4 30.9 copy-start.29
  149.7 1091.1 %all-gather.21.cloned.1.call-start = ((), (), s32[]{:S(2)}) async-start(), calls=%async_computation.17 | async-start | bytes 78643200 | tf_op jit(solution)/shard_map/all_gather | solution.py:147
  150.3 23.5 copy-start.58
  150.3 1617.3 %all-gather.23.cloned.1.call-start = ((), (), s32[]{:S(2)}) async-start(), calls=%async_computation.18 | async-start | bytes 39321600 | tf_op jit(solution)/shard_map/all_gather | solution.py:148
  151.1 1768.2 %reduce-scatter.20.cloned.1.call-start = ((), (), s32[]{:S(2)}) async-start(), calls=%async_computation.22 | async-start | bytes 2359296 | tf_op jit(solution)/shard_map/reduce_scatter | solution.py:80
  187.4 22.2 copy-start.56
  187.5 22.2 copy-start.46
  191.2 1735.7 %copy-start.19 = (bf16[256,768]{1,0:T(8,128)(2,1)}, bf16[256,768]{1,0:T(8,128)(2,1)S(1)}, u32[]{:S(2)}) copy-start(bf16[256,768]{1,0:T(8,128)(2,1)S(1)} %gather_fusion.8) | copy-start | bytes 1179652
  211.3 1715.6 %copy-start.5 = (f32[256,768]{1,0:T(8,128)}, f32[256,768]{1,0:T(8,128)S(1)}, u32[]{:S(2)}) copy-start(f32[256,768]{1,0:T(8,128)S(1)} %get-tuple-element.111) | copy-start | bytes 2359300
  1767.7 41.3 copy-start.57
  1819.4 19.1 copy-start.39
  1869.2 25.5 copy-start.44
  1869.3 25.6 copy-start.48
  1869.3 50.0 %copy-start.50 = (f32[768]{0:T(1024)S(1)}, f32[768]{0:T(1024)}, u32[]{:S(2)}) copy-start(f32[768]{0:T(1024)} %param.23) | copy-start | bytes 9220
  1869.3 50.0 %copy-start.60 = (f32[256]{0:T(256)S(1)}, f32[256]{0:T(256)}, u32[]{:S(2)}) copy-start(f32[256]{0:T(256)} %copy-done.59) | copy-start | bytes 3076
  1869.3 57.6 %copy-start.71 = (f32[256]{0:T(256)S(1)}, f32[256]{0:T(256)}, u32[]{:S(2)}) copy-start(f32[256]{0:T(256)} %copy-done.70) | copy-start | bytes 3076
  1894.7 89.9 %reduce-scatter.22.cloned.1.call-start = ((), (), s32[]{:S(2)}) async-start(), calls=%async_computation.23 | async-start | bytes 1310720 | tf_op jit(solution)/shard_map/reduce_scatter | solution.py:324
  1895.5 32.3 copy-start.42
  1921.5 19.1 copy-start.17
  1921.5 19.1 copy-start.38
  1959.7 52.7 %reduce-scatter.24.cloned.1.call-start = ((), (), s32[]{:S(2)}) async-start(), calls=%async_computation.24 | async-start | bytes 1310720 | tf_op jit(solution)/shard_map/reduce_scatter | solution.py:327
  1968.5 17.2 copy-start.16
  1968.5 389.1 %reduce-scatter.26.cloned.1.call-start = ((), (), s32[]{:S(2)}) async-start(), calls=%async_computation.25 | async-start | bytes 2359296 | tf_op jit(solution)/shard_map/reduce_scatter | solution.py:80
  1972.7 39.8 copy-start.14
  1974.9 40.9 copy-start.40
  1985.7 39.8 copy-start.31
  2015.6 349.0 %reduce-scatter.18.cloned.1.call-start = ((), (), s32[]{:S(2)}) async-start(), calls=%async_computation.19 | async-start | bytes 2359296 | tf_op jit(solution)/shard_map/reduce_scatter | solution.py:80
  2025.5 25.5 copy-start.3
  2051.0 316.5 %reduce-scatter.28.cloned.1.call-start = ((), (), s32[]{:S(2)}) async-start(), calls=%async_computation.27 | async-start | bytes 5013504 | tf_op jit(solution)/shard_map/reduce_scatter | solution.py:378
  2054.1 314.1 %reduce-scatter.34.cloned.1.call-start = ((), (), s32[]{:S(2)}) async-start(), calls=%async_computation.31 | async-start | bytes 5013504 | tf_op jit(solution)/shard_map/reduce_scatter | solution.py:381
  2057.2 882.6 %reduce-scatter.38.cloned.1.call-start = ((), (), s32[]{:S(2)}) async-start(), calls=%async_computation.35 | async-start | bytes 80216064 | tf_op jit(solution)/shard_map/reduce_scatter | solution.py:384
  2152.3 2160.2 %reduce-scatter.36.cloned.1.call-start = ((), (), s32[]{:S(2)}) async-start(), calls=%async_computation.33 | async-start | bytes 160432128 | tf_op jit(solution)/shard_map/reduce_scatter | solution.py:383
  2349.1 15.5 copy-start.6
  2349.1 2024.0 %reduce-scatter.40.cloned.1.call-start = ((), (), s32[]{:S(2)}) async-start(), calls=%async_computation.37 | async-start | bytes 835584
  2352.3 2083.0 %reduce-scatter.30.cloned.1.call-start = ((), (), s32[]{:S(2)}) async-start(), calls=%async_computation.29 | async-start | bytes 1671168 | tf_op jit(solution)/shard_map/reduce_scatter | solution.py:379
  2355.0 2142.6 %reduce-scatter.32.cloned.1.call-start = ((), (), s32[]{:S(2)}) async-start(), calls=%async_computation.30 | async-start | bytes 1671168 | tf_op jit(solution)/shard_map/reduce_scatter | solution.py:380
  2357.5 2179.7 %all-gather.25.cloned.1.call-start = ((), (), s32[]{:S(2)}) async-start(), calls=%async_computation.20 | async-start | bytes 1966080 | tf_op jit(solution)/shard_map/all_gather | solution.py:363
  2367.4 2173.6 %all-gather.31.cloned.1.call-start = ((), (), s32[]{:S(2)}) async-start(), calls=%async_computation.28 | async-start | bytes 1474560 | tf_op jit(solution)/shard_map/all_gather | solution.py:387
  2368.2 2188.7 %all-gather.33.cloned.1.call-start = ((), (), s32[]{:S(2)}) async-start(), calls=%async_computation.32 | async-start | bytes 1474560 | tf_op jit(solution)/shard_map/all_gather | solution.py:390
  2368.9 2218.6 %all-gather.29.cloned.1.call-start = ((), (), s32[]{:S(2)}) async-start(), calls=%async_computation.26 | async-start | bytes 3932160 | tf_op jit(solution)/shard_map/all_gather | solution.py:364
  2369.6 2319.9 %all-gather.37.cloned.1.call-start = ((), (), s32[]{:S(2)}) async-start(), calls=%async_computation.36 | async-start | bytes 19660800 | tf_op jit(solution)/shard_map/all_gather | solution.py:393
  2946.3 1934.9 %all-gather.35.cloned.1.call-start = ((), (), s32[]{:S(2)}) async-start(), calls=%async_computation.34 | async-start | bytes 39321600 | tf_op jit(solution)/shard_map/all_gather | solution.py:392
  4324.0 179.9 %copy-start.66 = (f32[768]{0:T(1024)S(1)}, f32[768]{0:T(1024)}, u32[]{:S(2)}) copy-start(f32[768]{0:T(1024)} %get-tuple-element.102) | copy-start | bytes 9220
  4541.0 340.3 %copy-start.32 = (f32[384,768]{1,0:T(8,128)S(1)}, f32[384,768]{1,0:T(8,128)}, u32[]{:S(2)}) copy-start(f32[384,768]{1,0:T(8,128)} %all-gather.31.cloned.1.call-done) | copy-start | bytes 3538948
  4556.9 326.9 %copy-start.33 = (f32[384,768]{1,0:T(8,128)S(1)}, f32[384,768]{1,0:T(8,128)}, u32[]{:S(2)}) copy-start(f32[384,768]{1,0:T(8,128)} %all-gather.33.cloned.1.call-done) | copy-start | bytes 3538948
  (36 other events, 241.5 us)
Sparse Core Ops, SparseCore 0:
  9.6 22.3 all-gather.14
  33.5 61.9 all-gather.16
  97.1 48.8 all-gather.18
  147.5 18.4 all-gather.26
  168.6 27.3 reduce-scatter.15
  197.4 1043.3 all-gather.20
  1242.4 525.2 all-gather.22
  1894.9 24.3 reduce-scatter.19
  1959.8 24.8 reduce-scatter.21
  1987.6 24.7 reduce-scatter.23
  2015.7 26.1 reduce-scatter.25
  2051.1 26.1 reduce-scatter.17
  2081.7 75.5 reduce-scatter.27
  2161.6 74.7 reduce-scatter.33
  2240.5 699.2 reduce-scatter.37
  2943.9 1368.6 reduce-scatter.35
  4316.5 56.6 reduce-scatter.39
  4376.7 58.5 reduce-scatter.29
  4439.0 58.5 reduce-scatter.31
  4499.5 19.0 all-gather.24
  4520.1 17.6 all-gather.30
  4539.3 17.4 all-gather.32
  4559.0 28.4 all-gather.28
  4589.6 99.9 all-gather.36
  4691.7 189.5 all-gather.34
where the time goes:
time: 4940 us; the launch traced here: 4930 us
  waiting for transfers between devices  4010 us (81%)
  local copies, waits for them, and re-layouts  356 us (7%)
  matrix products  243 us (5%)
  blocking collectives  193 us (4%)
  other arithmetic  108 us (2%)
    reduce_scatter x1, waiting for transfers between devices, on_device(): lax.psum_scatter(weight_grads[5], ('dp', 'ctx'), scatter_dimension=0, til...  1370 us
    all_gather x1, waiting for transfers between devices, on_device(): lax.all_gather(w_expert_in, 'dp', axis=0, tiled=True)  1010 us
    reduce_scatter x1, waiting for transfers between devices, on_device(): lax.psum_scatter(weight_grads[6], ('dp', 'ctx'), scatter_dimension=0, til...  570 us
    all_gather x1, waiting for transfers between devices, on_device(): lax.all_gather(w_expert_out, 'dp', axis=0, tiled=True)  486 us
    all_gather x1, waiting for transfers between devices, on_device(): lax.all_gather(shares_out[5], 'ctx', axis=0, tiled=True)  192 us
    transpose x1, local copies, waits for them, and re-layouts, on_device(): jnp.einsum('ecd,ecf->def', inputs_slot, grad_hidden, preferred_element_ty...  148 us
  transfers between devices with their start and end apart: 25, of which 15 were waited for; matrix products, arithmetic and copies ran while one was open for 10% of the time, Pallas kernels for 0%

commit v1 on v0

v1 whole, which is shorter than its diff:
```python
import jax
import jax.numpy as jnp
from jax import lax
from jax.sharding import PartitionSpec as P

D = 1536
HEAD_DIM = 64
EXPERTS = 40
TOP_K = 8
FF = 512
EPS = 1e-06
THETA = 10000.0
NEG = -1e30
LANES = 128
ALL = ("dp", "ctx", "tensor")
BF = jnp.bfloat16
F32 = jnp.float32


def rope_tables(position):
    halves = HEAD_DIM // 2
    frequency = THETA ** (-2.0 * jnp.arange(halves, dtype=F32) / HEAD_DIM)
    angles = position[:, None] * frequency[None, :]
    return (jnp.cos(angles)[:, None, :], jnp.sin(angles)[:, None, :])


def rotate(values, cosine_table, sine_table):
    halves = values.shape[-1] // 2
    first_half, second_half = (values[..., :halves], values[..., halves:])
    return jnp.concatenate(
        [
            first_half * cosine_table - second_half * sine_table,
            second_half * cosine_table + first_half * sine_table,
        ],
        axis=-1,
    )


def dot(a, b, dims):
    return lax.dot_general(a, b, (dims, ((), ())), preferred_element_type=F32)


def norm_forward(rows, gain):
    inverse = lax.rsqrt(jnp.mean(rows * rows, axis=1, keepdims=True) + EPS)
    return (inverse, (rows * inverse * gain[None, :]).astype(BF))


def norm_backward(rows, gain, inverse, grad_normed):
    weighted = grad_normed * gain[None, :]
    inner = jnp.sum(weighted * rows, axis=1, keepdims=True)
    grad_rows = weighted * inverse - rows * (inverse * inverse * inverse * inner / D)
    return (grad_rows, jnp.sum(grad_normed * rows * inverse, axis=0))


def exchange(parts, at, count):
    result = lax.dynamic_update_index_in_dim(
        jnp.zeros_like(parts), lax.dynamic_index_in_dim(parts, at, 0), at, 0
    )
    for hop in range(1, count):
        sent = lax.dynamic_index_in_dim(parts, (at + hop) % count, 0)
        got = lax.ppermute(sent, "dp", [(i, (i + hop) % count) for i in range(count)])
        result = lax.dynamic_update_index_in_dim(result, got, (at - hop) % count, 0)
    return result


def on_device(
    tokens,
    segments,
    order,
    routes,
    gain_one,
    w_query,
    w_key,
    w_value,
    w_output,
    gain_two,
    w_router,
    w_expert_in,
    w_expert_out,
    cotangent,
):
    nd, nc, nt = (lax.axis_size("dp"), lax.axis_size("ctx"), lax.axis_size("tensor"))
    dp_at, ctx_at, tensor_at = (
        lax.axis_index("dp"),
        lax.axis_index("ctx"),
        lax.axis_index("tensor"),
    )
    n_rows, part_width = tokens.shape
    sub = n_rows // nt
    pack_len = order.shape[1]
    d_local = w_query.shape[0]
    q_width, kv_width = (w_query.shape[1], w_key.shape[1])
    q_heads, kv_heads = (q_width // HEAD_DIM, kv_width // HEAD_DIM)
    group = q_heads // kv_heads
    qkv_width = q_width + 2 * kv_width
    local_count = w_expert_in.shape[1]
    capacity = n_rows * 3 // 8

    gains = lax.all_gather(jnp.stack([gain_one, gain_two]), "tensor", axis=1, tiled=True)
    gain_one_full, gain_two_full = (gains[0], gains[1])
    tokens_full = lax.all_gather(tokens, "tensor", axis=1, tiled=True)
    packed = jnp.concatenate([w_query, w_key, w_value, w_router], axis=1)
    share = d_local // nc
    packed = lax.dynamic_slice_in_dim(packed, ctx_at * share, share, 0)
    packed = lax.all_gather(packed, ("dp", "ctx"), axis=0, tiled=True)
    qkv_w, router_w = (packed[:, :qkv_width], packed[:, qkv_width:])
    output_w = lax.all_gather(
        lax.dynamic_slice_in_dim(w_output, ctx_at * share, share, 0),
        ("dp", "ctx"),
        axis=0,
        tiled=True,
    )
    cot_sub = lax.all_to_all(cotangent, "tensor", 0, 1, tiled=True)
    cot_all = lax.all_gather(cot_sub, ALL, axis=0, tiled=True)
    tokens_sub = lax.dynamic_slice_in_dim(tokens_full, tensor_at * sub, sub, 0).astype(F32)

    by_expert = local_count % nc == 0
    own_count = local_count // nc if by_expert else local_count
    units = FF // nd if by_expert else FF // (nd * nc)
    first_expert = tensor_at * local_count + (ctx_at * own_count if by_expert else 0)
    if by_expert:
        own_in = lax.dynamic_slice_in_dim(w_expert_in, ctx_at * own_count, own_count, 1)
        own_out = lax.dynamic_slice_in_dim(w_expert_out, ctx_at * own_count, own_count, 1)
        own_in = own_in.reshape(d_local, own_count, 2, nd, units)
        own_out = own_out.reshape(d_local, own_count, nd, units)
    else:
        own_in = w_expert_in.reshape(d_local, own_count, 2, nd, nc, units)
        own_out = w_expert_out.reshape(d_local, own_count, nd, nc, units)
        own_in = lax.dynamic_index_in_dim(own_in, ctx_at, 4, False)
        own_out = lax.dynamic_index_in_dim(own_out, ctx_at, 3, False)
    own_in = jnp.transpose(own_in, (3, 0, 2, 1, 4)).reshape(nd, d_local, 2 * own_count * units)
    own_out = jnp.transpose(own_out, (2, 0, 1, 3)).reshape(nd, d_local, own_count * units)
    width = own_count * units
    expert_w = exchange(jnp.concatenate([own_in, own_out], axis=2), dp_at, nd)
    expert_w = expert_w.reshape(D, 3 * width)
    upper_w, lower_w = (expert_w[:, : 2 * width], expert_w[:, 2 * width :])

    order_row = order[0]
    places = jnp.arange(pack_len, dtype=jnp.int32)
    dealt = jnp.sum(jnp.where(order_row[:, None] == places[None, :], places[:, None], 0), axis=0)
    sub_start = ctx_at * n_rows + tensor_at * sub
    dealt_sub = lax.dynamic_slice_in_dim(dealt, sub_start, sub)
    experts_all = jnp.arange(EXPERTS, dtype=jnp.int32)
    uses = jnp.any(routes[:, :, None] == experts_all[None, None, :], axis=1)
    earlier = (dealt_sub[:, None] // n_rows == dealt[None, :] // n_rows) & (
        dealt[None, :] < dealt_sub[:, None]
    )
    ranks = dot(earlier.astype(BF), uses.astype(BF), ((1,), (0,)))
    uses_sub = lax.dynamic_slice_in_dim(uses, sub_start, sub, 0)
    kept = (uses_sub & (ranks < capacity)).astype(F32)

    segment_row = segments[0]
    local_segs = lax.dynamic_slice_in_dim(segment_row, ctx_at * n_rows, n_rows)
    local_places = ctx_at * n_rows + jnp.arange(n_rows, dtype=jnp.int32)
    starts = jnp.sum((segment_row[None, :] < local_segs[:, None]).astype(jnp.int32), axis=1)
    cosine_table, sine_table = rope_tables((local_places - starts).astype(F32))
    _, h_one = norm_forward(tokens_full.astype(F32), gain_one_full)
    projected = dot(h_one, qkv_w, ((1,), (0,)))
    turned = rotate(
        projected[:, : q_width + kv_width].reshape(n_rows, q_heads + kv_heads, HEAD_DIM),
        cosine_table,
        sine_table,
    ).astype(BF)
    queries = turned[:, :q_heads].reshape(n_rows, kv_heads, group, HEAD_DIM)
    kv_rows = jnp.concatenate(
        [
            turned[:, q_heads:].reshape(n_rows, kv_width),
            projected[:, q_width + kv_width :].astype(BF),
        ],
        axis=1,
    )
    kv_all = lax.all_gather(kv_rows, "ctx", axis=0, tiled=True)
    key_heads = kv_all[:, :kv_width].reshape(pack_len, kv_heads, HEAD_DIM)
    value_heads = kv_all[:, kv_width:].reshape(pack_len, kv_heads, HEAD_DIM)
    allowed = (local_segs[:, None] == segment_row[None, :]) & (
        local_places[:, None] >= places[None, :]
    )
    score_scale = HEAD_DIM ** (-0.5)
    scores = score_scale * jnp.einsum(
        "bagd,pad->agbp", queries, key_heads, preferred_element_type=F32
    )
    scores = jnp.where(allowed[None, None], scores, NEG)
    highest = jnp.max(scores, axis=-1, keepdims=True)
    weights = jnp.exp(scores - highest)
    totals = jnp.sum(weights, axis=-1, keepdims=True)
    shares_low = (weights / totals).astype(BF)
    log_totals = highest + jnp.log(totals)
    attended = (
        jnp.einsum("agbp,pad->bagd", shares_low, value_heads, preferred_element_type=F32)
        .astype(BF)
        .reshape(n_rows, q_width)
    )
    attended_sub = lax.all_to_all(attended, "tensor", 0, 1, tiled=True)
    output_full = lax.all_gather(output_w, "tensor", axis=1, tiled=True)
    middle = tokens_sub + dot(attended_sub, output_full, ((1,), (1,)))

    inverse_two, h_two = norm_forward(middle, gain_two_full)
    logits = jnp.where(uses_sub, dot(h_two, router_w, ((1,), (0,))), NEG)
    raised = jnp.exp(logits - jnp.max(logits, axis=1, keepdims=True))
    gates = raised / jnp.sum(raised, axis=1, keepdims=True)
    gates_kept = gates * kept
    gates_high = gates_kept.astype(BF)
    gates_low = (gates_kept - gates_high.astype(F32)).astype(BF)
    extra = jnp.zeros((sub, LANES - 2 * EXPERTS), BF)
    h_all = lax.all_gather(
        jnp.concatenate([h_two, gates_high, gates_low, extra], axis=1), ALL, axis=0, tiled=True
    )
    gates_all = (
        h_all[:, D : D + EXPERTS].astype(F32) + h_all[:, D + EXPERTS : D + 2 * EXPERTS].astype(F32)
    )
    total_rows = h_all.shape[0]
    gates_own = lax.dynamic_slice_in_dim(gates_all, first_expert, own_count, 1)
    h_all = h_all[:, :D]

    gate_wide = jnp.broadcast_to(gates_own[:, :, None], (total_rows, own_count, units)).reshape(
        total_rows, width
    )
    hidden = dot(h_all, upper_w, ((1,), (0,)))
    grad_raw = dot(cot_all, lower_w, ((1,), (0,)))
    gate_part, up_part = (hidden[:, :width], hidden[:, width:])
    sigmoid = jax.nn.sigmoid(gate_part)
    silu = gate_part * sigmoid
    active = (silu * up_part).astype(BF).astype(F32)
    active_gated = (active * gate_wide).astype(BF)
    grad_gates = jnp.sum((grad_raw * active).reshape(total_rows, own_count, units), axis=2)
    grad_active = grad_raw * gate_wide
    grad_hidden = jnp.concatenate(
        [
            grad_active * up_part * sigmoid * (1.0 + gate_part * (1.0 - sigmoid)),
            grad_active * silu,
        ],
        axis=1,
    ).astype(BF)
    grad_in = dot(grad_hidden, upper_w, ((1,), (1,))).astype(BF)
    grad_gates = lax.dynamic_update_slice_in_dim(
        jnp.zeros((total_rows, LANES), BF), grad_gates.astype(BF), first_expert, 1
    )
    mixed = dot(active_gated, lower_w, ((1,), (1,))).astype(BF)
    back_sub = lax.psum_scatter(
        jnp.concatenate([grad_in, grad_gates], axis=1), ALL, scatter_dimension=0, tiled=True
    ).astype(F32)
    mixed_sub = lax.psum_scatter(mixed, ALL, scatter_dimension=0, tiled=True).astype(F32)
    grad_upper = dot(h_all, grad_hidden, ((0,), (0,))).astype(BF)
    grad_lower = dot(cot_all, active_gated, ((0,), (0,))).astype(BF)
    grad_expert = jnp.concatenate([grad_upper, grad_lower], axis=1).reshape(nd, d_local, 3 * width)
    grad_expert = exchange(grad_expert, dp_at, nd)
    grad_expert = lax.all_gather(grad_expert, "ctx", axis=0)
    grad_up = grad_expert[..., : 2 * width].reshape(nc, nd, d_local, 2, own_count, units)
    grad_low = grad_expert[..., 2 * width :].reshape(nc, nd, d_local, own_count, units)
    if by_expert:
        grad_up = jnp.transpose(grad_up, (2, 0, 4, 3, 1, 5))
        grad_low = jnp.transpose(grad_low, (2, 0, 3, 1, 4))
    else:
        grad_up = jnp.transpose(grad_up, (2, 4, 3, 1, 0, 5))
        grad_low = jnp.transpose(grad_low, (2, 3, 1, 0, 4))
    grad_expert_in = grad_up.reshape(d_local, local_count, 2 * FF).astype(F32)
    grad_expert_out = grad_low.reshape(d_local, local_count, FF).astype(F32)

    result = lax.all_to_all((middle + mixed_sub).astype(BF), "tensor", 1, 0, tiled=True)

    gate_grads = back_sub[:, D : D + EXPERTS] * kept
    logit_grads = (
        gates * (gate_grads - jnp.sum(gates * gate_grads, axis=1, keepdims=True))
    ).astype(BF)
    grad_norm_two = back_sub[:, :D] + dot(logit_grads, router_w, ((1,), (1,)))
    grad_middle, grad_gain_two = norm_backward(middle, gain_two_full, inverse_two, grad_norm_two)
    grad_middle = grad_middle + cot_sub.astype(F32)
    extra = jnp.zeros((sub, LANES - EXPERTS), BF)
    grad_attn = lax.all_gather(
        jnp.concatenate([grad_middle.astype(BF), logit_grads, extra], axis=1),
        "tensor",
        axis=0,
        tiled=True,
    )
    logit_grads_full = grad_attn[:, D : D + EXPERTS]
    grad_attn = grad_attn[:, :D]
    h_two_full = lax.dynamic_slice_in_dim(h_all, (dp_at * nc + ctx_at) * n_rows, n_rows, 0)
    grad_router = dot(h_two_full, logit_grads_full, ((0,), (0,)))

    grad_output_w = dot(grad_attn, attended, ((0,), (0,)))
    grad_blended = (
        dot(grad_attn, output_w, ((1,), (0,)))
        .astype(BF)
        .reshape(n_rows, kv_heads, group, HEAD_DIM)
    )
    shares = jnp.exp(scores - log_totals)
    grad_shares = jnp.einsum(
        "bagd,pad->agbp", grad_blended, value_heads, preferred_element_type=F32
    )
    inner = jnp.sum(shares * grad_shares, axis=-1, keepdims=True)
    grad_scores = (shares * (grad_shares - inner)).astype(BF)
    grad_queries = score_scale * jnp.einsum(
        "agbp,pad->bagd", grad_scores, key_heads, preferred_element_type=F32
    )
    grad_keys = score_scale * jnp.einsum(
        "agbp,bagd->pad", grad_scores, queries, preferred_element_type=F32
    )
    grad_values = jnp.einsum(
        "agbp,bagd->pad", shares_low, grad_blended, preferred_element_type=F32
    )
    grad_kv = lax.psum_scatter(
        jnp.concatenate(
            [grad_keys.reshape(pack_len, kv_width), grad_values.reshape(pack_len, kv_width)],
            axis=1,
        ).astype(BF),
        "ctx",
        scatter_dimension=0,
        tiled=True,
    ).astype(F32)
    grad_turned = jnp.concatenate(
        [
            grad_queries.reshape(n_rows, q_heads, HEAD_DIM),
            grad_kv[:, :kv_width].reshape(n_rows, kv_heads, HEAD_DIM),
        ],
        axis=1,
    )
    grad_qkv = jnp.concatenate(
        [
            rotate(grad_turned, cosine_table, -sine_table)
            .astype(BF)
            .reshape(n_rows, q_width + kv_width),
            grad_kv[:, kv_width:].astype(BF),
        ],
        axis=1,
    )
    qkv_full = lax.all_gather(qkv_w, "tensor", axis=1, tiled=True)
    grad_qkv_sub = lax.all_to_all(grad_qkv, "tensor", 0, 1, tiled=True)
    grad_norm_one = dot(grad_qkv_sub, qkv_full, ((1,), (1,)))
    inverse_sub = lax.rsqrt(jnp.mean(tokens_sub * tokens_sub, axis=1, keepdims=True) + EPS)
    grad_tokens, grad_gain_one = norm_backward(
        tokens_sub, gain_one_full, inverse_sub, grad_norm_one
    )
    grad_tokens = lax.all_to_all(grad_tokens + grad_middle, "tensor", 1, 0, tiled=True)

    grad_qkv_w = dot(h_one, grad_qkv, ((0,), (0,)))
    weight_grads = jnp.concatenate([grad_qkv_w, grad_output_w, grad_router], axis=1).astype(BF)
    weight_grads = lax.psum_scatter(weight_grads, ("dp", "ctx"), scatter_dimension=0, tiled=True)
    weight_grads = lax.all_gather(weight_grads, "ctx", axis=0, tiled=True).astype(F32)
    edges = [0, q_width, q_width + kv_width, qkv_width, qkv_width + q_width]
    gain_grads = lax.psum(jnp.stack([grad_gain_one, grad_gain_two]), ALL)
    gain_grads = lax.dynamic_slice_in_dim(gain_grads, tensor_at * part_width, part_width, 1)
    return (
        result,
        grad_tokens,
        gain_grads[0],
        weight_grads[:, edges[0] : edges[1]],
        weight_grads[:, edges[1] : edges[2]],
        weight_grads[:, edges[2] : edges[3]],
        weight_grads[:, edges[3] : edges[4]],
        gain_grads[1],
        weight_grads[:, edges[4] :],
        grad_expert_in,
        grad_expert_out,
    )


def solution(mesh):
    return jax.shard_map(
        on_device,
        mesh=mesh,
        in_specs=(
            P(("dp", "ctx"), "tensor"),
            P("dp", None),
            P("dp", None),
            P("dp", None),
            P("tensor"),
            P("dp", "tensor"),
            P("dp", "tensor"),
            P("dp", "tensor"),
            P("dp", "tensor"),
            P("tensor"),
            P("dp", None),
            P("dp", "tensor", None),
            P("dp", "tensor", None),
            P(("dp", "ctx"), "tensor"),
        ),
        out_specs=(
            P(("dp", "ctx"), "tensor"),
            P(("dp", "ctx"), "tensor"),
            P("tensor"),
            P("dp", "tensor"),
            P("dp", "tensor"),
            P("dp", "tensor"),
            P("dp", "tensor"),
            P("tensor"),
            P("dp", None),
            P("dp", "tensor", None),
            P("dp", "tensor", None),
        ),
        check_vma=False,
    )
```

time: 4940 us -> 1750 us (0.35)
  waiting for transfers between devices: 4010 us -> 1080 us
  blocking collectives: 193 us -> 89.2 us
  local copies, waits for them, and re-layouts: 356 us -> 268 us
  matrix products: 243 us -> 171 us
    reduce_scatter x12 -> x2, waiting for transfers between devices: 2100 us -> 57.4 us  [the longest x1 57.4 us: on_device(): lax.psum_scatter(weight_grads, ('dp', 'ctx'), scatter_dimension=0, tiled=...]
    all_gather x12 -> x9, waiting for transfers between devices: 1860 us -> 466 us  [the longest x1 103 us: on_device(): cot_all = lax.all_gather(cot_sub, ALL, axis=0, tiled=True)]
    unnamed x26 -> x15, waiting for transfers between devices: 50.7 us -> 318 us
    ppermute x0 -> x6, waiting for transfers between devices: none -> 236 us  [exchange(): lax.ppermute(sent, 'dp', [(i, (i + hop) % count) for i in range(count)])]
    transpose x2, local copies, waits for them, and re-layouts: 218 us -> 7.81 us  [the longest x1 4.72 us: on_device(): jnp.transpose(own_in, (3, 0, 2, 1, 4))]
    all_gather x12 -> x3, blocking collectives: 135 us -> 29.2 us  [the longest x1 13.2 us: on_device(): lax.all_gather(jnp.concatenate([grad_middle.astype(BF), logit_grads, extr...]
    unnamed x159 -> x103, local copies, waits for them, and re-layouts: 49.3 us -> 133 us
    dot_general x26 -> x22, matrix products: 241 us -> 171 us  [the longest x16 148 us: dot(): return lax.dot_general(a, b, (dims, ((), ())), preferred_element_type=F32)]
  transfers between devices with their start and end apart: 25 -> 23, of which waited for: 15 -> 16; matrix products, arithmetic and copies ran while one was open for 10% -> 21% of each run, Pallas kernels for 0% -> 0%
where the time goes in v1:
time: 1750 us; the launch traced here: 1730 us
  waiting for transfers between devices  1080 us (62%)
  local copies, waits for them, and re-layouts  268 us (15%)
  matrix products  171 us (10%)
  blocking collectives  89.2 us (5%)
  other arithmetic  80.6 us (5%)
  starting transfers between devices  26 us (1%)
    unnamed x15, waiting for transfers between devices  318 us
    ppermute x6, waiting for transfers between devices, exchange(): lax.ppermute(sent, 'dp', [(i, (i + hop) % count) for i in range(count)])  236 us
    dot_general x16, matrix products, dot(): return lax.dot_general(a, b, (dims, ((), ())), preferred_element_type=F32)  148 us
    unnamed x103, local copies, waits for them, and re-layouts  133 us
    all_gather x1, waiting for transfers between devices, on_device(): cot_all = lax.all_gather(cot_sub, ALL, axis=0, tiled=True)  103 us
    all_gather x1, waiting for transfers between devices, on_device(): qkv_full = lax.all_gather(qkv_w, 'tensor', axis=1, tiled=True)  97.2 us
    all_gather x1, waiting for transfers between devices, on_device(): grad_expert = lax.all_gather(grad_expert, 'ctx', axis=0)  82.5 us
    reduce_scatter x1, waiting for transfers between devices, on_device(): lax.psum_scatter(weight_grads, ('dp', 'ctx'), scatter_dimension=0, tiled=...  57.4 us
  transfers between devices with their start and end apart: 23, of which 16 were waited for; matrix products, arithmetic and copies ran while one was open for 21% of the time, Pallas kernels for 0%

profile of v1, /device:TPU:0, one launch (start us, length us, event | category | flops | bytes accessed | tf_op | source)
XLA Modules:
  0.0 1732.6 jit_solution(15310656353392868599)
XLA Ops:
  13.2 5.3 all_gather.48
  20.2 10.7 all_gather.47
  31.9 32.8 %all-gather.10.cloned.1.call-done = bf16[1536,1320]{1,0:T(8,128)(2,1)} async-done(((bf16[96,1320]{1,0:T(8,128)(2,1)}), bf16[1536,1320]{1,0:T(8,128)(2,1)}) %all-gather.10.cloned.1.call-update) | async-done | bytes 4055056 | tf_op jit(solution)/shard_map/all_gather | solution.py:105
  64.7 3.4 fusion.51
  70.5 37.9 %all-gather.14.cloned.1.call-done = bf16[1536,768]{1,0:T(8,128)(2,1)} async-done(((bf16[96,768]{1,0:T(8,128)(2,1)}), bf16[1536,768]{1,0:T(8,128)(2,1)}) %all-gather.14.cloned.1.call-update) | async-done | bytes 2359312 | tf_op jit(solution)/shard_map/all_gather | solution.py:107
  108.9 17.1 all-gather.12.cloned.1.call-done
  134.1 3.2 copy-done.2
  144.9 3.6 all-to-all-start
  149.1 45.2 %all-gather.16.cloned.1.call-done = bf16[1536,1536]{1,0:T(8,128)(2,1)} async-done(((bf16[1536,768]{1,0:T(8,128)(2,1)}), bf16[1536,1536]{1,0:T(8,128)(2,1)}) %all-gather.16.cloned.1.call-update) | async-done | bytes 4718608 | tf_op jit(solution)/shard_map/all_gather | solution.py:194
  194.3 3.7 multiply_reduce_fusion.2
  201.1 9.1 all_to_all.92
  211.2 4.7 constant_dynamic-slice_fusion.4
  215.9 6.3 copy.311
  222.2 4.7 copy.262
  230.0 4.0 copy.312
  234.0 3.1 copy.264
  237.1 5.4 fusion.17
  254.7 37.0 %collective-permute-done = bf16[1,384,1920]{1,2,0:T(8,128)(2,1)} collective-permute-done((bf16[1,384,1920]{1,2,0:T(8,128)(2,1)}, bf16[1,384,1920]{1,2,0:T(8,128)(2,1)}, u32[]{:S(2)}, u32[]{:S(2)}) %collective-permute-start) | collective-permute-done | bytes 1474592 | tf_op jit(solution)/shard_map/ppermute | solution.py:61
  294.3 77.8 %collective-permute-done.1 = bf16[1,384,1920]{1,2,0:T(8,128)(2,1)} collective-permute-done((bf16[1,384,1920]{1,2,0:T(8,128)(2,1)}, bf16[1,384,1920]{1,2,0:T(8,128)(2,1)}, u32[]{:S(2)}, u32[]{:S(2)}) %collective-permute-start.1) | collective-permute-done | bytes 1474592 | tf_op jit(solution)/shard_map/ppermute | solution.py:61
  383.8 50.0 %all-gather.18.cloned.1.call-done = bf16[4096,1664]{0,1:T(8,128)(2,1)} async-done(((bf16[128,1664]{0,1:T(8,128)(2,1)}), bf16[4096,1664]{0,1:T(8,128)(2,1)}) %all-gather.18.cloned.1.call-update) | async-done | bytes 13631504 | tf_op jit(solution)/shard_map/all_gather | solution.py:205
  434.9 22.6 %fusion.8 = f32[4096,1280]{0,1:T(8,128)} fusion(bf16[1536,1920]{1,0:T(8,128)(2,1)} %bitcast.22, bf16[4096,1664]{0,1:T(8,128)(2,1)} %all-gather.18.cloned.1.call-done), kind=kOutput, calls=%fused_computation.41 | convolution fusion | flops 16106127360 | bytes 37486592 | tf_op jit(solution)/shard_map/dot_general | solution.py:40
  457.6 103.0 %all-gather.20.cloned.1.call-done = bf16[4096,1536]{0,1:T(8,128)(2,1)} async-done(((bf16[128,1536]{0,1:T(8,128)(2,1)}), bf16[4096,1536]{0,1:T(8,128)(2,1)}) %all-gather.20.cloned.1.call-update) | async-done | bytes 12582928 | tf_op jit(solution)/shard_map/all_gather | solution.py:114
  560.6 28.3 %multiply_convert_fusion.1 = (bf16[4096,640]{0,1:T(8,128)(2,1)}, bf16[4096,640]{0,1:T(8,128)(2,1)}, f32[4096,640]{0,1:T(8,128)}, bf16[4096,640]{0,1:T(8,128)(2,1)}) fusion(f32[4096,1280]{0,1:T(8,128)} %fusion.8, f32[4096,5]{0,1:T(8,128)S(1)} %convert_add_fusion.1, bf16[4096,1536]{0,1:T(8,128)(2,1)} %all-gather.20.cloned.1.call-done, ...), kind=kOutput, calls=%fused_computation.21 | convolution fusion | flops 8100249600 | bytes 61816832 | tf_op jit(solution)/shard_map/dot_general | solution.py:40
  588.9 4.7 reduce_sum.132
  593.6 23.4 %convolution_convert_fusion.1 = bf16[4096,1536]{0,1:T(8,128)(2,1)} fusion(bf16[4096,640]{0,1:T(8,128)(2,1)} %get-tuple-element.101, bf16[4096,640]{0,1:T(8,128)(2,1)} %get-tuple-element.100, bf16[1536,1920]{1,0:T(8,128)(2,1)} %bitcast.22), kind=kOutput, calls=%fused_computation.5 | convolution fusion | flops 16133390336 | bytes 27000832 | tf_op jit(solution)/shard_map/dot_general | solution.py:40
  619.7 14.8 pad_maximum_fusion
  634.4 17.9 %copy.306 = bf16[4096,1664]{1,0:T(8,128)(2,1)} copy(bf16[4096,1664]{0,1:T(8,128)(2,1)} %pad_maximum_fusion) | data formatting | bytes 27262976
  652.5 290.2 %reduce-scatter.15.cloned.1.call-done = bf16[128,1664]{1,0:T(8,128)(2,1)} async-done(((bf16[4096,1664]{1,0:T(8,128)(2,1)}), bf16[128,1664]{1,0:T(8,128)(2,1)}) %reduce-scatter.15.cloned.1.call-update) | async-done | bytes 426000
  947.6 13.2 all_gather.55
  963.4 5.7 fusion.24
  969.1 6.9 fusion
  976.3 4.8 fusion.2
  981.1 4.8 fusion.23
  987.1 3.8 fusion.4
  993.3 14.0 convolution_convert_fusion
  1007.4 4.3 slice.148
  1011.8 13.1 fusion.10
  1024.9 23.4 %convolution_convert_fusion.2 = bf16[1536,1280]{0,1:T(8,128)(2,1)S(1)} fusion(bf16[4096,640]{0,1:T(8,128)(2,1)} %get-tuple-element.101, bf16[4096,640]{0,1:T(8,128)(2,1)} %get-tuple-element.100, bf16[4096,1664]{0,1:T(8,128)(2,1)} %all-gather.18.cloned.1.call-done), kind=kOutput, calls=%fused_computation.29 | convolution fusion | flops 16129064960 | bytes 27000832 | tf_op jit(solution)/shard_map/dot_general | solution.py:40
  1051.3 8.8 copy.310
  1073.4 49.4 %collective-permute-done.3 = bf16[1,384,1920]{2,1,0:T(8,128)(2,1)S(1)} collective-permute-done((bf16[1,384,1920]{2,1,0:T(8,128)(2,1)S(1)}, bf16[1,384,1920]{2,1,0:T(8,128)(2,1)S(1)}, u32[]{:S(2)}, u32[]{:S(2)}) %collective-permute-start.3) | collective-permute-done | bytes 1474592 | tf_op jit(solution)/shard_map/ppermute | solution.py:61
  1124.1 72.0 %collective-permute-done.4 = bf16[1,384,1920]{2,1,0:T(8,128)(2,1)S(1)} collective-permute-done((bf16[1,384,1920]{2,1,0:T(8,128)(2,1)S(1)}, bf16[1,384,1920]{2,1,0:T(8,128)(2,1)S(1)}, u32[]{:S(2)}, u32[]{:S(2)}) %collective-permute-start.4) | collective-permute-done | bytes 1474592 | tf_op jit(solution)/shard_map/ppermute | solution.py:61
  1199.1 5.5 slice-done.5
  1218.1 9.2 copy.308
  1227.5 4.2 pad_maximum_fusion.7
  1232.7 3.5 all-to-all-start.3
  1236.4 27.6 %reduce-scatter.13.cloned.1.call-done = bf16[128,1536]{1,0:T(8,128)(2,1)} async-done(((bf16[4096,1536]{1,0:T(8,128)(2,1)}), bf16[128,1536]{1,0:T(8,128)(2,1)}) %reduce-scatter.13.cloned.1.call-update) | async-done | bytes 393232
  1265.3 97.2 %all-gather.22.cloned.1.call-done = bf16[1536,2560]{1,0:T(8,128)(2,1)} async-done(((bf16[1536,1280]{1,0:T(8,128)(2,1)}), bf16[1536,2560]{1,0:T(8,128)(2,1)}) %all-gather.22.cloned.1.call-update) | async-done | bytes 7864336 | tf_op jit(solution)/shard_map/all_gather | solution.py:326
  1362.5 5.7 fusion.32
  1369.7 3.5 all-to-all-start.1
  1374.3 5.5 all-to-all-done.1
  1379.8 3.6 all-to-all-start.4
  1383.5 51.0 %psum.7 = f32[2,1536]{1,0:T(2,128)S(1)} all-reduce(f32[2,1536]{1,0:T(2,128)S(1)} %pad_maximum_fusion.12), channel_id=1, replica_groups=mesh['dp'=4,'ctx'=4,'tensor'=2] {'dp','ctx','tensor'}, use_global_device_ids=true, to_apply=%region_20.21 | all-reduce | flops 3072 | bytes 24576 | tf_op jit(solution)/shard_map/psum | solution.py:340
  1435.2 82.5 %all-gather.26.cloned.1.call-done = bf16[4,4,384,1920]{3,2,1,0:T(8,128)(2,1)} async-done(((bf16[1,4,384,1920]{3,2,1,0:T(8,128)(2,1)}), bf16[4,4,384,1920]{3,2,1,0:T(8,128)(2,1)}) %all-gather.26.cloned.1.call-update) | async-done | bytes 23592976 | tf_op jit(solution)/shard_map/all_gather | solution.py:247
  1517.7 13.3 slice.177
  1531.0 21.0 %copy.313 = bf16[4,4,384,1280]{2,3,1,0:T(8,128)(2,1)} copy(bf16[4,4,384,1280]{3,2,1,0:T(8,128)(2,1)} %slice.177) | data formatting | bytes 31457280
  1552.0 57.4 %reduce-scatter.17.cloned.1.call-done = bf16[96,2088]{1,0:T(8,128)(2,1)} async-done(((bf16[1536,2088]{1,0:T(8,128)(2,1)}), bf16[96,2088]{1,0:T(8,128)(2,1)}) %reduce-scatter.17.cloned.1.call-update) | async-done | bytes 400912 | tf_op jit(solution)/shard_map/reduce_scatter | solution.py:337
  1609.4 9.2 convert_bitcast_fusion
  1618.6 10.5 copy.287
  1629.1 30.7 %copy.291 = f32[384,20,1024]{2,0,1:T(8,128)} copy(f32[384,20,1024]{0,2,1:T(8,128)} %bitcast.172) | data formatting | bytes 62914560
  1659.8 7.6 slice.178
  1667.4 10.6 copy.314
  1678.0 11.3 convert_bitcast_fusion.1
  1689.3 12.8 copy.289
  1702.1 15.7 copy.292
  (239 shorter events, 124.1 us)
Async XLA Ops:
  7.2 2.7 copy-start
  7.2 57.5 %all-gather.10.cloned.1.call-start = ((), (), s32[]{:S(2)}) async-start(), calls=%async_computation.9 | async-start | bytes 4595712 | tf_op jit(solution)/shard_map/all_gather | solution.py:105
  9.8 98.6 %all-gather.14.cloned.1.call-start = ((), (), s32[]{:S(2)}) async-start(), calls=%async_computation.11 | async-start | bytes 2506752 | tf_op jit(solution)/shard_map/all_gather | solution.py:107
  10.6 115.4 %all-gather.12.cloned.1.call-start = ((), (), s32[]{:S(2)}) async-start(), calls=%async_computation.10 | async-start | bytes 1310720 | tf_op jit(solution)/shard_map/all_gather | solution.py:172
  19.3 49.1 %copy-start.30 = (f32[1536]{0:T(1024)}, f32[1536]{0:T(1024)S(1)}, u32[]{:S(2)}) copy-start(f32[1536]{0:T(1024)S(1)} %get-tuple-element.95) | copy-start | bytes 18436
  30.9 163.4 %copy-start.5 = (bf16[256,1536]{0,1:T(8,128)(2,1)}, bf16[256,1536]{0,1:T(8,128)(2,1)S(1)}, u32[]{:S(2)}) copy-start(bf16[256,1536]{0,1:T(8,128)(2,1)S(1)} %all_gather.47) | copy-start | bytes 2359300
  31.1 37.6 %copy-start.36 = (f32[256]{0:T(256)}, f32[256]{0:T(256)S(1)}, u32[]{:S(2)}) copy-start(f32[256]{0:T(256)S(1)} %add_rsqrt_fusion) | copy-start | bytes 3076
  31.9 36.8 %copy-start.28 = (f32[256,32]{0,1:T(8,128)}, f32[256,32]{0,1:T(8,128)S(1)}, u32[]{:S(2)}) copy-start(f32[256,32]{0,1:T(8,128)S(1)} %get-tuple-element.131) | copy-start | bytes 98308
  68.2 1.8 copy-start.38
  68.2 40.4 %copy-start.35 = (s32[1,1024]{1,0:T(1,128)S(1)}, s32[1,1024]{1,0:T(1,128)}, u32[]{:S(2)}) copy-start(s32[1,1024]{1,0:T(1,128)} %param.15) | copy-start | bytes 12292
  69.7 124.5 %all-gather.16.cloned.1.call-start = ((), (), s32[]{:S(2)}) async-start(), calls=%async_computation.12 | async-start | bytes 7077888 | tf_op jit(solution)/shard_map/all_gather | solution.py:194
  108.9 22.6 %copy-start.20 = (bf16[256,12,64]{0,2,1:T(8,128)(2,1)}, bf16[256,12,64]{0,2,1:T(8,128)(2,1)S(1)}, u32[]{:S(2)}) copy-start(bf16[256,12,64]{0,2,1:T(8,128)(2,1)S(1)} %pad_maximum_fusion.9) | copy-start | bytes 1179652
  129.5 2.0 copy-start.18
  131.5 5.7 copy-start.2
  140.3 2.6 copy-start.3
  144.0 50.2 %copy-start.22 = (bf16[4,64,3,256]{3,1,2,0:T(8,128)(2,1)}, bf16[4,64,3,256]{3,1,2,0:T(8,128)(2,1)S(1)}, u32[]{:S(2)}) copy-start(bf16[4,64,3,256]{3,1,2,0:T(8,128)(2,1)S(1)} %convolution_convert_fusion.8) | copy-start | bytes 1179652
  144.9 56.1 %copy-start.27 = (bf16[256,768]{1,0:T(8,128)(2,1)S(1)}, bf16[256,768]{1,0:T(8,128)(2,1)}, u32[]{:S(2)}) copy-start(bf16[256,768]{1,0:T(8,128)(2,1)} %param.27) | copy-start | bytes 1179652
  144.9 49.3 %all-to-all-start = ((bf16[2,128,768]{1,2,0:T(8,128)(2,1)}), bf16[2,128,768]{1,2,0:T(8,128)(2,1)S(1)}, u32[]{:S(2)}, u32[]{:S(2)}) async-start(bf16[2,128,768]{1,2,0:T(8,128)(2,1)} %copy.259), calls=%async_computation | async-start | bytes 786432 | tf_op jit(solution)/shard_map/all_to_all | solution.py:193
  148.5 285.2 %all-gather.18.cloned.1.call-start = ((), (), s32[]{:S(2)}) async-start(), calls=%async_computation.13 | async-start | bytes 14057472 | tf_op jit(solution)/shard_map/all_gather | solution.py:205
  198.0 748.4 %copy-start.7 = (f32[128,1536]{0,1:T(8,128)}, f32[128,1536]{0,1:T(8,128)S(1)}, u32[]{:S(2)}) copy-start(f32[128,1536]{0,1:T(8,128)S(1)} %get-tuple-element.135) | copy-start | bytes 2359300
  201.0 359.6 %all-gather.20.cloned.1.call-start = ((), (), s32[]{:S(2)}) async-start(), calls=%async_computation.14 | async-start | bytes 12976128 | tf_op jit(solution)/shard_map/all_gather | solution.py:114
  211.1 731.6 %reduce-scatter.15.cloned.1.call-start = ((), (), s32[]{:S(2)}) async-start(), calls=%async_computation.20 | async-start | bytes 14057472
  242.5 49.2 %collective-permute-start = (bf16[1,384,1920]{1,2,0:T(8,128)(2,1)}, bf16[1,384,1920]{1,2,0:T(8,128)(2,1)}, u32[]{:S(2)}, u32[]{:S(2)}) collective-permute-start(bf16[1,384,1920]{1,2,0:T(8,128)(2,1)} %get-tuple-element.111), channel_id=1, source_target_pairs={{0,8},{8,16},{16,24},{24,0},{1,9},{9,17},{17,25},{25,1},{2,10},{10... | collective-permute-start | bytes 4423688 | tf_op jit(solution)/shard_map/ppermute | solution.py:61
  244.1 128.0 %collective-permute-start.1 = (bf16[1,384,1920]{1,2,0:T(8,128)(2,1)}, bf16[1,384,1920]{1,2,0:T(8,128)(2,1)}, u32[]{:S(2)}, u32[]{:S(2)}) collective-permute-start(bf16[1,384,1920]{1,2,0:T(8,128)(2,1)} %get-tuple-element.112), channel_id=1, source_target_pairs={{0,16},{8,24},{16,0},{24,8},{1,17},{9,25},{17,1},{25,9},{2,18},{10... | collective-permute-start | bytes 4423688 | tf_op jit(solution)/shard_map/ppermute | solution.py:61
  246.5 128.2 %collective-permute-start.2 = (bf16[1,384,1920]{1,2,0:T(8,128)(2,1)}, bf16[1,384,1920]{1,2,0:T(8,128)(2,1)}, u32[]{:S(2)}, u32[]{:S(2)}) collective-permute-start(bf16[1,384,1920]{1,2,0:T(8,128)(2,1)} %get-tuple-element.109), channel_id=1, source_target_pairs={{0,24},{8,0},{16,8},{24,16},{1,25},{9,1},{17,9},{25,17},{2,26},{10... | collective-permute-start | bytes 4423688 | tf_op jit(solution)/shard_map/ppermute | solution.py:61
  250.5 3.0 copy-start.14
  377.2 5.3 copy-start.15
  652.4 294.0 %copy-start.11 = (bf16[128,2,768]{0,2,1:T(8,128)(2,1)S(1)}, bf16[128,2,768]{0,2,1:T(8,128)(2,1)}, u32[]{:S(2)}) copy-start(bf16[128,2,768]{0,2,1:T(8,128)(2,1)} %copy.271) | copy-start | bytes 1179652
  652.4 557.6 %reduce-scatter.11.cloned.1.call-start = ((), (), s32[]{:S(2)}) async-start(), calls=%async_computation.15 | async-start | bytes 1310720 | tf_op jit(solution)/shard_map/reduce_scatter | solution.py:301
  944.0 17.7 %copy-start.24 = (bf16[1536,768]{1,0:T(8,128)(2,1)S(1)}, bf16[1536,768]{1,0:T(8,128)(2,1)}, u32[]{:S(2)}) copy-start(bf16[1536,768]{1,0:T(8,128)(2,1)} %all-gather.14.cloned.1.call-done) | copy-start | bytes 7077892
  963.4 12.7 slice-start
  969.1 7.0 slice-start.1
  969.1 7.2 slice-start.2
  976.3 4.8 copy-start.21
  981.1 4.9 copy-start.25
  987.1 277.0 %reduce-scatter.13.cloned.1.call-start = ((), (), s32[]{:S(2)}) async-start(), calls=%async_computation.19 | async-start | bytes 12976128
  990.9 2.4 copy-start.16
  1007.3 355.1 %all-gather.22.cloned.1.call-start = ((), (), s32[]{:S(2)}) async-start(), calls=%async_computation.16 | async-start | bytes 11796480 | tf_op jit(solution)/shard_map/all_gather | solution.py:326
  1011.7 505.9 %all-gather.26.cloned.1.call-start = ((), (), s32[]{:S(2)}) async-start(), calls=%async_computation.18 | async-start | bytes 29491200 | tf_op jit(solution)/shard_map/all_gather | solution.py:247
  1062.9 59.9 %collective-permute-start.3 = (bf16[1,384,1920]{2,1,0:T(8,128)(2,1)S(1)}, bf16[1,384,1920]{2,1,0:T(8,128)(2,1)S(1)}, u32[]{:S(2)}, u32[]{:S(2)}) collective-permute-start(bf16[1,384,1920]{2,1,0:T(8,128)(2,1)S(1)} %get-tuple-element.108), channel_id=1, source_target_pairs={{0,8},{8,16},{16,24},{24,0},{1,9},{9,17},{17,25},{25,1},{2,10},{10... | collective-permute-start | bytes 4423688 | tf_op jit(solution)/shard_map/ppermute | solution.py:61
  1064.0 132.0 %collective-permute-start.4 = (bf16[1,384,1920]{2,1,0:T(8,128)(2,1)S(1)}, bf16[1,384,1920]{2,1,0:T(8,128)(2,1)S(1)}, u32[]{:S(2)}, u32[]{:S(2)}) collective-permute-start(bf16[1,384,1920]{2,1,0:T(8,128)(2,1)S(1)} %get-tuple-element.107), channel_id=1, source_target_pairs={{0,16},{8,24},{16,0},{24,8},{1,17},{9,25},{17,1},{25,9},{2,18},{10... | collective-permute-start | bytes 4423688 | tf_op jit(solution)/shard_map/ppermute | solution.py:61
  1066.3 130.9 %collective-permute-start.5 = (bf16[1,384,1920]{2,1,0:T(8,128)(2,1)S(1)}, bf16[1,384,1920]{2,1,0:T(8,128)(2,1)S(1)}, u32[]{:S(2)}, u32[]{:S(2)}) collective-permute-start(bf16[1,384,1920]{2,1,0:T(8,128)(2,1)S(1)} %get-tuple-element.106), channel_id=1, source_target_pairs={{0,24},{8,0},{16,8},{24,16},{1,25},{9,1},{17,9},{25,17},{2,26},{10... | collective-permute-start | bytes 4423688 | tf_op jit(solution)/shard_map/ppermute | solution.py:61
  1198.5 410.9 %reduce-scatter.17.cloned.1.call-start = ((), (), s32[]{:S(2)}) async-start(), calls=%async_computation.21 | async-start | bytes 7102464 | tf_op jit(solution)/shard_map/reduce_scatter | solution.py:337
  1199.0 8.8 slice-start.3
  1199.0 5.6 slice-start.5
  1199.1 5.6 copy-start.13
  1199.1 6.6 copy-start.23
  1199.1 8.8 slice-start.4
  1204.6 3.2 copy-start.19
  1205.6 5.5 copy-start.29
  1205.6 5.5 copy-start.32
  1207.9 4.7 copy-start.31
  1207.9 4.7 copy-start.37
  1210.0 5.1 copy-start.4
  1210.0 5.1 copy-start.26
  1227.3 8.9 copy-start.6
  1232.7 129.8 %all-to-all-start.3 = ((bf16[2,128,1280]{1,2,0:T(8,128)(2,1)}), bf16[2,128,1280]{1,2,0:T(8,128)(2,1)S(1)}, u32[]{:S(2)}, u32[]{:S(2)}) async-start(bf16[2,128,1280]{1,2,0:T(8,128)(2,1)} %copy.277), calls=%async_computation.4 | async-start | bytes 1310720 | tf_op jit(solution)/shard_map/all_to_all | solution.py:327
  1362.5 5.7 copy-start.8
  1362.5 5.7 copy-start.10
  1368.2 15.3 copy-start.33
  1369.7 10.1 all-to-all-start.1
  1379.8 55.4 %all-to-all-start.4 = ((f32[128,2,768]{2,0,1:T(8,128)}), f32[128,2,768]{2,0,1:T(8,128)S(1)}, u32[]{:S(2)}, u32[]{:S(2)}) async-start(f32[128,2,768]{2,0,1:T(8,128)} %copy.279), calls=%async_computation.5 | async-start | bytes 1572864 | tf_op jit(solution)/shard_map/all_to_all | solution.py:333
  1383.4 334.4 %all-gather.24.cloned.1.call-start = ((), (), s32[]{:S(2)}) async-start(), calls=%async_computation.17 | async-start | bytes 2088960 | tf_op jit(solution)/shard_map/all_gather | solution.py:338
  1702.1 23.7 %copy-start.1 = (bf16[384,768]{1,0:T(8,128)(2,1)S(1)}, bf16[384,768]{1,0:T(8,128)(2,1)}, u32[]{:S(2)}) copy-start(bf16[384,768]{1,0:T(8,128)(2,1)} %param.22) | copy-start | bytes 1769476
  (4 other events, 4.2 us)
Sparse Core Ops, SparseCore 0:
  10.9 53.7 all-gather.9
  67.5 40.8 all-gather.13
  110.5 15.4 all-gather.11
  127.4 66.8 all-gather.15
  201.1 232.5 all-gather.17
  437.1 123.4 all-gather.19
  652.5 290.1 reduce-scatter.14
  987.2 23.9 reduce-scatter.10
  1017.8 246.2 reduce-scatter.12
  1265.5 96.9 all-gather.21
  1364.0 153.5 all-gather.25
  1521.5 87.8 reduce-scatter.16
  1611.0 19.1 all-gather.23

commit v2 on v1

--- a/solution.py
+++ b/solution.py
@@ -1,6 +1,8 @@
 import jax
 import jax.numpy as jnp
 from jax import lax
+from jax.experimental import pallas as pl
+from jax.experimental.pallas import tpu as pltpu
 from jax.sharding import PartitionSpec as P
 
 D = 1536
@@ -15,6 +17,322 @@
 ALL = ("dp", "ctx", "tensor")
 BF = jnp.bfloat16
 F32 = jnp.float32
+MESH = pl.DeviceIdType.MESH
+COST = pl.CostEstimate(flops=0, bytes_accessed=250_000_000, transcendentals=0)
+
+
+def place():
+    ctx = lax.axis_index("ctx")
+    return (lax.axis_index("dp"), ctx // 2, ctx % 2, lax.axis_index("tensor"))
+
+
+def device(z, y, k, x):
+    return {"dp": z, "ctx": y * 2 + k, "tensor": x}
+
+
+def greet(partners):
+    barrier = pltpu.get_barrier_semaphore()
+    for partner in partners:
+        pl.semaphore_signal(barrier, inc=1, device_id=partner, device_id_type=MESH)
+    pl.semaphore_wait(barrier, len(partners))
+
+
+def partners_of(nd, z, y, k, x):
+    return [device((z + hop) % nd, y, k, x) for hop in range(1, nd)] + [
+        device(z, y, k, 1 - x),
+        device(z, 1 - y, k, x),
+        device(z, y, 1 - k, x),
+    ]
+
+
+def gather_kernel(own_ref, out_ref, local_sem, send_sem, recv_sem):
+    nd, width = (out_ref.shape[0], own_ref.shape[2])
+    wide = out_ref.shape[-1] != width
+    z, y, k, x = place()
+    up, down = (device((z + 1) % nd, y, k, x), device((z + nd - 1) % nd, y, k, x))
+    greet([up, down, device(z, y, k, 1 - x), device(z, 1 - y, k, x), device(z, y, 1 - k, x)])
+    low = jnp.minimum(z, nd - 1 - z)
+    places = []
+    for step in range(nd):
+        near = (step + 1) // 2
+        zigzag = low + near if step % 2 else low - near
+        from_low = jnp.where(step <= 2 * low, zigzag, step)
+        places.append(jnp.where(2 * z < nd, from_low, nd - 1 - from_low))
+    sends = []
+
+    def at(piece):
+        step, dy, dk, dx, half = piece
+        chip, core, side = ((y + dy) % 2, (k + dk) % 2, (x + dx) % 2)
+        if not wide:
+            return out_ref.at[places[step], chip, core, side, half]
+        columns = pl.ds(pl.multiple_of(side * width, LANES), width)
+        return out_ref.at[places[step], chip, core, half, :, columns]
+
+    def slot(piece):
+        step, dy, dk, dx, half = piece
+        return (((places[step] * 2 + dy) * 2 + dk) * 2 + dx) * 2 + half
+
+    def send(piece, link, condition=None):
+        step, dy, dk, dx, half = piece
+        if link == "up":
+            target, there = (up, piece)
+        elif link == "down":
+            target, there = (down, piece)
+        elif link == "x":
+            target, there = (device(z, y, k, 1 - x), (step, dy, dk, 1 - dx, half))
+        elif link == "y":
+            target, there = (device(z, 1 - y, k, x), (step, 1 - dy, dk, dx, half))
+        else:
+            target, there = (device(z, y, 1 - k, x), (step, dy, 1 - dk, dx, half))
+        own = piece[:4] == (0, 0, 0, 0)
+        copy = pltpu.make_async_remote_copy(
+            src_ref=own_ref.at[half] if own else at(piece),
+            dst_ref=at(piece),
+            send_sem=send_sem.at[len(sends)],
+            recv_sem=recv_sem.at[slot(there)],
+            device_id=target,
+            device_id_type=MESH,
+        )
+        if condition is None:
+            copy.start()
+        else:
+            pl.when(condition)(copy.start)
+        sends.append((copy, condition))
+
+    def arrived(piece):
+        pltpu.make_async_remote_copy(
+            src_ref=at(piece),
+            dst_ref=at(piece),
+            send_sem=send_sem.at[0],
+            recv_sem=recv_sem.at[slot(piece)],
+            device_id=device(z, y, k, 1 - x),
+            device_id_type=MESH,
+        ).wait_recv()
+
+    own_copies = []
+    for half in range(2):
+        own_copy = pltpu.make_async_copy(
+            own_ref.at[half], at((0, 0, 0, 0, half)), local_sem.at[half]
+        )
+        own_copy.start()
+        own_copies.append(own_copy)
+    links = (("x", "y"), ("y", "x"))
+    for step in range(nd + 2):
+        if step < nd:
+            came = places[step]
+            for half in range(2):
+                piece = (step, 0, 0, 0, half)
+                if step:
+                    arrived(piece)
+                send(piece, "up", (came <= z) & (z < nd - 1))
+                send(piece, "down", (came >= z) & (z > 0))
+                send(piece, links[half][0])
+            for half in range(2):
+                piece = (step, 0, 0, 0, half)
+                send(piece, links[half][1])
+                send(piece, "k")
+        if 1 <= step < nd + 1:
+            for half in range(2):
+                piece = (step - 1, half, 0, 1 - half, half)
+                arrived(piece)
+                send(piece, links[half][1])
+                send(piece, "k")
+        if 2 <= step:
+            for half in range(2):
+                for d in range(2):
+                    piece = (step - 2, 1, 0, d, 0) if half == 0 else (step - 2, d, 0, 1, 1)
+                    arrived(piece)
+                    send(piece, "k")
+    for step in range(nd):
+        for dy in range(2):
+            for dx in range(2):
+                for half in range(2):
+                    arrived((step, dy, 1, dx, half))
+    for own_copy in own_copies:
+        own_copy.wait()
+    for copy, condition in sends:
+        if condition is None:
+            copy.wait_send()
+        else:
+            pl.when(condition)(copy.wait_send)
+
+
+def gather_rows(own, nd, collective_id, wide=False):
+    rows, width = own.shape
+    half = rows // 2
+    shape = (nd, 2, 2, 2, half, 2 * width) if wide else (nd, 2, 2, 2, 2, half, width)
+    out = pl.pallas_call(
+        gather_kernel,
+        in_specs=[pl.BlockSpec(memory_space=pltpu.VMEM)],
+        out_specs=pl.BlockSpec(memory_space=pl.ANY),
+        out_shape=jax.ShapeDtypeStruct(shape, own.dtype),
+        scratch_shapes=[
+            pltpu.SemaphoreType.DMA((2,)),
+            pltpu.SemaphoreType.DMA((nd * 18,)),
+            pltpu.SemaphoreType.DMA((nd * 16,)),
+        ],
+        compiler_params=pltpu.CompilerParams(collective_id=collective_id, has_side_effects=True),
+        cost_estimate=COST,
+        name="gather_rows",
+    )(own.reshape(2, half, width))
+    return out.reshape(-1, shape[-1])
+
+
+def reduce_kernel(
+    part_ref, out_ref, own, from_core, first, second, across, load_sem, send_sem, recv_sem
+):
+    nd = part_ref.shape[0]
+    z, y, k, x = place()
+    greet(partners_of(nd, z, y, k, x))
+    order = [hop for hop in (2, 1, 3, 0)] if nd == 4 else list(range(1, nd)) + [0]
+    sends, loads = ([], [])
+
+    def spot(step, dy, dx, half):
+        return ((step * 2 + dy) * 2 + dx) * 2 + half
+
+    def send(source, there, target, slot):
+        copy = pltpu.make_async_remote_copy(
+            src_ref=source,
+            dst_ref=there,
+            send_sem=send_sem.at[len(sends)],
+            recv_sem=recv_sem.at[slot],
+            device_id=target,
+            device_id_type=MESH,
+        )
+        copy.start()
+        sends.append(copy)
+
+    def arrived(there, slot):
+        pltpu.make_async_remote_copy(
+            src_ref=there,
+            dst_ref=there,
+            send_sem=send_sem.at[0],
+            recv_sem=recv_sem.at[slot],
+            device_id=device(z, y, k, 1 - x),
+            device_id_type=MESH,
+        ).wait_recv()
+
+    def add(to, what, index):
+        to_rows = own.shape[1]
+
+        def body(i, carry):
+            rows = pl.ds(i * 16, 16)
+            total = own[to, rows, :].astype(F32) + what[index, rows, :].astype(F32)
+            own[to, rows, :] = total.astype(BF)
+            return carry
+
+        lax.fori_loop(0, to_rows // 16, body, 0)
+
+    core_slot, first_slot, second_slot, across_slot = (0, nd * 4, nd * 8, nd * 10)
+    for step, dz in enumerate(order):
+        for dy in range(2):
+            for dx in range(2):
+                there = pl.ds(spot(step, dy, dx, 0), 2)
+                block = ((z + dz) % nd, (y + dy) % 2)
+                send(
+                    part_ref.at[block[0], block[1], 1 - k, (x + dx) % 2],
+                    from_core.at[there],
+                    device(z, y, 1 - k, x),
+                    core_slot + (step * 2 + dy) * 2 + dx,
+                )
+                load = pltpu.make_async_copy(
+                    part_ref.at[block[0], block[1], k, (x + dx) % 2],
+                    own.at[there],
+                    load_sem.at[len(loads)],
+                )
+                load.start()
+                loads.append(load)
+    x_partner, y_partner = (device(z, y, k, 1 - x), device(z, 1 - y, k, x))
+    for step in range(nd + 2):
+        if step < nd:
+            for at in range(4):
+                loads[step * 4 + at].wait()
+                base = spot(step, 0, 0, 0) + at * 2
+                arrived(from_core.at[pl.ds(base, 2)], core_slot + step * 4 + at)
+
+            def pair(i, carry, step=step):
+                add(step * 8 + i, from_core, step * 8 + i)
+                return carry
+
+            lax.fori_loop(0, 8, pair, 0)
+            for d in range(2):
+                slot = step * 4 + d
+                send(own.at[spot(step, 1, d, 0)], first.at[slot], y_partner, first_slot + slot)
+                slot = step * 4 + 2 + d
+                send(own.at[spot(step, d, 1, 1)], first.at[slot], x_partner, first_slot + slot)
+        if 1 <= step < nd + 1:
+            now = step - 1
+            for d in (1, 0):
+                slot = now * 4 + d
+                arrived(first.at[slot], first_slot + slot)
+                add(spot(now, 0, d, 0), first, slot)
+                slot = now * 4 + 2 + d
+                arrived(first.at[slot], first_slot + slot)
+                add(spot(now, d, 0, 1), first, slot)
+                if d == 1:
+                    slot = now * 2
+                    send(own.at[spot(now, 0, 1, 0)], second.at[slot], x_partner, second_slot + slot)
+                    slot = now * 2 + 1
+                    send(own.at[spot(now, 1, 0, 1)], second.at[slot], y_partner, second_slot + slot)
+        if 2 <= step:
+            now = step - 2
+            for half in range(2):
+                slot = now * 2 + half
+                arrived(second.at[slot], second_slot + slot)
+                add(spot(now, 0, 0, half), second, slot)
+            hop = order[now]
+            if hop:
+                slot = nd - hop - 1
+                send(
+                    own.at[pl.ds(spot(now, 0, 0, 0), 2)],
+                    across.at[slot],
+                    device((z + hop) % nd, y, k, x),
+                    across_slot + slot,
+                )
+    for slot in range(nd - 1):
+        arrived(across.at[slot], across_slot + slot)
+    mine = spot(order.index(0), 0, 0, 0)
+    for half in range(2):
+
+        def total(i, carry, half=half):
+            rows = pl.ds(i * 16, 16)
+            value = own[mine + half, rows, :].astype(F32)
+            for slot in range(nd - 1):
+                value = value + across[slot, half, rows, :].astype(F32)
+            out_ref[half, rows, :] = value
+            return carry
+
+        lax.fori_loop(0, own.shape[1] // 16, total, 0)
+    for copy in sends:
+        copy.wait_send()
+
+
+def reduce_rows(part, nd, collective_id):
+    total, width = part.shape
+    rows = total // (nd * 8)
+    half = rows // 2
+    out = pl.pallas_call(
+        reduce_kernel,
+        in_specs=[pl.BlockSpec(memory_space=pl.ANY)],
+        out_specs=pl.BlockSpec(memory_space=pltpu.VMEM),
+        out_shape=jax.ShapeDtypeStruct((2, half, width), F32),
+        scratch_shapes=[
+            pltpu.VMEM((nd * 8, half, width), BF),
+            pltpu.VMEM((nd * 8, half, width), BF),
+            pltpu.VMEM((nd * 4, half, width), BF),
+            pltpu.VMEM((nd * 2, half, width), BF),
+            pltpu.VMEM((nd - 1, 2, half, width), BF),
+            pltpu.SemaphoreType.DMA((nd * 4,)),
+            pltpu.SemaphoreType.DMA((nd * 11,)),
+            pltpu.SemaphoreType.DMA((nd * 11,)),
+        ],
+        compiler_params=pltpu.CompilerParams(
+            collective_id=collective_id, has_side_effects=True, vmem_limit_bytes=48 << 20
+        ),
+        cost_estimate=COST,
+        name="reduce_rows",
+    )(part.reshape(nd, 2, 2, 2, 2, half, width))
+    return out.reshape(rows, width)
 
 
 def rope_tables(position):
@@ -61,6 +379,40 @@
         got = lax.ppermute(sent, "dp", [(i, (i + hop) % count) for i in range(count)])
         result = lax.dynamic_update_index_in_dim(result, got, (at - hop) % count, 0)
     return result
+
+
+def expert_major_kernel(gate_ref, up_ref, low_ref, out_ref):
+    count, units = (gate_ref.shape[0], gate_ref.shape[2])
+    for part, ref in enumerate((gate_ref, up_ref, low_ref)):
+        for at in range(count):
+            out_ref[0, :, (part * count + at) * units : (part * count + at + 1) * units] = ref[at]
+
+
+def expert_major(received, own_count, units):
+    nd, d_local, _ = received.shape
+
+    def spec(part):
+        return pl.BlockSpec((nd, d_local, units), lambda e: (0, 0, part * own_count + e))
+
+    return pl.pallas_call(
+        expert_major_kernel,
+        grid=(own_count,),
+        in_specs=[spec(0), spec(1), spec(2)],
+        out_specs=pl.BlockSpec((1, d_local, 3 * nd * units), lambda e: (e, 0, 0)),
+        out_shape=jax.ShapeDtypeStruct((own_count, d_local, 3 * nd * units), received.dtype),
+        name="expert_major",
+    )(received, received, received)
+
+
+def scatter_rows(partial, at, count):
+    if count != 2:
+        return lax.psum_scatter(
+            partial.astype(BF), "tensor", scatter_dimension=0, tiled=True
+        ).astype(F32)
+    half = partial.shape[0] // 2
+    sent = lax.dynamic_slice_in_dim(partial, (1 - at) * half, half, 0).astype(BF)
+    got = lax.ppermute(sent, "tensor", [(0, 1), (1, 0)])
+    return lax.dynamic_slice_in_dim(partial, at * half, half, 0) + got.astype(F32)
 
 
 def on_device(
@@ -110,8 +462,15 @@
         axis=0,
         tiled=True,
     )
-    cot_sub = lax.all_to_all(cotangent, "tensor", 0, 1, tiled=True)
-    cot_all = lax.all_gather(cot_sub, ALL, axis=0, tiled=True)
+    kernels = (nd, nc, nt) == (4, 4, 2)
+    if kernels:
+        cot_all = gather_rows(cotangent, nd, 1, wide=True)
+        cot_sub = lax.dynamic_slice_in_dim(
+            cot_all, (dp_at * nc + ctx_at) * n_rows + tensor_at * sub, sub, 0
+        )
+    else:
+        cot_sub = lax.all_to_all(cotangent, "tensor", 0, 1, tiled=True)
+        cot_all = lax.all_gather(cot_sub, ALL, axis=0, tiled=True)
     tokens_sub = lax.dynamic_slice_in_dim(tokens_full, tensor_at * sub, sub, 0).astype(F32)
 
     by_expert = local_count % nc == 0
@@ -131,9 +490,9 @@
     own_in = jnp.transpose(own_in, (3, 0, 2, 1, 4)).reshape(nd, d_local, 2 * own_count * units)
     own_out = jnp.transpose(own_out, (2, 0, 1, 3)).reshape(nd, d_local, own_count * units)
     width = own_count * units
-    expert_w = exchange(jnp.concatenate([own_in, own_out], axis=2), dp_at, nd)
-    expert_w = expert_w.reshape(D, 3 * width)
-    upper_w, lower_w = (expert_w[:, : 2 * width], expert_w[:, 2 * width :])
+    expert_parts = jnp.concatenate([own_in, own_out], axis=2)
+    tokens_full, expert_parts = lax.optimization_barrier((tokens_full, expert_parts))
+    expert_w = exchange(expert_parts, dp_at, nd)
 
     order_row = order[0]
     places = jnp.arange(pack_len, dtype=jnp.int32)
@@ -155,6 +514,8 @@
     starts = jnp.sum((segment_row[None, :] < local_segs[:, None]).astype(jnp.int32), axis=1)
     cosine_table, sine_table = rope_tables((local_places - starts).astype(F32))
     _, h_one = norm_forward(tokens_full.astype(F32), gain_one_full)
+    if kernels:
+        h_one, cot_all, cot_sub = lax.optimization_barrier((h_one, cot_all, cot_sub))
     projected = dot(h_one, qkv_w, ((1,), (0,)))
     turned = rotate(
         projected[:, : q_width + kv_width].reshape(n_rows, q_heads + kv_heads, HEAD_DIM),
@@ -190,9 +551,7 @@
         .astype(BF)
         .reshape(n_rows, q_width)
     )
-    attended_sub = lax.all_to_all(attended, "tensor", 0, 1, tiled=True)
-    output_full = lax.all_gather(output_w, "tensor", axis=1, tiled=True)
-    middle = tokens_sub + dot(attended_sub, output_full, ((1,), (1,)))
+    middle = tokens_sub + scatter_rows(dot(attended, output_w, ((1,), (1,))), tensor_at, nt)
 
     inverse_two, h_two = norm_forward(middle, gain_two_full)
     logits = jnp.where(uses_sub, dot(h_two, router_w, ((1,), (0,))), NEG)
@@ -202,9 +561,14 @@
     gates_high = gates_kept.astype(BF)
     gates_low = (gates_kept - gates_high.astype(F32)).astype(BF)
     extra = jnp.zeros((sub, LANES - 2 * EXPERTS), BF)
-    h_all = lax.all_gather(
-        jnp.concatenate([h_two, gates_high, gates_low, extra], axis=1), ALL, axis=0, tiled=True
-    )
+    h_ext = jnp.concatenate([h_two, gates_high, gates_low, extra], axis=1)
+    h_ext, expert_w = lax.optimization_barrier((h_ext, expert_w))
+    expert_w = expert_w.reshape(D, 3 * width)
+    upper_w, lower_w = (expert_w[:, : 2 * width], expert_w[:, 2 * width :])
+    if kernels:
+        h_all = gather_rows(h_ext, nd, 2)
+    else:
+        h_all = lax.all_gather(h_ext, ALL, axis=0, tiled=True)
     gates_all = (
         h_all[:, D : D + EXPERTS].astype(F32) + h_all[:, D + EXPERTS : D + 2 * EXPERTS].astype(F32)
     )
@@ -236,25 +600,33 @@
         jnp.zeros((total_rows, LANES), BF), grad_gates.astype(BF), first_expert, 1
     )
     mixed = dot(active_gated, lower_w, ((1,), (1,))).astype(BF)
-    back_sub = lax.psum_scatter(
-        jnp.concatenate([grad_in, grad_gates], axis=1), ALL, scatter_dimension=0, tiled=True
-    ).astype(F32)
-    mixed_sub = lax.psum_scatter(mixed, ALL, scatter_dimension=0, tiled=True).astype(F32)
+    back = jnp.concatenate([grad_in, grad_gates], axis=1)
     grad_upper = dot(h_all, grad_hidden, ((0,), (0,))).astype(BF)
     grad_lower = dot(cot_all, active_gated, ((0,), (0,))).astype(BF)
     grad_expert = jnp.concatenate([grad_upper, grad_lower], axis=1).reshape(nd, d_local, 3 * width)
+    if kernels:
+        back, grad_expert = lax.optimization_barrier((back, grad_expert))
+        back_sub = reduce_rows(back, nd, 3)
+        mixed, back_sub = lax.optimization_barrier((mixed, back_sub))
+        mixed_sub = reduce_rows(mixed, nd, 4)
+        back_sub, mixed_sub = lax.optimization_barrier((back_sub, mixed_sub))
+    else:
+        back_sub = lax.psum_scatter(back, ALL, scatter_dimension=0, tiled=True).astype(F32)
+        mixed_sub = lax.psum_scatter(mixed, ALL, scatter_dimension=0, tiled=True).astype(F32)
     grad_expert = exchange(grad_expert, dp_at, nd)
-    grad_expert = lax.all_gather(grad_expert, "ctx", axis=0)
-    grad_up = grad_expert[..., : 2 * width].reshape(nc, nd, d_local, 2, own_count, units)
-    grad_low = grad_expert[..., 2 * width :].reshape(nc, nd, d_local, own_count, units)
     if by_expert:
-        grad_up = jnp.transpose(grad_up, (2, 0, 4, 3, 1, 5))
-        grad_low = jnp.transpose(grad_low, (2, 0, 3, 1, 4))
+        grad_expert = expert_major(grad_expert, own_count, units)
+        grad_expert = lax.all_gather(grad_expert, "ctx", axis=0, tiled=True)
+        grad_expert = jnp.transpose(grad_expert, (1, 0, 2)).astype(F32)
+        grad_expert_in, grad_expert_out = (grad_expert[..., : 2 * FF], grad_expert[..., 2 * FF :])
     else:
+        grad_expert = lax.all_gather(grad_expert, "ctx", axis=0)
+        grad_up = grad_expert[..., : 2 * width].reshape(nc, nd, d_local, 2, own_count, units)
+        grad_low = grad_expert[..., 2 * width :].reshape(nc, nd, d_local, own_count, units)
         grad_up = jnp.transpose(grad_up, (2, 4, 3, 1, 0, 5))
         grad_low = jnp.transpose(grad_low, (2, 3, 1, 0, 4))
-    grad_expert_in = grad_up.reshape(d_local, local_count, 2 * FF).astype(F32)
-    grad_expert_out = grad_low.reshape(d_local, local_count, FF).astype(F32)
+        grad_expert_in = grad_up.reshape(d_local, local_count, 2 * FF).astype(F32)
+        grad_expert_out = grad_low.reshape(d_local, local_count, FF).astype(F32)
 
     result = lax.all_to_all((middle + mixed_sub).astype(BF), "tensor", 1, 0, tiled=True)
 
@@ -323,9 +695,7 @@
         ],
         axis=1,
     )
-    qkv_full = lax.all_gather(qkv_w, "tensor", axis=1, tiled=True)
-    grad_qkv_sub = lax.all_to_all(grad_qkv, "tensor", 0, 1, tiled=True)
-    grad_norm_one = dot(grad_qkv_sub, qkv_full, ((1,), (1,)))
+    grad_norm_one = scatter_rows(dot(grad_qkv, qkv_w, ((1,), (1,))), tensor_at, nt)
     inverse_sub = lax.rsqrt(jnp.mean(tokens_sub * tokens_sub, axis=1, keepdims=True) + EPS)
     grad_tokens, grad_gain_one = norm_backward(
         tokens_sub, gain_one_full, inverse_sub, grad_norm_one
@@ -337,7 +707,9 @@
     weight_grads = lax.psum_scatter(weight_grads, ("dp", "ctx"), scatter_dimension=0, tiled=True)
     weight_grads = lax.all_gather(weight_grads, "ctx", axis=0, tiled=True).astype(F32)
     edges = [0, q_width, q_width + kv_width, qkv_width, qkv_width + q_width]
-    gain_grads = lax.psum(jnp.stack([grad_gain_one, grad_gain_two]), ALL)
+    gain_grads = jnp.sum(
+        lax.all_gather(jnp.stack([grad_gain_one, grad_gain_two]), ALL, axis=0), axis=0
+    )
     gain_grads = lax.dynamic_slice_in_dim(gain_grads, tensor_at * part_width, part_width, 1)
     return (
         result,

time: 1750 us -> 1250 us (0.71)
  waiting for transfers between devices: 1080 us -> 358 us
  Pallas kernels: 0 us -> 292 us
  local copies, waits for them, and re-layouts: 268 us -> 174 us
  blocking collectives: 89.2 us -> 127 us
    all_gather x5 -> x1, waiting for transfers between devices: 378 us -> 43.1 us  [on_device(): grad_expert = lax.all_gather(grad_expert, 'ctx', axis=0, tiled=True)]
    unnamed x15 -> x7, waiting for transfers between devices: 318 us -> 0.11 us
    pallas_call x0 -> x5, Pallas kernels: none -> 292 us  [the longest x2 149 us: gather_rows(): pl.pallas_call(gather_kernel, in_specs=[pl.BlockSpec(memory_space=pltpu.V...]
    unnamed x103 -> x133, local copies, waits for them, and re-layouts: 133 us -> 30.4 us
    all_gather x0 -> x1, blocking collectives: none -> 97.1 us  [on_device(): lax.all_gather(jnp.stack([grad_gain_one, grad_gain_two]), ALL, axis=0)]
    psum x1 -> x0, blocking collectives: 51 us -> none  [on_device(): gain_grads = lax.psum(jnp.stack([grad_gain_one, grad_gain_two]), ALL)]
    ppermute x6, waiting for transfers between devices: 236 us -> 197 us  [exchange(): lax.ppermute(sent, 'dp', [(i, (i + hop) % count) for i in range(count)])]
    all_gather x1, waiting for transfers between devices: 37.9 us -> 0.02 us  [on_device(): lax.all_gather(lax.dynamic_slice_in_dim(w_output, ctx_at * share, share,...]
  transfers between devices with their start and end apart: 23 -> 17, of which waited for: 16 -> 10; matrix products, arithmetic and copies ran while one was open for 21% -> 10% of each run, Pallas kernels for 0% -> 5%
where the time goes in v2:
time: 1250 us; the launch traced here: 1240 us
  waiting for transfers between devices  358 us (29%)
  Pallas kernels  292 us (23%)
  local copies, waits for them, and re-layouts  174 us (14%)
  matrix products  168 us (13%)
  blocking collectives  127 us (10%)
  other arithmetic  90 us (7%)
  starting transfers between devices  19 us (2%)
  between operations  15.5 us (1%)
    ppermute x6, waiting for transfers between devices, exchange(): lax.ppermute(sent, 'dp', [(i, (i + hop) % count) for i in range(count)])  197 us
    pallas_call x2, Pallas kernels, gather_rows(): pl.pallas_call(gather_kernel, in_specs=[pl.BlockSpec(memory_space=pltpu.V...  149 us
    dot_general x16, matrix products, dot(): return lax.dot_general(a, b, (dims, ((), ())), preferred_element_type=F32)  141 us
    pallas_call x2, Pallas kernels, reduce_rows(): pl.pallas_call(reduce_kernel, in_specs=[pl.BlockSpec(memory_space=pl.ANY)...  135 us
    all_gather x1, blocking collectives, on_device(): lax.all_gather(jnp.stack([grad_gain_one, grad_gain_two]), ALL, axis=0)  97.1 us
    reduce_scatter x1, waiting for transfers between devices, on_device(): lax.psum_scatter(weight_grads, ('dp', 'ctx'), scatter_dimension=0, tiled=...  87.8 us
    all_gather x1, waiting for transfers between devices, on_device(): grad_expert = lax.all_gather(grad_expert, 'ctx', axis=0, tiled=True)  43.1 us
    unnamed x133, local copies, waits for them, and re-layouts  30.4 us
  transfers between devices with their start and end apart: 17, of which 10 were waited for; matrix products, arithmetic and copies ran while one was open for 10% of the time, Pallas kernels for 5%

profile of v2, /device:TPU:0, one launch (start us, length us, event | category | flops | bytes accessed | tf_op | source)
XLA Modules:
  0.0 1243.4 jit_solution(2320077163216768392)
XLA Ops:
  9.9 3.0 constant_dynamic-slice_fusion.10
  12.9 2.8 copy.170
  17.3 2.8 copy.137
  20.1 4.9 constant_dynamic-slice_fusion.11
  24.9 6.3 copy.169
  31.2 4.7 copy.133
  35.9 6.3 copy.136
  42.2 13.0 %all_gather.30 = bf16[256,1536]{1,0:T(8,128)(2,1)S(1)} all-gather(bf16[256,768]{1,0:T(8,128)(2,1)} %param.14), channel_id=1, replica_groups=mesh['dp'=4,'ctx'=4,'tensor'=2] {'tensor'}, dimensions={1}, use_global_device_ids=true | all-gather | bytes 1179648 | tf_op jit(solution)/shard_map/all_gather | solution.py:453
  55.2 5.5 pad_maximum_fusion.5
  60.8 59.9 %gather_rows.2 = bf16[4,2,2,2,128,1536]{5,4,3,2,1,0:T(8,128)(2,1)} custom-call(bf16[2,128,768]{2,1,0:T(8,128)(2,1)} %bitcast.184), custom_call_target="tpu_custom_call" | custom-call | bytes 250000000 | tf_op jit(solution)/shard_map/gather_rows/pallas_call | solution.py:164
  120.7 4.4 all_gather.31
  129.1 3.3 fusion.12
  135.6 3.0 broadcast.251.clone
  138.6 5.6 constant_dynamic-slice_fusion.2
  150.2 36.1 %collective-permute-done.1 = bf16[1,384,1920]{2,1,0:T(8,128)(2,1)} collective-permute-done((bf16[1,384,1920]{2,1,0:T(8,128)(2,1)}, bf16[1,384,1920]{2,1,0:T(8,128)(2,1)}, u32[]{:S(2)}, u32[]{:S(2)}) %collective-permute-start.1) | collective-permute-done | bytes 1474592 | tf_op jit(solution)/shard_map/ppermute | solution.py:379
  188.9 68.0 %collective-permute-done.2 = bf16[1,384,1920]{2,1,0:T(8,128)(2,1)} collective-permute-done((bf16[1,384,1920]{2,1,0:T(8,128)(2,1)}, bf16[1,384,1920]{2,1,0:T(8,128)(2,1)}, u32[]{:S(2)}, u32[]{:S(2)}) %collective-permute-start.2) | collective-permute-done | bytes 1474592 | tf_op jit(solution)/shard_map/ppermute | solution.py:379
  256.9 2.6 constant_dynamic-update-slice_fusion.3
  267.8 5.2 divide_convert_fusion
  273.2 4.1 convolution_convert_fusion.8
  281.7 2.6 constant_dynamic-update-slice_fusion.2
  284.9 5.4 collective-permute-done
  295.6 89.3 %gather_rows.3 = bf16[4,2,2,2,2,64,1664]{6,5,4,3,2,1,0:T(8,128)(2,1)} custom-call(bf16[2,64,1664]{2,1,0:T(8,128)(2,1)} %bitcast.179), custom_call_target="tpu_custom_call" | custom-call | bytes 250000000 | tf_op jit(solution)/shard_map/gather_rows/pallas_call | solution.py:164
  387.0 22.6 %fusion.8 = f32[4096,1280]{0,1:T(8,128)} fusion(bf16[1536,1920]{1,0:T(8,128)(2,1)} %bitcast.25, bf16[4096,1664]{1,0:T(8,128)(2,1)} %bitcast.143), kind=kOutput, calls=%fused_computation.33 | convolution fusion | flops 16106127360 | bytes 37486592 | tf_op jit(solution)/shard_map/dot_general | solution.py:358
  410.8 28.5 %multiply_convert_fusion.1 = (bf16[4096,640]{0,1:T(8,128)(2,1)}, bf16[4096,640]{0,1:T(8,128)(2,1)}, f32[4096,640]{0,1:T(8,128)}, bf16[4096,640]{0,1:T(8,128)(2,1)}) fusion(f32[4096,1280]{0,1:T(8,128)} %fusion.8, f32[4096,5]{0,1:T(8,128)S(1)} %copy.146, bf16[4096,1536]{1,0:T(8,128)(2,1)} %bitcast.148, bf16[1536,1920]{1,0:T(8,128)(2,1)} %bitcast.25), kind=kOutput, calls=%fused_computation.20 | convolution fusion | flops 8100249600 | bytes 61816832 | tf_op jit(solution)/shard_map/dot_general | solution.py:358
  439.3 3.9 fusion.4
  443.2 14.1 %convolution_convert_fusion = bf16[4096,1536]{1,0:T(8,128)(2,1)} fusion(bf16[4096,640]{0,1:T(8,128)(2,1)S(1)} %fusion.4, bf16[1536,1920]{1,0:T(8,128)(2,1)} %bitcast.25), kind=kOutput, calls=%fused_computation.3 | convolution fusion | flops 8059355136 | bytes 19791872 | tf_op jit(solution)/shard_map/dot_general | solution.py:358
  457.3 9.6 convolution_convert_fusion.5
  466.9 23.5 %convolution_convert_fusion.1 = bf16[4096,1536]{0,1:T(8,128)(2,1)} fusion(bf16[4096,640]{0,1:T(8,128)(2,1)} %get-tuple-element.107, bf16[4096,640]{0,1:T(8,128)(2,1)} %get-tuple-element.106, bf16[1536,1920]{1,0:T(8,128)(2,1)} %bitcast.25), kind=kOutput, calls=%fused_computation.4 | convolution fusion | flops 16133390336 | bytes 27000832 | tf_op jit(solution)/shard_map/dot_general | solution.py:358
  490.5 20.8 %convolution_convert_fusion.2 = bf16[1536,1280]{0,1:T(8,128)(2,1)S(1)} fusion(bf16[4096,640]{0,1:T(8,128)(2,1)} %get-tuple-element.107, bf16[4096,640]{0,1:T(8,128)(2,1)S(1)} %bitcast.162, bf16[4096,1664]{1,0:T(8,128)(2,1)} %bitcast.144), kind=kOutput, calls=%fused_computation.24 | convolution fusion | flops 16129064960 | bytes 27000832 | tf_op jit(solution)/shard_map/dot_general | solution.py:358
  511.2 4.4 pad_maximum_fusion.6
  515.7 8.6 copy.147
  524.3 4.7 reduce_sum.141
  529.6 14.4 %pad_maximum_fusion = bf16[4096,1664]{0,1:T(8,128)(2,1)} fusion(bf16[4096,128]{0,1:T(8,128)(2,1)S(1)} %dynamic_update_slice.32, bf16[4096,1536]{0,1:T(8,128)(2,1)} %convolution_convert_fusion.1), kind=kLoop, calls=%fused_computation.5 | loop fusion | flops 27262976 | bytes 27262976 | tf_op jit(solution)/shard_map/concatenate | solution.py:603
  544.0 17.9 %copy.148 = bf16[4096,1664]{1,0:T(8,128)(2,1)} copy(bf16[4096,1664]{0,1:T(8,128)(2,1)} %pad_maximum_fusion) | data formatting | bytes 27262976 | tf_op jit(solution)/shard_map/optimization_barrier | solution.py:608
  562.0 71.7 %reduce_rows.2 = f32[2,64,1664]{2,1,0:T(8,128)S(1)} custom-call(bf16[4,2,2,2,2,64,1664]{6,5,4,3,2,1,0:T(8,128)(2,1)} %bitcast.146), custom_call_target="tpu_custom_call" | custom-call | bytes 250000000 | tf_op jit(solution)/shard_map/reduce_rows/pallas_call | solution.py:314
  633.8 63.5 %reduce_rows.3 = f32[2,64,1536]{2,1,0:T(8,128)S(1)} custom-call(bf16[4,2,2,2,2,64,1536]{6,5,4,3,2,1,0:T(8,128)(2,1)} %bitcast.156), custom_call_target="tpu_custom_call" | custom-call | bytes 250000000 | tf_op jit(solution)/shard_map/reduce_rows/pallas_call | solution.py:314
  702.8 12.5 %all_gather.35 = bf16[256,1664]{1,0:T(8,128)(2,1)S(1)} all-gather(bf16[128,1664]{1,0:T(8,128)(2,1)S(1)} %concatenate.55), channel_id=1, replica_groups=mesh['dp'=4,'ctx'=4,'tensor'=2] {'tensor'}, dimensions={0}, use_global_device_ids=true | all-gather | bytes 1277952 | tf_op jit(solution)/shard_map/all_gather | solution.py:641
  716.3 3.3 convolution_convert_fusion.7
  720.7 4.9 fusion.23
  725.7 10.3 fusion
  736.0 6.7 fusion.2
  742.7 2.7 copy-done.3
  748.6 6.4 slice.157
  758.1 4.0 convolution_multiply_fusion
  762.1 11.7 reduce-scatter.5.cloned.1.call-done
  777.9 3.0 pad_maximum_fusion.4
  780.9 9.2 copy.167
  790.3 87.8 %reduce-scatter.7.cloned.1.call-done = bf16[96,2088]{1,0:T(8,128)(2,1)} async-done(((bf16[1536,2088]{1,0:T(8,128)(2,1)}), bf16[96,2088]{1,0:T(8,128)(2,1)}) %reduce-scatter.7.cloned.1.call-update) | async-done | bytes 400912 | tf_op jit(solution)/shard_map/reduce_scatter | solution.py:707
  878.2 3.0 broadcast.251
  881.2 4.2 constant_dynamic-slice_fusion.8
  889.8 32.7 %collective-permute-done.5 = bf16[1,384,1920]{2,1,0:T(8,128)(2,1)S(1)} collective-permute-done((bf16[1,384,1920]{2,1,0:T(8,128)(2,1)S(1)}, bf16[1,384,1920]{2,1,0:T(8,128)(2,1)S(1)}, u32[]{:S(2)}, u32[]{:S(2)}) %collective-permute-start.5) | collective-permute-done | bytes 1474592 | tf_op jit(solution)/shard_map/ppermute | solution.py:379
  923.7 60.0 %collective-permute-done.6 = bf16[1,384,1920]{2,1,0:T(8,128)(2,1)S(1)} collective-permute-done((bf16[1,384,1920]{2,1,0:T(8,128)(2,1)S(1)}, bf16[1,384,1920]{2,1,0:T(8,128)(2,1)S(1)}, u32[]{:S(2)}, u32[]{:S(2)}) %collective-permute-start.6) | collective-permute-done | bytes 1474592 | tf_op jit(solution)/shard_map/ppermute | solution.py:379
  986.1 7.2 expert_major.1
  994.2 3.5 fusion.10
  999.3 9.5 collective-permute-done.4
  1011.3 3.5 all-to-all-start
  1016.9 4.0 all-to-all-done
  1020.8 3.5 all-to-all-start.1
  1024.4 97.1 %all-gather.1 = f32[32,2,1536]{2,1,0:T(2,128)S(1)} all-gather(f32[1,2,1536]{2,1,0:T(2,128)S(1)} %maximum_bitcast_fusion), channel_id=2, replica_groups=mesh['dp'=4,'ctx'=4,'tensor'=2] {'dp','ctx','tensor'}, dimensions={0}, use_global_device_ids=true | all-gather | bytes 405504 | tf_op jit(solution)/shard_map/all_gather | solution.py:711
  1126.0 2.8 fusion.66
  1128.8 43.1 %all-gather.16.cloned.1.call-done = bf16[20,384,1536]{2,1,0:T(8,128)(2,1)} async-done(((bf16[5,384,1536]{2,1,0:T(8,128)(2,1)}), bf16[20,384,1536]{2,1,0:T(8,128)(2,1)}) %all-gather.16.cloned.1.call-update) | async-done | bytes 23592976 | tf_op jit(solution)/shard_map/all_gather | solution.py:619
  1171.9 25.9 %convert_bitcast_fusion = f32[384,20,1536]{2,0,1:T(8,128)} fusion(bf16[20,384,1536]{2,1,0:T(8,128)(2,1)} %all-gather.16.cloned.1.call-done), kind=kLoop, calls=%fused_computation | loop fusion | flops 11796480 | bytes 70778880 | tf_op jit(solution)/shard_map/convert_element_type | solution.py:620
  1197.9 22.7 %slice.176 = f32[384,20,1024]{2,0,1:T(8,128)} slice(f32[384,20,1536]{2,0,1:T(8,128)} %convert_bitcast_fusion), slice={[0:384], [0:20], [0:1024]} | slice | bytes 62914560 | tf_op jit(solution)/shard_map/slice | solution.py:621
  1220.6 14.1 %slice.177 = f32[384,20,512]{2,0,1:T(8,128)} slice(f32[384,20,1536]{2,0,1:T(8,128)} %convert_bitcast_fusion), slice={[0:384], [0:20], [1024:1536]} | slice | bytes 31457280 | tf_op jit(solution)/shard_map/slice | solution.py:621
  (250 shorter events, 81.3 us)
Async XLA Ops:
  7.2 140.9 %copy-start = (bf16[384,768]{1,0:T(8,128)(2,1)S(1)}, bf16[384,768]{1,0:T(8,128)(2,1)}, u32[]{:S(2)}) copy-start(bf16[384,768]{1,0:T(8,128)(2,1)} %param.22) | copy-start | bytes 1769476
  7.2 121.9 %all-gather.8.cloned.1.call-start = ((), (), s32[]{:S(2)}) async-start(), calls=%async_computation.4 | async-start | bytes 4595712 | tf_op jit(solution)/shard_map/all_gather | solution.py:457
  9.8 249.8 %all-gather.10.cloned.1.call-start = ((), (), s32[]{:S(2)}) async-start(), calls=%async_computation.5 | async-start | bytes 1310720 | tf_op jit(solution)/shard_map/all_gather | solution.py:533
  55.2 235.1 %copy-start.8 = (bf16[256,1536]{1,0:T(8,128)(2,1)}, bf16[256,1536]{1,0:T(8,128)(2,1)S(1)}, u32[]{:S(2)}) copy-start(bf16[256,1536]{1,0:T(8,128)(2,1)S(1)} %all_gather.30) | copy-start | bytes 2359300
  55.2 5.5 copy-start.50
  60.7 66.7 %copy-start.40 = (s32[1,1024]{1,0:T(1,128)S(1)}, s32[1,1024]{1,0:T(1,128)}, u32[]{:S(2)}) copy-start(s32[1,1024]{1,0:T(1,128)} %param.15) | copy-start | bytes 12292
  125.2 7.9 copy-start.36
  125.2 166.0 %copy-start.33 = (f32[1536]{0:T(1024)}, f32[1536]{0:T(1024)S(1)}, u32[]{:S(2)}) copy-start(f32[1536]{0:T(1024)S(1)} %get-tuple-element.98) | copy-start | bytes 18436
  127.4 5.6 copy-start.25
  135.5 141.9 %all-gather.12.cloned.1.call-start = ((), (), s32[]{:S(2)}) async-start(), calls=%async_computation.6 | async-start | bytes 2506752 | tf_op jit(solution)/shard_map/all_gather | solution.py:459
  138.6 10.6 copy-start.54
  138.6 11.2 copy-start.39
  138.6 11.3 copy-start.48
  144.2 42.1 %collective-permute-start.1 = (bf16[1,384,1920]{2,1,0:T(8,128)(2,1)}, bf16[1,384,1920]{2,1,0:T(8,128)(2,1)}, u32[]{:S(2)}, u32[]{:S(2)}) collective-permute-start(bf16[1,384,1920]{2,1,0:T(8,128)(2,1)} %get-tuple-element.118), channel_id=1, source_target_pairs={{0,8},{8,16},{16,24},{24,0},{1,9},{9,17},{17,25},{25,1},{2,10},{10... | collective-permute-start | bytes 4423688 | tf_op jit(solution)/shard_map/ppermute | solution.py:379
  145.0 112.0 %collective-permute-start.2 = (bf16[1,384,1920]{2,1,0:T(8,128)(2,1)}, bf16[1,384,1920]{2,1,0:T(8,128)(2,1)}, u32[]{:S(2)}, u32[]{:S(2)}) collective-permute-start(bf16[1,384,1920]{2,1,0:T(8,128)(2,1)} %get-tuple-element.117), channel_id=1, source_target_pairs={{0,16},{8,24},{16,0},{24,8},{1,17},{9,25},{17,1},{25,9},{2,18},{10... | collective-permute-start | bytes 4423688 | tf_op jit(solution)/shard_map/ppermute | solution.py:379
  146.3 135.4 %collective-permute-start.3 = (bf16[1,384,1920]{2,1,0:T(8,128)(2,1)}, bf16[1,384,1920]{2,1,0:T(8,128)(2,1)}, u32[]{:S(2)}, u32[]{:S(2)}) collective-permute-start(bf16[1,384,1920]{2,1,0:T(8,128)(2,1)} %get-tuple-element.116), channel_id=1, source_target_pairs={{0,24},{8,0},{16,8},{24,16},{1,25},{9,1},{17,9},{25,17},{2,26},{10... | collective-permute-start | bytes 4423688 | tf_op jit(solution)/shard_map/ppermute | solution.py:379
  148.8 625.0 %reduce-scatter.5.cloned.1.call-start = ((), (), s32[]{:S(2)}) async-start(), calls=%async_computation.7 | async-start | bytes 1310720 | tf_op jit(solution)/shard_map/reduce_scatter | solution.py:673
  150.2 115.6 %copy-start.6 = (pred[256,1024]{0,1:T(8,128)(4,1)}, pred[256,1024]{0,1:T(8,128)(4,1)S(1)}, u32[]{:S(2)}) copy-start(pred[256,1024]{0,1:T(8,128)(4,1)S(1)} %fusion.25) | copy-start | bytes 786436
  273.2 6.9 copy-start.13
  277.3 16.1 %copy-start.19 = (bf16[4,64,3,256]{3,1,2,0:T(8,128)(2,1)}, bf16[4,64,3,256]{3,1,2,0:T(8,128)(2,1)S(1)}, u32[]{:S(2)}) copy-start(bf16[4,64,3,256]{3,1,2,0:T(8,128)(2,1)S(1)} %convolution_convert_fusion.8) | copy-start | bytes 1179652
  280.1 10.3 collective-permute-start
  291.1 93.7 %copy-start.52 = (f32[128]{0:T(128)}, f32[128]{0:T(128)S(1)}, u32[]{:S(2)}) copy-start(f32[128]{0:T(128)S(1)} %get-tuple-element.104) | copy-start | bytes 1540
  291.2 93.7 %copy-start.44 = (f32[128]{0:T(128)}, f32[128]{0:T(128)S(1)}, u32[]{:S(2)}) copy-start(f32[128]{0:T(128)S(1)} %add_rsqrt_fusion.2) | copy-start | bytes 1540
  293.5 91.4 %copy-start.29 = (f32[128,40]{0,1:T(8,128)}, f32[128,40]{0,1:T(8,128)S(1)}, u32[]{:S(2)}) copy-start(f32[128,40]{0,1:T(8,128)S(1)} %get-tuple-element.143) | copy-start | bytes 61444
  439.3 18.0 %slice-start.3 = ((s8[12582912]{0:T(1024)(128)(4,1)}), s8[4194304]{0:T(1024)(128)(4,1)S(1)}, s32[]{:S(2)}) async-start(s8[12582912]{0:T(1024)(128)(4,1)} %bitcast.149), calls=%async_computation.14 | async-start | bytes 8388608
  443.2 14.1 %slice-start.4 = ((s8[12582912]{0:T(1024)(128)(4,1)}), s8[4194304]{0:T(1024)(128)(4,1)S(1)}, s32[]{:S(2)}) async-start(s8[12582912]{0:T(1024)(128)(4,1)} %bitcast.149), calls=%async_computation.15 | async-start | bytes 8388608
  443.2 14.1 %slice-start.5 = ((s8[12582912]{0:T(1024)(128)(4,1)}), s8[4194304]{0:T(1024)(128)(4,1)S(1)}, s32[]{:S(2)}) async-start(s8[12582912]{0:T(1024)(128)(4,1)} %bitcast.149), calls=%async_computation.16 | async-start | bytes 8388608
  457.3 33.1 %slice-start.6 = ((s8[5242880]{0:T(1024)(128)(4,1)}), s8[1048576]{0:T(1024)(128)(4,1)S(1)}, s32[]{:S(2)}) async-start(s8[5242880]{0:T(1024)(128)(4,1)} %bitcast.161), calls=%async_computation.17 | async-start | bytes 2097152
  466.9 23.6 %slice-start.7 = ((s8[5242880]{0:T(1024)(128)(4,1)}), s8[4194304]{0:T(1024)(128)(4,1)S(1)}, s32[]{:S(2)}) async-start(s8[5242880]{0:T(1024)(128)(4,1)} %bitcast.161), calls=%async_computation.18 | async-start | bytes 8388608
  633.7 64.8 %copy-start.30 = (f32[128,40]{0,1:T(8,128)S(1)}, f32[128,40]{0,1:T(8,128)}, u32[]{:S(2)}) copy-start(f32[128,40]{0,1:T(8,128)} %copy-done.29) | copy-start | bytes 61444
  633.7 64.8 %copy-start.41 = (pred[128,40]{0,1:T(8,128)(4,1)S(1)}, pred[128,40]{0,1:T(8,128)(4,1)}, u32[]{:S(2)}) copy-start(pred[128,40]{0,1:T(8,128)(4,1)} %get-tuple-element.144) | copy-start | bytes 15364
  633.7 64.8 %copy-start.43 = (f32[128]{0:T(128)S(1)}, f32[128]{0:T(128)}, u32[]{:S(2)}) copy-start(f32[128]{0:T(128)} %copy-done.42) | copy-start | bytes 1540
  633.7 64.8 %copy-start.47 = (f32[128]{0:T(128)S(1)}, f32[128]{0:T(128)}, u32[]{:S(2)}) copy-start(f32[128]{0:T(128)} %copy-done.46) | copy-start | bytes 1540
  633.7 66.4 %copy-start.5 = (f32[128,1536]{1,0:T(8,128)S(1)}, f32[128,1536]{1,0:T(8,128)}, u32[]{:S(2)}) copy-start(f32[128,1536]{1,0:T(8,128)} %copy-done.4) | copy-start | bytes 2359300
  633.7 66.4 %copy-start.34 = (f32[1536]{0:T(1024)S(1)}, f32[1536]{0:T(1024)}, u32[]{:S(2)}) copy-start(f32[1536]{0:T(1024)} %copy-done.33) | copy-start | bytes 18436
  633.7 66.4 %copy-start.45 = (f32[128]{0:T(128)S(1)}, f32[128]{0:T(128)}, u32[]{:S(2)}) copy-start(f32[128]{0:T(128)} %copy-done.44) | copy-start | bytes 1540
  633.7 67.8 %copy-start.53 = (f32[128]{0:T(128)S(1)}, f32[128]{0:T(128)}, u32[]{:S(2)}) copy-start(f32[128]{0:T(128)} %copy-done.52) | copy-start | bytes 1540
  633.8 68.7 %copy-start.21 = (bf16[128,1536]{1,0:T(8,128)(2,1)S(1)}, bf16[128,1536]{1,0:T(8,128)(2,1)}, u32[]{:S(2)}) copy-start(bf16[128,1536]{1,0:T(8,128)(2,1)} %constant_dynamic-slice_fusion.9) | copy-start | bytes 1179652
  716.3 9.4 copy-start.7
  716.3 9.4 copy-start.14
  716.3 9.4 copy-start.35
  720.7 15.3 %slice-start = ((s8[12582912]{0:T(1024)(128)(4,1)}), s8[4194304]{0:T(1024)(128)(4,1)S(1)}, s32[]{:S(2)}) async-start(s8[12582912]{0:T(1024)(128)(4,1)} %bitcast.140), calls=%async_computation.11 | async-start | bytes 8388608
  725.7 10.3 slice-start.1
  725.7 10.3 slice-start.2
  736.0 9.4 copy-start.18
  748.5 129.6 %reduce-scatter.7.cloned.1.call-start = ((), (), s32[]{:S(2)}) async-start(), calls=%async_computation.10 | async-start | bytes 7102464 | tf_op jit(solution)/shard_map/reduce_scatter | solution.py:707
  748.6 6.4 copy-start.24
  748.6 7.4 copy-start.20
  748.6 9.6 copy-start.16
  755.9 18.9 %copy-start.32 = (f32[256,32]{0,1:T(8,128)S(1)}, f32[256,32]{0,1:T(8,128)}, u32[]{:S(2)}) copy-start(f32[256,32]{0,1:T(8,128)} %copy-done.31) | copy-start | bytes 98308
  755.9 18.9 %copy-start.38 = (f32[256,32]{0,1:T(8,128)S(1)}, f32[256,32]{0,1:T(8,128)}, u32[]{:S(2)}) copy-start(f32[256,32]{0,1:T(8,128)} %get-tuple-element.137) | copy-start | bytes 98308
  790.1 332.2 %all-gather.14.cloned.1.call-start = ((), (), s32[]{:S(2)}) async-start(), calls=%async_computation.8 | async-start | bytes 2088960 | tf_op jit(solution)/shard_map/all_gather | solution.py:708
  878.1 293.8 %all-gather.16.cloned.1.call-start = ((), (), s32[]{:S(2)}) async-start(), calls=%async_computation.9 | async-start | bytes 29491200 | tf_op jit(solution)/shard_map/all_gather | solution.py:619
  885.4 37.1 %collective-permute-start.5 = (bf16[1,384,1920]{2,1,0:T(8,128)(2,1)S(1)}, bf16[1,384,1920]{2,1,0:T(8,128)(2,1)S(1)}, u32[]{:S(2)}, u32[]{:S(2)}) collective-permute-start(bf16[1,384,1920]{2,1,0:T(8,128)(2,1)S(1)} %get-tuple-element.114), channel_id=1, source_target_pairs={{0,8},{8,16},{16,24},{24,0},{1,9},{9,17},{17,25},{25,1},{2,10},{10... | collective-permute-start | bytes 4423688 | tf_op jit(solution)/shard_map/ppermute | solution.py:379
  886.6 97.1 %collective-permute-start.6 = (bf16[1,384,1920]{2,1,0:T(8,128)(2,1)S(1)}, bf16[1,384,1920]{2,1,0:T(8,128)(2,1)S(1)}, u32[]{:S(2)}, u32[]{:S(2)}) collective-permute-start(bf16[1,384,1920]{2,1,0:T(8,128)(2,1)S(1)} %get-tuple-element.113), channel_id=1, source_target_pairs={{0,16},{8,24},{16,0},{24,8},{1,17},{9,25},{17,1},{25,9},{2,18},{10... | collective-permute-start | bytes 4423688 | tf_op jit(solution)/shard_map/ppermute | solution.py:379
  887.4 97.5 %collective-permute-start.7 = (bf16[1,384,1920]{2,1,0:T(8,128)(2,1)S(1)}, bf16[1,384,1920]{2,1,0:T(8,128)(2,1)S(1)}, u32[]{:S(2)}, u32[]{:S(2)}) collective-permute-start(bf16[1,384,1920]{2,1,0:T(8,128)(2,1)S(1)} %get-tuple-element.112), channel_id=1, source_target_pairs={{0,24},{8,0},{16,8},{24,16},{1,25},{9,1},{17,9},{25,17},{2,26},{10... | collective-permute-start | bytes 4423688 | tf_op jit(solution)/shard_map/ppermute | solution.py:379
  994.2 14.6 %copy-start.9 = (bf16[256,1536]{1,0:T(8,128)(2,1)S(1)}, bf16[256,1536]{1,0:T(8,128)(2,1)}, u32[]{:S(2)}) copy-start(bf16[256,1536]{1,0:T(8,128)(2,1)} %copy-done.8) | copy-start | bytes 2359300
  994.2 14.6 %copy-start.37 = (f32[1536]{0:T(1024)S(1)}, f32[1536]{0:T(1024)}, u32[]{:S(2)}) copy-start(f32[1536]{0:T(1024)} %copy-done.36) | copy-start | bytes 18436
  994.2 14.9 %copy-start.12 = (f32[128,1536]{1,0:T(8,128)S(1)}, f32[128,1536]{1,0:T(8,128)}, u32[]{:S(2)}) copy-start(f32[128,1536]{1,0:T(8,128)} %copy-done.11) | copy-start | bytes 2359300
  994.2 14.9 %copy-start.22 = (bf16[128,1536]{1,0:T(8,128)(2,1)S(1)}, bf16[128,1536]{1,0:T(8,128)(2,1)}, u32[]{:S(2)}) copy-start(bf16[128,1536]{1,0:T(8,128)(2,1)} %constant_dynamic-slice_fusion.9) | copy-start | bytes 1179652
  997.8 11.0 collective-permute-start.4
  1011.3 9.5 all-to-all-start
  1020.8 101.5 %all-to-all-start.1 = ((f32[128,2,768]{2,0,1:T(8,128)}), f32[128,2,768]{2,0,1:T(8,128)S(1)}, u32[]{:S(2)}, u32[]{:S(2)}) async-start(f32[128,2,768]{2,0,1:T(8,128)} %bitcast.135), calls=%async_computation.2 | async-start | bytes 1572864 | tf_op jit(solution)/shard_map/all_to_all | solution.py:703
  1220.6 15.7 %copy-start.1 = (bf16[384,768]{1,0:T(8,128)(2,1)S(1)}, bf16[384,768]{1,0:T(8,128)(2,1)}, u32[]{:S(2)}) copy-start(bf16[384,768]{1,0:T(8,128)(2,1)} %param.22) | copy-start | bytes 1769476
  (16 other events, 40.6 us)
Sparse Core Ops, SparseCore 0:
  10.9 53.7 all-gather.7
  135.6 15.0 all-gather.9
  153.6 104.6 all-gather.11
  748.6 25.1 reduce-scatter.4
  790.2 87.8 reduce-scatter.6
  879.5 19.4 all-gather.13
  993.5 178.4 all-gather.15

commit v3 on v2

--- a/solution.py
+++ b/solution.py
@@ -1,3 +1,5 @@
+import functools
+
 import jax
 import jax.numpy as jnp
 from jax import lax
@@ -45,12 +47,51 @@
     ]
 
 
-def gather_kernel(own_ref, out_ref, local_sem, send_sem, recv_sem):
+def gather_kernel(own_count, *refs):
+    if own_count:
+        own_ref, in_ref, low_ref, out_ref, upper_ref, lower_ref = refs[:6]
+        move_local_sem, move_send_sem, move_recv_sem, local_sem, send_sem, recv_sem = refs[6:]
+    else:
+        own_ref, out_ref, local_sem, send_sem, recv_sem = refs
     nd, width = (out_ref.shape[0], own_ref.shape[2])
     wide = out_ref.shape[-1] != width
     z, y, k, x = place()
     up, down = (device((z + 1) % nd, y, k, x), device((z + nd - 1) % nd, y, k, x))
-    greet([up, down, device(z, y, k, 1 - x), device(z, 1 - y, k, x), device(z, y, 1 - k, x)])
+    greet(partners_of(nd, z, y, k, x))
+    moves, kept = ([], [])
+
+    def move(hop):
+        rows, units = (in_ref.shape[1], low_ref.shape[2] // nd)
+        to_z, from_z = ((z + hop) % nd, (z + nd - hop) % nd)
+        for part in range(3):
+            for e in range(own_count):
+                source_ref, base = (in_ref, part * nd * units) if part < 2 else (low_ref, 0)
+                to_ref = upper_ref if part < 2 else lower_ref
+                columns = pl.ds((part % 2 * own_count + e) * units, units)
+                source = source_ref.at[
+                    (y * 2 + k) * own_count + e,
+                    :,
+                    pl.ds(pl.multiple_of(base + to_z * units, LANES), units),
+                ]
+                target = to_ref.at[pl.ds(pl.multiple_of(z * rows, 16), rows), columns]
+                if hop == 0:
+                    copy = pltpu.make_async_copy(source, target, move_local_sem.at[len(kept)])
+                    copy.start()
+                    kept.append(copy)
+                    continue
+                slot = len(moves)
+                copy = pltpu.make_async_remote_copy(
+                    src_ref=source,
+                    dst_ref=target,
+                    send_sem=move_send_sem.at[slot],
+                    recv_sem=move_recv_sem.at[slot],
+                    device_id=device(to_z, y, k, x),
+                    device_id_type=MESH,
+                )
+                copy.start()
+                arrival = to_ref.at[pl.ds(pl.multiple_of(from_z * rows, 16), rows), columns]
+                moves.append((copy, arrival, slot))
+
     low = jnp.minimum(z, nd - 1 - z)
     places = []
     for step in range(nd):
@@ -131,6 +172,8 @@
                 piece = (step, 0, 0, 0, half)
                 send(piece, links[half][1])
                 send(piece, "k")
+            if own_count:
+                move((step + 1) % nd)
         if 1 <= step < nd + 1:
             for half in range(2):
                 piece = (step - 1, half, 0, 1 - half, half)
@@ -148,8 +191,18 @@
             for dx in range(2):
                 for half in range(2):
                     arrived((step, dy, 1, dx, half))
-    for own_copy in own_copies:
+    for own_copy in own_copies + kept:
         own_copy.wait()
+    for copy, arrival, slot in moves:
+        pltpu.make_async_remote_copy(
+            src_ref=arrival,
+            dst_ref=arrival,
+            send_sem=move_send_sem.at[slot],
+            recv_sem=move_recv_sem.at[slot],
+            device_id=device(z, y, k, 1 - x),
+            device_id_type=MESH,
+        ).wait_recv()
+        copy.wait_send()
     for copy, condition in sends:
         if condition is None:
             copy.wait_send()
@@ -157,31 +210,48 @@
             pl.when(condition)(copy.wait_send)
 
 
-def gather_rows(own, nd, collective_id, wide=False):
+def gather_rows(own, nd, collective_id, wide=False, weights=None, own_count=0):
     rows, width = own.shape
     half = rows // 2
     shape = (nd, 2, 2, 2, half, 2 * width) if wide else (nd, 2, 2, 2, 2, half, width)
+    shapes = [jax.ShapeDtypeStruct(shape, own.dtype)]
+    operands = [own.reshape(2, half, width)]
+    semaphores = [
+        pltpu.SemaphoreType.DMA((2,)),
+        pltpu.SemaphoreType.DMA((nd * 18,)),
+        pltpu.SemaphoreType.DMA((nd * 16,)),
+    ]
+    if weights:
+        depth, count = (nd * weights[0].shape[1], 3 * own_count)
+        operands += list(weights)
+        units = weights[1].shape[2] // nd
+        for parts in (2, 1):
+            shapes.append(jax.ShapeDtypeStruct((depth, parts * own_count * units), own.dtype))
+        semaphores = [
+            pltpu.SemaphoreType.DMA((count,)),
+            pltpu.SemaphoreType.DMA(((nd - 1) * count,)),
+            pltpu.SemaphoreType.DMA(((nd - 1) * count,)),
+        ] + semaphores
     out = pl.pallas_call(
-        gather_kernel,
-        in_specs=[pl.BlockSpec(memory_space=pltpu.VMEM)],
-        out_specs=pl.BlockSpec(memory_space=pl.ANY),
-        out_shape=jax.ShapeDtypeStruct(shape, own.dtype),
-        scratch_shapes=[
-            pltpu.SemaphoreType.DMA((2,)),
-            pltpu.SemaphoreType.DMA((nd * 18,)),
-            pltpu.SemaphoreType.DMA((nd * 16,)),
-        ],
+        functools.partial(gather_kernel, own_count),
+        in_specs=[pl.BlockSpec(memory_space=pltpu.VMEM)]
+        + [pl.BlockSpec(memory_space=pl.ANY)] * (len(operands) - 1),
+        out_specs=[pl.BlockSpec(memory_space=pl.ANY)] * len(shapes),
+        out_shape=shapes,
+        scratch_shapes=semaphores,
         compiler_params=pltpu.CompilerParams(collective_id=collective_id, has_side_effects=True),
         cost_estimate=COST,
         name="gather_rows",
-    )(own.reshape(2, half, width))
-    return out.reshape(-1, shape[-1])
-
-
-def reduce_kernel(
-    part_ref, out_ref, own, from_core, first, second, across, load_sem, send_sem, recv_sem
-):
-    nd = part_ref.shape[0]
+    )(*operands)
+    gathered = out[0].reshape(-1, shape[-1])
+    return (gathered, out[1], out[2]) if weights else gathered
+
+
+def reduce_kernel(count, *refs):
+    parts, moved_ref, out_ref, arrived_ref = (refs[:count], *refs[count : count + 3])
+    own, from_core, first, second, across, load_sem, send_sem, recv_sem = refs[count + 3 : -3]
+    move_local_sem, move_send_sem, move_recv_sem = refs[-3:]
+    nd = parts[0].shape[0]
     z, y, k, x = place()
     greet(partners_of(nd, z, y, k, x))
     order = [hop for hop in (2, 1, 3, 0)] if nd == 4 else list(range(1, nd)) + [0]
@@ -223,32 +293,58 @@
 
         lax.fori_loop(0, to_rows // 16, body, 0)
 
-    core_slot, first_slot, second_slot, across_slot = (0, nd * 4, nd * 8, nd * 10)
+    spans, start = ([], 0)
+    for ref in parts:
+        spans.append(pl.ds(start, ref.shape[-1]))
+        start += ref.shape[-1]
+    first_slot, second_slot, across_slot, core_slot = (0, nd * 4, nd * 6, nd * 7)
     for step, dz in enumerate(order):
         for dy in range(2):
             for dx in range(2):
                 there = pl.ds(spot(step, dy, dx, 0), 2)
                 block = ((z + dz) % nd, (y + dy) % 2)
-                send(
-                    part_ref.at[block[0], block[1], 1 - k, (x + dx) % 2],
-                    from_core.at[there],
-                    device(z, y, 1 - k, x),
-                    core_slot + (step * 2 + dy) * 2 + dx,
-                )
-                load = pltpu.make_async_copy(
-                    part_ref.at[block[0], block[1], k, (x + dx) % 2],
-                    own.at[there],
-                    load_sem.at[len(loads)],
-                )
-                load.start()
-                loads.append(load)
+                for ref, span in zip(parts, spans):
+                    send(
+                        ref.at[block[0], block[1], 1 - k, (x + dx) % 2],
+                        from_core.at[there, :, span],
+                        device(z, y, 1 - k, x),
+                        core_slot + len(loads),
+                    )
+                    load = pltpu.make_async_copy(
+                        ref.at[block[0], block[1], k, (x + dx) % 2],
+                        own.at[there, :, span],
+                        load_sem.at[len(loads)],
+                    )
+                    load.start()
+                    loads.append(load)
     x_partner, y_partner = (device(z, y, k, 1 - x), device(z, 1 - y, k, x))
+    kept = pltpu.make_async_copy(moved_ref.at[z], arrived_ref.at[z], move_local_sem)
+    kept.start()
+    moves = []
+
+    def move(hop):
+        to_z = (z + hop) % nd
+        copy = pltpu.make_async_remote_copy(
+            src_ref=moved_ref.at[to_z],
+            dst_ref=arrived_ref.at[z],
+            send_sem=move_send_sem.at[hop - 1],
+            recv_sem=move_recv_sem.at[hop - 1],
+            device_id=device(to_z, y, k, x),
+            device_id_type=MESH,
+        )
+        copy.start()
+        moves.append((copy, hop))
+
     for step in range(nd + 2):
+        if step == 0 or 3 <= step < nd + 1:
+            move(step - 1 if step else 1)
         if step < nd:
             for at in range(4):
-                loads[step * 4 + at].wait()
                 base = spot(step, 0, 0, 0) + at * 2
-                arrived(from_core.at[pl.ds(base, 2)], core_slot + step * 4 + at)
+                for which, span in enumerate(spans):
+                    slot = (step * 4 + at) * count + which
+                    loads[slot].wait()
+                    arrived(from_core.at[pl.ds(base, 2), :, span], core_slot + slot)
 
             def pair(i, carry, step=step):
                 add(step * 8 + i, from_core, step * 8 + i)
@@ -303,36 +399,255 @@
             return carry
 
         lax.fori_loop(0, own.shape[1] // 16, total, 0)
+    kept.wait()
+    for copy, hop in moves:
+        there = arrived_ref.at[(z + nd - hop) % nd]
+        pltpu.make_async_remote_copy(
+            src_ref=there,
+            dst_ref=there,
+            send_sem=move_send_sem.at[hop - 1],
+            recv_sem=move_recv_sem.at[hop - 1],
+            device_id=x_partner,
+            device_id_type=MESH,
+        ).wait_recv()
+        copy.wait_send()
     for copy in sends:
         copy.wait_send()
 
 
-def reduce_rows(part, nd, collective_id):
-    total, width = part.shape
-    rows = total // (nd * 8)
-    half = rows // 2
+def reduce_rows(parts, moved, nd, collective_id):
+    moved = moved.reshape(nd, moved.shape[0] // nd, moved.shape[1])
+    rows = parts[0].shape[0] // (nd * 8)
+    width = sum(part.shape[1] for part in parts)
+    half, count = (rows // 2, len(parts))
+    sends = nd * (4 * count + 7)
     out = pl.pallas_call(
-        reduce_kernel,
-        in_specs=[pl.BlockSpec(memory_space=pl.ANY)],
-        out_specs=pl.BlockSpec(memory_space=pltpu.VMEM),
-        out_shape=jax.ShapeDtypeStruct((2, half, width), F32),
+        functools.partial(reduce_kernel, count),
+        in_specs=[pl.BlockSpec(memory_space=pl.ANY)] * (count + 1),
+        out_specs=[pl.BlockSpec(memory_space=pltpu.VMEM), pl.BlockSpec(memory_space=pl.ANY)],
+        out_shape=[
+            jax.ShapeDtypeStruct((2, half, width), F32),
+            jax.ShapeDtypeStruct(moved.shape, moved.dtype),
+        ],
         scratch_shapes=[
             pltpu.VMEM((nd * 8, half, width), BF),
             pltpu.VMEM((nd * 8, half, width), BF),
             pltpu.VMEM((nd * 4, half, width), BF),
             pltpu.VMEM((nd * 2, half, width), BF),
             pltpu.VMEM((nd - 1, 2, half, width), BF),
-            pltpu.SemaphoreType.DMA((nd * 4,)),
-            pltpu.SemaphoreType.DMA((nd * 11,)),
-            pltpu.SemaphoreType.DMA((nd * 11,)),
+            pltpu.SemaphoreType.DMA((nd * 4 * count,)),
+            pltpu.SemaphoreType.DMA((sends,)),
+            pltpu.SemaphoreType.DMA((sends,)),
+            pltpu.SemaphoreType.DMA,
+            pltpu.SemaphoreType.DMA((nd - 1,)),
+            pltpu.SemaphoreType.DMA((nd - 1,)),
         ],
         compiler_params=pltpu.CompilerParams(
             collective_id=collective_id, has_side_effects=True, vmem_limit_bytes=48 << 20
         ),
         cost_estimate=COST,
         name="reduce_rows",
-    )(part.reshape(nd, 2, 2, 2, 2, half, width))
-    return out.reshape(rows, width)
+    )(*[part.reshape(nd, 2, 2, 2, 2, half, part.shape[1]) for part in parts], moved)
+    return (out[0].reshape(rows, width), out[1])
+
+
+def sum_kernel(across_dp, part_ref, gain_ref, out_ref, total_ref, *scratch):
+    own, from_core, from_chip, across, result, gains, load_sem, send_sem, recv_sem, gain_sems = scratch
+    nd = part_ref.shape[0]
+    z, y, k, x = place()
+    y_partner, core = (device(z, 1 - y, k, x), device(z, y, 1 - k, x))
+    x_partner = device(z, y, k, 1 - x)
+    greet([device((z + hop) % nd, y, k, x) for hop in range(1, nd)] + [x_partner, y_partner, core])
+    gain_sends = []
+
+    def gain_copy(slot, target):
+        copy = pltpu.make_async_remote_copy(
+            src_ref=gains.at[0, slot],
+            dst_ref=gains.at[1, slot],
+            send_sem=gain_sems.at[0, slot],
+            recv_sem=gain_sems.at[1, slot],
+            device_id=target,
+            device_id_type=MESH,
+        )
+        copy.start()
+        gain_sends.append(copy)
+
+    gains[0, 0] = gain_ref[...]
+    gain_copy(0, core)
+    order = ([2, 1, 3] if nd == 4 else list(range(1, nd))) + [0]
+    sends, loads = ([], [])
+    core_slot, chip_slot, across_slot, result_slot = (0, nd * 2, nd * 3, nd * 4)
+
+    def send(source, there, target, slot):
+        copy = pltpu.make_async_remote_copy(
+            src_ref=source,
+            dst_ref=there,
+            send_sem=send_sem.at[len(sends)],
+            recv_sem=recv_sem.at[slot],
+            device_id=target,
+            device_id_type=MESH,
+        )
+        copy.start()
+        sends.append(copy)
+
+    def arrived(there, slot):
+        pltpu.make_async_remote_copy(
+            src_ref=there,
+            dst_ref=there,
+            send_sem=send_sem.at[0],
+            recv_sem=recv_sem.at[slot],
+            device_id=core,
+            device_id_type=MESH,
+        ).wait_recv()
+
+    def add(to, what, index):
+        def body(i, carry):
+            rows = pl.ds(i * 16, 16)
+            total = own[to, rows, :].astype(F32) + what[index, rows, :].astype(F32)
+            own[to, rows, :] = total.astype(BF)
+            return carry
+
+        lax.fori_loop(0, own.shape[1] // 16, body, 0)
+
+    for step, dz in enumerate(order):
+        for dy in (1, 0):
+            at = step * 2 + dy
+            block = part_ref.at[(z + dz) % nd, (y + dy) % 2]
+            send(block.at[1 - k], from_core.at[at], core, core_slot + at)
+            load = pltpu.make_async_copy(block.at[k], own.at[at], load_sem.at[at])
+            load.start()
+            loads.append(load)
+    stages = [y_partner, x_partner]
+    if nd > 1:
+        stages += [device(z + 1 - z % 2 * 2, y, k, x), device((z + 2) % nd, y, k, x)]
+    for slot, target in enumerate(stages + [None], 1):
+        gain_sends[-1].wait_recv()
+        gains[0, slot] = gains[0, slot - 1] + gains[1, slot - 1]
+        if target is not None:
+            gain_copy(slot, target)
+    total_ref[...] = gains[0, len(stages) + 1]
+    for step in range(nd + 1):
+        if step < nd:
+            for dy in (1, 0):
+                at = step * 2 + dy
+                loads[step * 2 + 1 - dy].wait()
+                arrived(from_core.at[at], core_slot + at)
+                add(at, from_core, at)
+                if dy:
+                    send(own.at[at], from_chip.at[step], y_partner, chip_slot + step)
+        if step:
+            now = step - 1
+            arrived(from_chip.at[now], chip_slot + now)
+            hop = order[now]
+            if hop or across_dp:
+                add(now * 2, from_chip, now)
+            if hop:
+                slot = nd - hop - 1
+                target = device((z + hop) % nd, y, k, x)
+                send(own.at[now * 2], across.at[slot], target, across_slot + slot)
+    for slot in range(nd - 1):
+        arrived(across.at[slot], across_slot + slot)
+    mine = (nd - 1) * 2
+
+    def total(i, carry):
+        rows = pl.ds(i * 16, 16)
+        value = own[mine, rows, :].astype(F32)
+        if across_dp:
+            for slot in range(nd - 1):
+                value = value + across[slot, rows, :].astype(F32)
+            result[y, k, rows, :] = value.astype(BF)
+        else:
+            out_ref[rows, :] = value + from_chip[0, rows, :].astype(F32)
+        return carry
+
+    lax.fori_loop(0, own.shape[1] // 16, total, 0)
+    if across_dp:
+        send(result.at[y, k], result.at[y, k], y_partner, result_slot)
+        send(result.at[y, k], result.at[y, k], core, result_slot + 1)
+        arrived(result.at[1 - y, k], result_slot)
+        send(result.at[1 - y, k], result.at[1 - y, k], core, result_slot + 2)
+        arrived(result.at[y, 1 - k], result_slot + 1)
+        arrived(result.at[1 - y, 1 - k], result_slot + 2)
+
+        def widen(i, carry):
+            rows = pl.ds(i * 16, 16)
+            for chip in range(2):
+                for side in range(2):
+                    out_ref[chip, side, rows, :] = result[chip, side, rows, :].astype(F32)
+            return carry
+
+        lax.fori_loop(0, own.shape[1] // 16, widen, 0)
+    for copy in gain_sends:
+        copy.wait_send()
+    for copy in sends:
+        copy.wait_send()
+
+
+def sum_blocks(part, gain, nd, collective_id):
+    rows, width = (part.shape[0] // (nd * 4), part.shape[1])
+    shape = (2, 2, rows, width) if nd > 1 else (rows, width)
+    out = pl.pallas_call(
+        functools.partial(sum_kernel, nd > 1),
+        in_specs=[pl.BlockSpec(memory_space=pl.ANY), pl.BlockSpec(memory_space=pltpu.VMEM)],
+        out_specs=[pl.BlockSpec(memory_space=pltpu.VMEM)] * 2,
+        out_shape=[jax.ShapeDtypeStruct(shape, F32), jax.ShapeDtypeStruct(gain.shape, F32)],
+        scratch_shapes=[
+            pltpu.VMEM((nd * 2, rows, width), BF),
+            pltpu.VMEM((nd * 2, rows, width), BF),
+            pltpu.VMEM((nd, rows, width), BF),
+            pltpu.VMEM((max(nd - 1, 1), rows, width), BF),
+            pltpu.VMEM((2, 2, rows, width) if nd > 1 else (1, 1, 16, LANES), BF),
+            pltpu.VMEM((2, 6, *gain.shape), F32),
+            pltpu.SemaphoreType.DMA((nd * 2,)),
+            pltpu.SemaphoreType.DMA((nd * 4 + 3,)),
+            pltpu.SemaphoreType.DMA((nd * 4 + 3,)),
+            pltpu.SemaphoreType.DMA((2, 5)),
+        ],
+        compiler_params=pltpu.CompilerParams(
+            collective_id=collective_id, has_side_effects=True, vmem_limit_bytes=48 << 20
+        ),
+        cost_estimate=COST,
+        name="sum_blocks",
+    )(part.reshape(nd, 2, 2, rows, width), gain)
+    return (out[0].reshape(-1, width), out[1])
+
+
+def spread_kernel(up_ref, low_ref, in_ref, out_ref):
+    nc, nd = up_ref.shape[:2]
+    own_count = in_ref.shape[0] // nc
+    units = low_ref.shape[3] // own_count
+    for c in range(nc):
+        for e in range(own_count):
+            for part in range(3):
+                got_ref, to_ref, base = ((up_ref, in_ref, part) if part < 2 else (low_ref, out_ref, 0))
+                start = (base * own_count + e) * units
+                for at in range(nd):
+                    columns = slice((base * nd + at) * units, (base * nd + at + 1) * units)
+                    to_ref[c * own_count + e, :, columns] = got_ref[
+                        c, at, :, start : start + units
+                    ].astype(F32)
+
+
+def spread(up, low, own_count):
+    nc, nd, d_local, low_width = low.shape
+    experts, units = (nc * own_count, low_width // own_count)
+    block = 32
+    into, out = pl.pallas_call(
+        spread_kernel,
+        grid=(d_local // block,),
+        in_specs=[
+            pl.BlockSpec((nc, nd, block, ref.shape[3]), lambda i: (0, 0, i, 0)) for ref in (up, low)
+        ],
+        out_specs=[
+            pl.BlockSpec((experts, block, parts * nd * units), lambda i: (0, i, 0))
+            for parts in (2, 1)
+        ],
+        out_shape=[
+            jax.ShapeDtypeStruct((experts, d_local, parts * nd * units), F32) for parts in (2, 1)
+        ],
+        name="spread",
+    )(up, low)
+    return (jnp.transpose(into, (1, 0, 2)), jnp.transpose(out, (1, 0, 2)))
 
 
 def rope_tables(position):
@@ -379,29 +694,6 @@
         got = lax.ppermute(sent, "dp", [(i, (i + hop) % count) for i in range(count)])
         result = lax.dynamic_update_index_in_dim(result, got, (at - hop) % count, 0)
     return result
-
-
-def expert_major_kernel(gate_ref, up_ref, low_ref, out_ref):
-    count, units = (gate_ref.shape[0], gate_ref.shape[2])
-    for part, ref in enumerate((gate_ref, up_ref, low_ref)):
-        for at in range(count):
-            out_ref[0, :, (part * count + at) * units : (part * count + at + 1) * units] = ref[at]
-
-
-def expert_major(received, own_count, units):
-    nd, d_local, _ = received.shape
-
-    def spec(part):
-        return pl.BlockSpec((nd, d_local, units), lambda e: (0, 0, part * own_count + e))
-
-    return pl.pallas_call(
-        expert_major_kernel,
-        grid=(own_count,),
-        in_specs=[spec(0), spec(1), spec(2)],
-        out_specs=pl.BlockSpec((1, d_local, 3 * nd * units), lambda e: (e, 0, 0)),
-        out_shape=jax.ShapeDtypeStruct((own_count, d_local, 3 * nd * units), received.dtype),
-        name="expert_major",
-    )(received, received, received)
 
 
 def scatter_rows(partial, at, count):
@@ -463,8 +755,15 @@
         tiled=True,
     )
     kernels = (nd, nc, nt) == (4, 4, 2)
+    by_expert = local_count % nc == 0
+    own_count = local_count // nc if by_expert else local_count
+    units = FF // nd if by_expert else FF // (nd * nc)
+    width = own_count * units
     if kernels:
-        cot_all = gather_rows(cotangent, nd, 1, wide=True)
+        natural = [jnp.transpose(w, (1, 0, 2)) for w in (w_expert_in, w_expert_out)]
+        cot_all, upper_w, lower_w = gather_rows(
+            cotangent, nd, 1, wide=True, weights=natural, own_count=own_count
+        )
         cot_sub = lax.dynamic_slice_in_dim(
             cot_all, (dp_at * nc + ctx_at) * n_rows + tensor_at * sub, sub, 0
         )
@@ -473,26 +772,23 @@
         cot_all = lax.all_gather(cot_sub, ALL, axis=0, tiled=True)
     tokens_sub = lax.dynamic_slice_in_dim(tokens_full, tensor_at * sub, sub, 0).astype(F32)
 
-    by_expert = local_count % nc == 0
-    own_count = local_count // nc if by_expert else local_count
-    units = FF // nd if by_expert else FF // (nd * nc)
     first_expert = tensor_at * local_count + (ctx_at * own_count if by_expert else 0)
-    if by_expert:
-        own_in = lax.dynamic_slice_in_dim(w_expert_in, ctx_at * own_count, own_count, 1)
-        own_out = lax.dynamic_slice_in_dim(w_expert_out, ctx_at * own_count, own_count, 1)
-        own_in = own_in.reshape(d_local, own_count, 2, nd, units)
-        own_out = own_out.reshape(d_local, own_count, nd, units)
-    else:
-        own_in = w_expert_in.reshape(d_local, own_count, 2, nd, nc, units)
-        own_out = w_expert_out.reshape(d_local, own_count, nd, nc, units)
-        own_in = lax.dynamic_index_in_dim(own_in, ctx_at, 4, False)
-        own_out = lax.dynamic_index_in_dim(own_out, ctx_at, 3, False)
-    own_in = jnp.transpose(own_in, (3, 0, 2, 1, 4)).reshape(nd, d_local, 2 * own_count * units)
-    own_out = jnp.transpose(own_out, (2, 0, 1, 3)).reshape(nd, d_local, own_count * units)
-    width = own_count * units
-    expert_parts = jnp.concatenate([own_in, own_out], axis=2)
-    tokens_full, expert_parts = lax.optimization_barrier((tokens_full, expert_parts))
-    expert_w = exchange(expert_parts, dp_at, nd)
+    if not kernels:
+        if by_expert:
+            own_in = lax.dynamic_slice_in_dim(w_expert_in, ctx_at * own_count, own_count, 1)
+            own_out = lax.dynamic_slice_in_dim(w_expert_out, ctx_at * own_count, own_count, 1)
+            own_in = own_in.reshape(d_local, own_count, 2, nd, units)
+            own_out = own_out.reshape(d_local, own_count, nd, units)
+        else:
+            own_in = w_expert_in.reshape(d_local, own_count, 2, nd, nc, units)
+            own_out = w_expert_out.reshape(d_local, own_count, nd, nc, units)
+            own_in = lax.dynamic_index_in_dim(own_in, ctx_at, 4, False)
+            own_out = lax.dynamic_index_in_dim(own_out, ctx_at, 3, False)
+        own_in = jnp.transpose(own_in, (3, 0, 2, 1, 4)).reshape(nd, d_local, 2 * width)
+        own_out = jnp.transpose(own_out, (2, 0, 1, 3)).reshape(nd, d_local, width)
+        expert_w = exchange(jnp.concatenate([own_in, own_out], axis=2), dp_at, nd)
+        expert_w = expert_w.reshape(D, 3 * width)
+        upper_w, lower_w = (expert_w[:, : 2 * width], expert_w[:, 2 * width :])
 
     order_row = order[0]
     places = jnp.arange(pack_len, dtype=jnp.int32)
@@ -562,9 +858,6 @@
     gates_low = (gates_kept - gates_high.astype(F32)).astype(BF)
     extra = jnp.zeros((sub, LANES - 2 * EXPERTS), BF)
     h_ext = jnp.concatenate([h_two, gates_high, gates_low, extra], axis=1)
-    h_ext, expert_w = lax.optimization_barrier((h_ext, expert_w))
-    expert_w = expert_w.reshape(D, 3 * width)
-    upper_w, lower_w = (expert_w[:, : 2 * width], expert_w[:, 2 * width :])
     if kernels:
         h_all = gather_rows(h_ext, nd, 2)
     else:
@@ -600,31 +893,29 @@
         jnp.zeros((total_rows, LANES), BF), grad_gates.astype(BF), first_expert, 1
     )
     mixed = dot(active_gated, lower_w, ((1,), (1,))).astype(BF)
-    back = jnp.concatenate([grad_in, grad_gates], axis=1)
     grad_upper = dot(h_all, grad_hidden, ((0,), (0,))).astype(BF)
     grad_lower = dot(cot_all, active_gated, ((0,), (0,))).astype(BF)
-    grad_expert = jnp.concatenate([grad_upper, grad_lower], axis=1).reshape(nd, d_local, 3 * width)
     if kernels:
-        back, grad_expert = lax.optimization_barrier((back, grad_expert))
-        back_sub = reduce_rows(back, nd, 3)
+        grad_in, grad_upper, grad_lower = lax.optimization_barrier((grad_in, grad_upper, grad_lower))
+        back_sub, grad_upper = reduce_rows([grad_in, grad_gates], grad_upper, nd, 3)
         mixed, back_sub = lax.optimization_barrier((mixed, back_sub))
-        mixed_sub = reduce_rows(mixed, nd, 4)
+        mixed_sub, grad_lower = reduce_rows([mixed], grad_lower, nd, 4)
         back_sub, mixed_sub = lax.optimization_barrier((back_sub, mixed_sub))
+        grad_upper = lax.all_gather(grad_upper, "ctx", axis=0)
+        grad_lower = lax.all_gather(grad_lower, "ctx", axis=0)
+        grad_expert_in, grad_expert_out = spread(grad_upper, grad_lower, own_count)
     else:
+        back = jnp.concatenate([grad_in, grad_gates], axis=1)
         back_sub = lax.psum_scatter(back, ALL, scatter_dimension=0, tiled=True).astype(F32)
         mixed_sub = lax.psum_scatter(mixed, ALL, scatter_dimension=0, tiled=True).astype(F32)
-    grad_expert = exchange(grad_expert, dp_at, nd)
-    if by_expert:
-        grad_expert = expert_major(grad_expert, own_count, units)
-        grad_expert = lax.all_gather(grad_expert, "ctx", axis=0, tiled=True)
-        grad_expert = jnp.transpose(grad_expert, (1, 0, 2)).astype(F32)
-        grad_expert_in, grad_expert_out = (grad_expert[..., : 2 * FF], grad_expert[..., 2 * FF :])
-    else:
+        grad_expert = jnp.concatenate([grad_upper, grad_lower], axis=1)
+        grad_expert = exchange(grad_expert.reshape(nd, d_local, 3 * width), dp_at, nd)
         grad_expert = lax.all_gather(grad_expert, "ctx", axis=0)
-        grad_up = grad_expert[..., : 2 * width].reshape(nc, nd, d_local, 2, own_count, units)
-        grad_low = grad_expert[..., 2 * width :].reshape(nc, nd, d_local, own_count, units)
-        grad_up = jnp.transpose(grad_up, (2, 4, 3, 1, 0, 5))
-        grad_low = jnp.transpose(grad_low, (2, 3, 1, 0, 4))
+        split = (1, nc) if by_expert else (nc, 1)
+        grad_up = grad_expert[..., : 2 * width].reshape(*split, nd, d_local, 2, own_count, units)
+        grad_low = grad_expert[..., 2 * width :].reshape(*split, nd, d_local, own_count, units)
+        grad_up = jnp.transpose(grad_up, (3, 1, 5, 4, 2, 0, 6))
+        grad_low = jnp.transpose(grad_low, (3, 1, 4, 2, 0, 5))
         grad_expert_in = grad_up.reshape(d_local, local_count, 2 * FF).astype(F32)
         grad_expert_out = grad_low.reshape(d_local, local_count, FF).astype(F32)
 
@@ -670,15 +961,13 @@
     grad_values = jnp.einsum(
         "agbp,bagd->pad", shares_low, grad_blended, preferred_element_type=F32
     )
-    grad_kv = lax.psum_scatter(
-        jnp.concatenate(
-            [grad_keys.reshape(pack_len, kv_width), grad_values.reshape(pack_len, kv_width)],
-            axis=1,
-        ).astype(BF),
-        "ctx",
-        scatter_dimension=0,
-        tiled=True,
-    ).astype(F32)
+    grad_kv = jnp.concatenate(
+        [grad_keys.reshape(pack_len, kv_width), grad_values.reshape(pack_len, kv_width)], axis=1
+    ).astype(BF)
+    if kernels:
+        grad_kv, _ = sum_blocks(grad_kv, jnp.zeros((8, LANES), F32), 1, 5)
+    else:
+        grad_kv = lax.psum_scatter(grad_kv, "ctx", scatter_dimension=0, tiled=True).astype(F32)
     grad_turned = jnp.concatenate(
         [
             grad_queries.reshape(n_rows, q_heads, HEAD_DIM),
@@ -703,13 +992,18 @@
     grad_tokens = lax.all_to_all(grad_tokens + grad_middle, "tensor", 1, 0, tiled=True)
 
     grad_qkv_w = dot(h_one, grad_qkv, ((0,), (0,)))
-    weight_grads = jnp.concatenate([grad_qkv_w, grad_output_w, grad_router], axis=1).astype(BF)
-    weight_grads = lax.psum_scatter(weight_grads, ("dp", "ctx"), scatter_dimension=0, tiled=True)
-    weight_grads = lax.all_gather(weight_grads, "ctx", axis=0, tiled=True).astype(F32)
+    gain_grads = jnp.stack([grad_gain_one, grad_gain_two])
+    extra = jnp.zeros((D, LANES - EXPERTS), F32)
+    weight_grads = jnp.concatenate([grad_qkv_w, grad_output_w, grad_router, extra], axis=1).astype(BF)
+    if kernels:
+        weight_grads, gain_grads = sum_blocks(weight_grads, gain_grads, nd, 6)
+    else:
+        weight_grads = lax.psum_scatter(
+            weight_grads, ("dp", "ctx"), scatter_dimension=0, tiled=True
+        )
+        weight_grads = lax.all_gather(weight_grads, "ctx", axis=0, tiled=True).astype(F32)
+        gain_grads = jnp.sum(lax.all_gather(gain_grads, ALL, axis=0), axis=0)
     edges = [0, q_width, q_width + kv_width, qkv_width, qkv_width + q_width]
-    gain_grads = jnp.sum(
-        lax.all_gather(jnp.stack([grad_gain_one, grad_gain_two]), ALL, axis=0), axis=0
-    )
     gain_grads = lax.dynamic_slice_in_dim(gain_grads, tensor_at * part_width, part_width, 1)
     return (
         result,
@@ -720,7 +1014,7 @@
         weight_grads[:, edges[2] : edges[3]],
         weight_grads[:, edges[3] : edges[4]],
         gain_grads[1],
-        weight_grads[:, edges[4] :],
+        weight_grads[:, edges[4] : edges[4] + EXPERTS],
         grad_expert_in,
         grad_expert_out,
     )

time: 1250 us -> 1060 us (0.85)
  Pallas kernels: 292 us -> 622 us
  waiting for transfers between devices: 358 us -> 86.2 us
  blocking collectives: 127 us -> 26.1 us
  local copies, waits for them, and re-layouts: 174 us -> 83.8 us
  other arithmetic: 90 us -> 38.2 us
    pallas_call x5 -> x7, Pallas kernels: 292 us -> 622 us  [the longest x2 264 us: gather_rows(): pl.pallas_call(functools.partial(gather_kernel, own_count), in_specs=[pl....]
    ppermute x6 -> x0, waiting for transfers between devices: 197 us -> none  [exchange(): lax.ppermute(sent, 'dp', [(i, (i + hop) % count) for i in range(count)])]
    reduce_scatter x2 -> x0, waiting for transfers between devices: 99.5 us -> none  [the longest x1 87.8 us: on_device(): lax.psum_scatter(weight_grads, ('dp', 'ctx'), scatter_dimension=0, tiled=...]
    all_gather x1 -> x0, blocking collectives: 97.1 us -> none  [on_device(): lax.all_gather(jnp.stack([grad_gain_one, grad_gain_two]), ALL, axis=0)]
    all_gather x2, waiting for transfers between devices: 43.2 us -> 0.01 us  [the longest x1 0.01 us: on_device(): grad_lower = lax.all_gather(grad_lower, 'ctx', axis=0)]
    all_gather x1, waiting for transfers between devices: 0.02 us -> 41.9 us  [on_device(): kv_all = lax.all_gather(kv_rows, 'ctx', axis=0, tiled=True)]
    slice x3, local copies, waits for them, and re-layouts: 37.7 us -> 1.73 us  [the longest x1 0.94 us: on_device(): weight_grads[:, edges[4]:edges[4] + EXPERTS]]
    all_gather x1, waiting for transfers between devices: 0.02 us -> 29.7 us  [on_device(): lax.all_gather(lax.dynamic_slice_in_dim(w_output, ctx_at * share, share,...]
  transfers between devices with their start and end apart: 17 -> 9, of which waited for: 10 -> 4; matrix products, arithmetic and copies ran while one was open for 10% -> 11% of each run, Pallas kernels for 5% -> 29%
where the time goes in v3:
time: 1060 us; the launch traced here: 1050 us
  Pallas kernels  622 us (59%)
  matrix products  168 us (16%)
  waiting for transfers between devices  86.2 us (8%)
  local copies, waits for them, and re-layouts  83.8 us (8%)
  other arithmetic  38.2 us (4%)
  blocking collectives  26.1 us (2%)
  between operations  15.1 us (1%)
    pallas_call x2, Pallas kernels, gather_rows(): pl.pallas_call(functools.partial(gather_kernel, own_count), in_specs=[pl....  264 us
    pallas_call x2, Pallas kernels, reduce_rows(): pl.pallas_call(functools.partial(reduce_kernel, count), in_specs=[pl.Bloc...  228 us
    dot_general x16, matrix products, dot(): return lax.dot_general(a, b, (dims, ((), ())), preferred_element_type=F32)  147 us
    pallas_call x2, Pallas kernels, sum_blocks(): pl.pallas_call(functools.partial(sum_kernel, nd > 1), in_specs=[pl.BlockS...  104 us
    all_gather x1, waiting for transfers between devices, on_device(): kv_all = lax.all_gather(kv_rows, 'ctx', axis=0, tiled=True)  41.9 us
    all_gather x1, waiting for transfers between devices, on_device(): lax.all_gather(lax.dynamic_slice_in_dim(w_output, ctx_at * share, share,...  29.7 us
    pallas_call x1, Pallas kernels, spread(): pl.pallas_call(spread_kernel, grid=(d_local // block,), in_specs=[pl.Bloc...  25.6 us
  transfers between devices with their start and end apart: 9, of which 4 were waited for; matrix products, arithmetic and copies ran while one was open for 11% of the time, Pallas kernels for 29%

profile of v3, /device:TPU:0, one launch (start us, length us, event | category | flops | bytes accessed | tf_op | source)
XLA Modules:
  0.0 1047.8 jit_solution(462400050316842747)
XLA Ops:
  8.2 1.6 fusion.36
  11.3 201.5 %gather_rows.2 = (bf16[4,2,2,2,128,1536]{5,4,3,2,1,0:T(8,128)(2,1)}, bf16[1536,1280]{1,0:T(8,128)(2,1)}, bf16[1536,640]{1,0:T(8,128)(2,1)}) custom-call(bf16[2,128,768]{2,1,0:T(8,128)(2,1)} %bitcast.198, bf16[20,384,1024]{2,1,0:T(8,128)(2,1)} %bitcast.163, bf16[20,384,512]{2,1,0:T(8,128)(2,1)} %bitcast.172), custom_call_target="tpu_custom_call" | custom-call | bytes 250000000 | tf_op jit(solution)/shard_map/gather_rows/pallas_call | solution.py:235
  212.8 4.4 all_gather.31
  217.3 9.5 all_gather.30
  227.0 1.8 constant_dynamic-slice_fusion.3
  230.8 3.3 fusion.9
  235.8 1.6 copy.125
  238.4 1.6 pad_maximum_fusion.10
  244.0 41.9 %all-gather.10.cloned.1.call-done = bf16[1024,512]{1,0:T(8,128)(2,1)} async-done(((bf16[256,512]{1,0:T(8,128)(2,1)}), bf16[1024,512]{1,0:T(8,128)(2,1)}) %all-gather.10.cloned.1.call-update) | async-done | bytes 1048592 | tf_op jit(solution)/shard_map/all_gather | solution.py:829
  287.6 2.0 fusion.6
  289.6 2.6 fusion.3
  292.2 1.9 copy-done.5
  294.1 3.4 divide_convert_fusion
  297.6 2.6 copy-done.6
  301.4 29.7 %all-gather.12.cloned.1.call-done = bf16[1536,768]{1,0:T(8,128)(2,1)} async-done(((bf16[96,768]{1,0:T(8,128)(2,1)}), bf16[1536,768]{1,0:T(8,128)(2,1)}) %all-gather.12.cloned.1.call-update) | async-done | bytes 2359312 | tf_op jit(solution)/shard_map/all_gather | solution.py:751
  331.1 2.5 fusion.66
  334.4 1.5 collective-permute-start
  336.1 9.7 collective-permute-done
  347.7 1.3 fusion.65
  351.1 62.0 %gather_rows.3 = bf16[4,2,2,2,2,64,1664]{6,5,4,3,2,1,0:T(8,128)(2,1)} custom-call(bf16[2,64,1664]{2,1,0:T(8,128)(2,1)} %bitcast.192), custom_call_target="tpu_custom_call" | custom-call | bytes 250000000 | tf_op jit(solution)/shard_map/gather_rows/pallas_call | solution.py:235
  413.1 2.0 fusion.61
  415.1 22.6 %fusion.59 = f32[4096,1280]{0,1:T(8,128)} fusion(bf16[1536,1280]{1,0:T(8,128)(2,1)} %get-tuple-element.35, bf16[4096,1664]{1,0:T(8,128)(2,1)} %bitcast.158), kind=kOutput, calls=%fused_computation.168 | convolution fusion | flops 16106127360 | bytes 37486592 | tf_op jit(solution)/shard_map/dot_general | solution.py:673
  438.9 28.7 %multiply_convert_fusion.1 = (bf16[4096,640]{0,1:T(8,128)(2,1)}, bf16[4096,640]{0,1:T(8,128)(2,1)}, f32[4096,640]{0,1:T(8,128)}, bf16[4096,640]{0,1:T(8,128)(2,1)}) fusion(f32[4096,1280]{0,1:T(8,128)} %fusion.59, f32[4096,5]{0,1:T(8,128)S(1)} %copy.132, bf16[4096,1536]{1,0:T(8,128)(2,1)} %bitcast.166, bf16[1536,640]{1,0:T(8,128)(2,1)} %get-tuple-element.36), kind=kOutput, calls=%fused_computation.18 | convolution fusion | flops 8100249600 | bytes 61816832 | tf_op jit(solution)/shard_map/dot_general | solution.py:673
  467.6 23.6 %convolution_convert_fusion.1 = bf16[4096,1536]{1,0:T(8,128)(2,1)} fusion(bf16[1536,1280]{1,0:T(8,128)(2,1)} %get-tuple-element.35, bf16[4096,640]{0,1:T(8,128)(2,1)} %get-tuple-element.70, bf16[4096,640]{0,1:T(8,128)(2,1)} %get-tuple-element.69), kind=kOutput, calls=%fused_computation.3 | convolution fusion | flops 16133390336 | bytes 27000832 | tf_op jit(solution)/shard_map/dot_general | solution.py:673
  491.2 23.5 %convolution_convert_fusion.2 = bf16[1536,1280]{1,0:T(8,128)(2,1)} fusion(bf16[4096,640]{0,1:T(8,128)(2,1)} %get-tuple-element.70, bf16[4096,640]{0,1:T(8,128)(2,1)} %get-tuple-element.69, bf16[4096,1664]{1,0:T(8,128)(2,1)} %bitcast.159), kind=kOutput, calls=%fused_computation.22 | convolution fusion | flops 16129064960 | bytes 27000832 | tf_op jit(solution)/shard_map/dot_general | solution.py:673
  514.7 3.9 fusion.4
  518.6 12.8 %convolution_convert_fusion = bf16[4096,1536]{1,0:T(8,128)(2,1)} fusion(bf16[4096,640]{0,1:T(8,128)(2,1)S(1)} %fusion.4, bf16[1536,640]{1,0:T(8,128)(2,1)S(1)} %copy-done.33), kind=kOutput, calls=%fused_computation.2 | convolution fusion | flops 8059355136 | bytes 19791872 | tf_op jit(solution)/shard_map/dot_general | solution.py:673
  531.5 11.7 %convolution_convert_fusion.4 = bf16[1536,640]{1,0:T(8,128)(2,1)} fusion(bf16[4096,1536]{1,0:T(8,128)(2,1)S(1)} %bitcast.169, bf16[4096,640]{0,1:T(8,128)(2,1)S(1)} %fusion.4), kind=kOutput, calls=%fused_computation.31 | convolution fusion | flops 8054046720 | bytes 19791872 | tf_op jit(solution)/shard_map/dot_general | solution.py:673
  543.1 4.7 reduce_sum.132
  548.5 3.9 dynamic_update_slice.3
  552.4 120.3 %reduce_rows.2 = (f32[2,64,1664]{2,1,0:T(8,128)S(1)}, bf16[4,384,1280]{2,1,0:T(8,128)(2,1)S(1)}) custom-call(bf16[4,2,2,2,2,64,1536]{6,5,4,3,2,1,0:T(8,128)(2,1)} %bitcast.171, bf16[4,2,2,2,2,64,128]{6,5,4,3,2,1,0:T(8,128)(2,1)S(1)} %bitcast.149, bf16[4,384,1280]{2,1,0:T(8,128)(2,1)} %bitcast.181), custom_call_target="tpu_custom_call" | custom-call | bytes 250000000 | tf_op jit(solution)/shard_map/reduce_rows/pallas_call | solution.py:424
  672.7 1.9 copy-done.2
  674.6 108.1 %reduce_rows.3 = (f32[2,64,1536]{2,1,0:T(8,128)S(1)}, bf16[4,384,640]{2,1,0:T(8,128)(2,1)}) custom-call(bf16[4,2,2,2,2,64,1536]{6,5,4,3,2,1,0:T(8,128)(2,1)} %bitcast.170, bf16[4,384,640]{2,1,0:T(8,128)(2,1)S(1)} %bitcast.155), custom_call_target="tpu_custom_call" | custom-call | bytes 250000000 | tf_op jit(solution)/shard_map/reduce_rows/pallas_call | solution.py:424
  786.3 1.5 multiply_reduce_fusion
  789.1 12.2 %all_gather.35 = bf16[256,1664]{1,0:T(8,128)(2,1)S(1)} all-gather(bf16[128,1664]{1,0:T(8,128)(2,1)S(1)} %concatenate.59), channel_id=1, replica_groups=mesh['dp'=4,'ctx'=4,'tensor'=2] {'tensor'}, dimensions={0}, use_global_device_ids=true | all-gather | bytes 1277952 | tf_op jit(solution)/shard_map/all_gather | solution.py:932
  802.2 3.3 convolution_convert_fusion.7
  806.6 5.6 fusion.18
  812.2 2.2 concatenate.61
  814.4 2.1 copy.142
  816.5 6.5 fusion
  823.1 6.7 fusion.2
  829.8 2.7 copy-done.7
  832.5 2.0 fusion.19
  835.5 15.2 %sum_blocks.2 = (f32[256,512]{1,0:T(8,128)S(1)}, f32[8,128]{1,0:T(8,128)}) custom-call(bf16[1,2,2,256,512]{4,3,2,1,0:T(8,128)(2,1)S(1)} %pad_maximum_fusion.3.part_ref, f32[8,128]{1,0:T(8,128)S(1)} %broadcast_in_dim.49.gain_ref), custom_call_target="tpu_custom_call" | custom-call | bytes 250000000 | tf_op jit(solution)/shard_map/sum_blocks/pallas_call | solution.py:589
  850.9 12.0 %slice.140 = bf16[4096,1536]{1,0:T(8,128)(2,1)} slice(bf16[4096,1664]{1,0:T(8,128)(2,1)} %bitcast.160), slice={[0:4096], [0:1536]} | slice | bytes 25165824 | tf_op jit(solution)/shard_map/slice | solution.py:870
  863.8 4.0 convolution_multiply_fusion
  868.0 3.6 fusion.7
  874.6 2.3 copy.146
  876.9 2.1 convolution_convert_fusion.5
  879.0 1.8 copy.148
  880.8 3.2 convolution_convert_fusion.3
  884.0 2.2 convolution_convert_fusion.6
  886.3 10.6 %concatenate.68.part_ref = bf16[4,2,2,96,2176]{4,3,2,1,0:T(8,128)(2,1)} concatenate(bf16[4,2,2,96,1280]{4,3,2,1,0:T(8,128)(2,1)} %bitcast.162, bf16[4,2,2,96,768]{4,3,2,1,0:T(8,128)(2,1)} %convolution_convert_fusion.6, bf16[4,2,2,96,40]{4,3,2,1,0:T(8,128)(2,1)} %bitcast.195, bf16[4,2,2,96,88]{4,3,2,1,0:T(8,128)(2,1)S(1)} %broadcast_in_dim.50), dimensions={4} | concatenate | bytes 13369344 | tf_op jit(solution)/shard_map/concatenate | solution.py:997
  896.9 1.5 fusion.27
  898.5 2.9 fusion.25
  902.1 3.5 all-to-all-start
  905.6 2.1 copy.165
  907.7 89.1 %sum_blocks.3 = (f32[2,2,96,2176]{3,2,1,0:T(8,128)S(1)}, f32[2,1536]{1,0:T(2,128)S(1)}) custom-call(bf16[4,2,2,96,2176]{4,3,2,1,0:T(8,128)(2,1)} %concatenate.68.part_ref, f32[2,1536]{1,0:T(2,128)S(1)} %pad_maximum_fusion.12.gain_ref), custom_call_target="tpu_custom_call" | custom-call | bytes 250000000 | tf_op jit(solution)/shard_map/sum_blocks/pallas_call | solution.py:589
  996.8 1.7 copy-done.3
  998.5 3.5 all-to-all-start.1
  1002.0 2.0 fusion.63
  1006.4 3.2 fusion.62
  1009.6 4.3 all-to-all-done.1
  1013.9 25.6 %spread.1 = (f32[20,384,1024]{2,1,0:T(8,128)}, f32[20,384,512]{2,1,0:T(8,128)}) custom-call(bf16[4,4,384,1280]{3,2,1,0:T(8,128)(2,1)} %bitcast.164, bf16[4,4,384,640]{3,2,1,0:T(8,128)(2,1)} %bitcast.173), custom_call_target="tpu_custom_call" | custom-call | tf_op jit(solution)/shard_map/spread/pallas_call | solution.py:635
  (219 shorter events, 37.7 us)
Async XLA Ops:
  7.2 232.9 %copy-start = (bf16[384,768]{1,0:T(8,128)(2,1)S(1)}, bf16[384,768]{1,0:T(8,128)(2,1)}, u32[]{:S(2)}) copy-start(bf16[384,768]{1,0:T(8,128)(2,1)} %param.22) | copy-start | bytes 1769476
  7.2 223.6 %all-gather.8.cloned.1.call-start = ((), (), s32[]{:S(2)}) async-start(), calls=%async_computation.2 | async-start | bytes 4595712 | tf_op jit(solution)/shard_map/all_gather | solution.py:749
  9.8 276.1 %all-gather.10.cloned.1.call-start = ((), (), s32[]{:S(2)}) async-start(), calls=%async_computation.3 | async-start | bytes 1310720 | tf_op jit(solution)/shard_map/all_gather | solution.py:829
  11.3 206.0 %copy-start.36 = (bf16[256,768]{1,0:T(8,128)(2,1)S(1)}, bf16[256,768]{1,0:T(8,128)(2,1)}, u32[]{:S(2)}) copy-start(bf16[256,768]{1,0:T(8,128)(2,1)} %param.14) | copy-start | bytes 1179652
  11.3 217.8 %copy-start.51 = (s32[1,1024]{1,0:T(1,128)S(1)}, s32[1,1024]{1,0:T(1,128)}, u32[]{:S(2)}) copy-start(s32[1,1024]{1,0:T(1,128)} %param.15) | copy-start | bytes 12292
  217.3 17.5 %copy-start.47 = (f32[1536]{0:T(1024)}, f32[1536]{0:T(1024)S(1)}, u32[]{:S(2)}) copy-start(f32[1536]{0:T(1024)S(1)} %get-tuple-element.62) | copy-start | bytes 18436
  217.3 129.4 %copy-start.43 = (f32[1536]{0:T(1024)}, f32[1536]{0:T(1024)S(1)}, u32[]{:S(2)}) copy-start(f32[1536]{0:T(1024)S(1)} %get-tuple-element.61) | copy-start | bytes 18436
  226.8 119.1 %copy-start.12 = (bf16[256,1536]{1,0:T(8,128)(2,1)}, bf16[256,1536]{1,0:T(8,128)(2,1)S(1)}, u32[]{:S(2)}) copy-start(bf16[256,1536]{1,0:T(8,128)(2,1)S(1)} %all_gather.30) | copy-start | bytes 2359300
  229.1 8.5 copy-start.17
  230.7 6.8 copy-start.39
  240.1 91.1 %all-gather.12.cloned.1.call-start = ((), (), s32[]{:S(2)}) async-start(), calls=%async_computation.4 | async-start | bytes 2506752 | tf_op jit(solution)/shard_map/all_gather | solution.py:751
  240.8 773.1 %all-gather.16.cloned.1.call-start = ((), (), s32[]{:S(2)}) async-start(), calls=%async_computation.6 | async-start | bytes 9830400 | tf_op jit(solution)/shard_map/all_gather | solution.py:905
  241.8 50.4 %copy-start.10 = (pred[256,1024]{0,1:T(8,128)(4,1)}, pred[256,1024]{0,1:T(8,128)(4,1)S(1)}, u32[]{:S(2)}) copy-start(pred[256,1024]{0,1:T(8,128)(4,1)S(1)} %fusion.21) | copy-start | bytes 786436
  244.0 45.6 %copy-start.21 = (bf16[256,12,64]{0,2,1:T(8,128)(2,1)}, bf16[256,12,64]{0,2,1:T(8,128)(2,1)S(1)}, u32[]{:S(2)}) copy-start(bf16[256,12,64]{0,2,1:T(8,128)(2,1)S(1)} %pad_maximum_fusion.9) | copy-start | bytes 1179652
  287.4 10.2 copy-start.15
  287.6 2.0 copy-start.19
  289.6 4.5 copy-start.5
  289.6 4.5 copy-start.41
  294.1 3.5 copy-start.45
  297.6 2.6 copy-start.6
  297.6 38.3 %copy-start.50 = (s32[1024,8]{0,1:T(8,128)S(1)}, s32[1024,8]{0,1:T(8,128)}, u32[]{:S(2)}) copy-start(s32[1024,8]{0,1:T(8,128)} %param.17) | copy-start | bytes 98308
  301.4 111.7 %copy-start.23 = (bf16[4,64,3,256]{3,1,2,0:T(8,128)(2,1)}, bf16[4,64,3,256]{3,1,2,0:T(8,128)(2,1)S(1)}, u32[]{:S(2)}) copy-start(bf16[4,64,3,256]{3,1,2,0:T(8,128)(2,1)S(1)} %convolution_convert_fusion.8) | copy-start | bytes 1179652
  334.4 11.5 %collective-permute-start = (bf16[128,1536]{1,0:T(8,128)(2,1)}, bf16[128,1536]{1,0:T(8,128)(2,1)S(1)}, u32[]{:S(2)}, u32[]{:S(2)}) collective-permute-start(bf16[128,1536]{1,0:T(8,128)(2,1)} %dynamic-slice_convert_fusion.1), channel_id=1, source_target_pairs={{0,1},{1,0},{2,3},{3,2},{4,5},{5,4},{6,7},{7,6},{8,9},{9,8},{10,11... | collective-permute-start | bytes 1179656 | tf_op jit(solution)/shard_map/ppermute | solution.py:706
  346.7 2.3 copy-start.60
  346.7 66.4 %copy-start.55 = (f32[128]{0:T(128)}, f32[128]{0:T(128)S(1)}, u32[]{:S(2)}) copy-start(f32[128]{0:T(128)S(1)} %add_rsqrt_fusion.2) | copy-start | bytes 1540
  349.0 64.1 %copy-start.37 = (f32[128,40]{0,1:T(8,128)}, f32[128,40]{0,1:T(8,128)S(1)}, u32[]{:S(2)}) copy-start(f32[128,40]{0,1:T(8,128)S(1)} %get-tuple-element.96) | copy-start | bytes 61444
  514.7 3.9 copy-start.33
  514.7 16.8 %slice-start = ((s8[12582912]{0:T(1024)(128)(4,1)}), s8[4194304]{0:T(1024)(128)(4,1)S(1)}, s32[]{:S(2)}) async-start(s8[12582912]{0:T(1024)(128)(4,1)} %bitcast.167), calls=%async_computation.7 | async-start | bytes 8388608
  518.6 12.8 %slice-start.1 = ((s8[12582912]{0:T(1024)(128)(4,1)}), s8[4194304]{0:T(1024)(128)(4,1)S(1)}, s32[]{:S(2)}) async-start(s8[12582912]{0:T(1024)(128)(4,1)} %bitcast.167), calls=%async_computation.8 | async-start | bytes 8388608
  518.6 12.8 %slice-start.2 = ((s8[12582912]{0:T(1024)(128)(4,1)}), s8[4194304]{0:T(1024)(128)(4,1)S(1)}, s32[]{:S(2)}) async-start(s8[12582912]{0:T(1024)(128)(4,1)} %bitcast.167), calls=%async_computation.9 | async-start | bytes 8388608
  552.4 122.2 %copy-start.4 = (bf16[1536,640]{1,0:T(8,128)(2,1)S(1)}, bf16[1536,640]{1,0:T(8,128)(2,1)}, u32[]{:S(2)}) copy-start(bf16[1536,640]{1,0:T(8,128)(2,1)} %convolution_convert_fusion.4) | copy-start | bytes 5898244
  674.6 108.9 %copy-start.42 = (f32[4,3,256]{2,1,0:T(4,128)S(1)}, f32[4,3,256]{2,1,0:T(4,128)}, u32[]{:S(2)}) copy-start(f32[4,3,256]{2,1,0:T(4,128)} %copy-done.41) | copy-start | bytes 36868
  674.6 108.9 %copy-start.46 = (f32[4,3,256]{2,1,0:T(4,128)S(1)}, f32[4,3,256]{2,1,0:T(4,128)}, u32[]{:S(2)}) copy-start(f32[4,3,256]{2,1,0:T(4,128)} %copy-done.45) | copy-start | bytes 36868
  782.7 2.0 copy-start.38
  782.7 2.0 copy-start.52
  782.7 1.9 copy-start.54
  782.8 3.6 copy-start.9
  782.8 3.6 copy-start.44
  782.8 3.6 copy-start.56
  782.8 5.0 copy-start.61
  782.8 5.9 copy-start.25
  782.8 231.1 %all-gather.14.cloned.1.call-start = ((), (), s32[]{:S(2)}) async-start(), calls=%async_computation.5 | async-start | bytes 19660800 | tf_op jit(solution)/shard_map/all_gather | solution.py:904
  802.2 14.4 %copy-start.11 = (pred[256,1024]{0,1:T(8,128)(4,1)S(1)}, pred[256,1024]{0,1:T(8,128)(4,1)}, u32[]{:S(2)}) copy-start(pred[256,1024]{0,1:T(8,128)(4,1)} %copy-done.10) | copy-start | bytes 786436
  802.2 14.4 %copy-start.16 = (bf16[1024,256]{0,1:T(8,128)(2,1)S(1)}, bf16[1024,256]{0,1:T(8,128)(2,1)}, u32[]{:S(2)}) copy-start(bf16[1024,256]{0,1:T(8,128)(2,1)} %copy-done.15) | copy-start | bytes 1572868
  823.1 9.4 copy-start.22
  829.8 2.7 copy-start.7
  832.5 2.9 copy-start.32
  850.9 12.9 %copy-start.20 = (bf16[1024,256]{0,1:T(8,128)(2,1)S(1)}, bf16[1024,256]{0,1:T(8,128)(2,1)}, u32[]{:S(2)}) copy-start(bf16[1024,256]{0,1:T(8,128)(2,1)} %copy-done.19) | copy-start | bytes 1572868
  862.9 4.9 copy-start.40
  862.9 4.9 copy-start.49
  863.8 4.2 copy-start.34
  867.8 5.9 copy-start.28
  868.0 12.8 %copy-start.18 = (bf16[256,1536]{1,0:T(8,128)(2,1)S(1)}, bf16[256,1536]{1,0:T(8,128)(2,1)}, u32[]{:S(2)}) copy-start(bf16[256,1536]{1,0:T(8,128)(2,1)} %copy-done.17) | copy-start | bytes 2359300
  868.0 12.8 %copy-start.35 = (bf16[256,256]{0,1:T(8,128)(2,1)S(1)}, bf16[256,256]{0,1:T(8,128)(2,1)}, u32[]{:S(2)}) copy-start(bf16[256,256]{0,1:T(8,128)(2,1)} %copy.144) | copy-start | bytes 393220
  873.6 10.4 copy-start.24
  873.6 23.3 %collective-permute-start.1 = (bf16[128,1536]{1,0:T(8,128)(2,1)}, bf16[128,1536]{1,0:T(8,128)(2,1)}, u32[]{:S(2)}, u32[]{:S(2)}) collective-permute-start(bf16[128,1536]{1,0:T(8,128)(2,1)} %dynamic-slice_convert_fusion), channel_id=1, source_target_pairs={{0,1},{1,0},{2,3},{3,2},{4,5},{5,4},{6,7},{7,6},{8,9},{9,8},{10,11... | collective-permute-start | bytes 1179656 | tf_op jit(solution)/shard_map/ppermute | solution.py:706
  880.8 3.2 copy-start.29
  886.3 10.6 %copy-start.59 = (f32[128]{0:T(128)S(1)}, f32[128]{0:T(128)}, u32[]{:S(2)}) copy-start(f32[128]{0:T(128)} %get-tuple-element.87) | copy-start | bytes 1540
  886.3 10.6 %copy-start.13 = (bf16[256,1536]{1,0:T(8,128)(2,1)S(1)}, bf16[256,1536]{1,0:T(8,128)(2,1)}, u32[]{:S(2)}) copy-start(bf16[256,1536]{1,0:T(8,128)(2,1)} %copy-done.12) | copy-start | bytes 2359300
  886.3 10.6 %copy-start.48 = (f32[1536]{0:T(1024)S(1)}, f32[1536]{0:T(1024)}, u32[]{:S(2)}) copy-start(f32[1536]{0:T(1024)} %copy-done.47) | copy-start | bytes 18436
  886.3 12.2 %copy-start.26 = (bf16[128,1536]{1,0:T(8,128)(2,1)S(1)}, bf16[128,1536]{1,0:T(8,128)(2,1)}, u32[]{:S(2)}) copy-start(bf16[128,1536]{1,0:T(8,128)(2,1)} %constant_dynamic-slice_fusion.3) | copy-start | bytes 1179652
  902.1 96.4 %all-to-all-start = ((bf16[128,2,768]{2,0,1:T(8,128)(2,1)}), bf16[128,2,768]{2,0,1:T(8,128)(2,1)S(1)}, u32[]{:S(2)}, u32[]{:S(2)}) async-start(bf16[128,2,768]{2,0,1:T(8,128)(2,1)} %bitcast.148), calls=%async_computation | async-start | bytes 786432 | tf_op jit(solution)/shard_map/all_to_all | solution.py:922
  998.5 15.4 %all-to-all-start.1 = ((f32[128,2,768]{2,0,1:T(8,128)}), f32[128,2,768]{2,0,1:T(8,128)S(1)}, u32[]{:S(2)}, u32[]{:S(2)}) async-start(f32[128,2,768]{2,0,1:T(8,128)} %bitcast.147), calls=%async_computation.1 | async-start | bytes 1572864 | tf_op jit(solution)/shard_map/all_to_all | solution.py:992
  1013.9 27.2 %copy-start.1 = (bf16[384,768]{1,0:T(8,128)(2,1)S(1)}, bf16[384,768]{1,0:T(8,128)(2,1)}, u32[]{:S(2)}) copy-start(bf16[384,768]{1,0:T(8,128)(2,1)} %param.22) | copy-start | bytes 1769476
  (10 other events, 12.3 us)
Sparse Core Ops, SparseCore 0:
  10.9 147.3 all-gather.7
  240.2 45.6 all-gather.9
  288.8 42.2 all-gather.11
  783.0 59.4 all-gather.15
  843.8 114.2 all-gather.13

commit v4 on v3

--- a/solution.py
+++ b/solution.py
@@ -47,37 +47,34 @@
     ]
 
 
-def gather_kernel(own_count, *refs):
-    if own_count:
-        own_ref, in_ref, low_ref, out_ref, upper_ref, lower_ref = refs[:6]
-        move_local_sem, move_send_sem, move_recv_sem, local_sem, send_sem, recv_sem = refs[6:]
-    else:
-        own_ref, out_ref, local_sem, send_sem, recv_sem = refs
+def gather_kernel(own_count, units, pairs, *refs):
+    own_ref, weight_ref, pair_refs = (refs[0], refs[1], refs[2 : 2 + pairs])
+    out_ref, moved_ref, paired_refs = (refs[2 + pairs], refs[3 + pairs], refs[4 + pairs : 4 + 2 * pairs])
+    local_sem, send_sem, recv_sem, move_local_sem, move_send_sem, move_recv_sem, pair_sem, held = refs[
+        4 + 2 * pairs :
+    ]
     nd, width = (out_ref.shape[0], own_ref.shape[2])
     wide = out_ref.shape[-1] != width
     z, y, k, x = place()
     up, down = (device((z + 1) % nd, y, k, x), device((z + nd - 1) % nd, y, k, x))
     greet(partners_of(nd, z, y, k, x))
     moves, kept = ([], [])
+    rows, parts = (weight_ref.shape[1], weight_ref.shape[2] // (nd * units))
 
     def move(hop):
-        rows, units = (in_ref.shape[1], low_ref.shape[2] // nd)
         to_z, from_z = ((z + hop) % nd, (z + nd - hop) % nd)
-        for part in range(3):
+        for part in range(parts):
             for e in range(own_count):
-                source_ref, base = (in_ref, part * nd * units) if part < 2 else (low_ref, 0)
-                to_ref = upper_ref if part < 2 else lower_ref
-                columns = pl.ds((part % 2 * own_count + e) * units, units)
-                source = source_ref.at[
-                    (y * 2 + k) * own_count + e,
-                    :,
-                    pl.ds(pl.multiple_of(base + to_z * units, LANES), units),
-                ]
-                target = to_ref.at[pl.ds(pl.multiple_of(z * rows, 16), rows), columns]
+                columns = pl.ds((part * own_count + e) * units, units)
+                start = pl.multiple_of((part * nd + to_z) * units, LANES)
+                source = weight_ref.at[(y * 2 + k) * own_count + e, :, pl.ds(start, units)]
+                target = moved_ref.at[pl.ds(pl.multiple_of(z * rows, 16), rows), columns]
                 if hop == 0:
-                    copy = pltpu.make_async_copy(source, target, move_local_sem.at[len(kept)])
+                    at = len(kept)
+                    copy = pltpu.make_async_copy(source, held.at[at], move_local_sem.at[0, at])
                     copy.start()
-                    kept.append(copy)
+                    put = pltpu.make_async_copy(held.at[at], target, move_local_sem.at[1, at])
+                    kept.append((copy, put))
                     continue
                 slot = len(moves)
                 copy = pltpu.make_async_remote_copy(
@@ -89,9 +86,26 @@
                     device_id_type=MESH,
                 )
                 copy.start()
-                arrival = to_ref.at[pl.ds(pl.multiple_of(from_z * rows, 16), rows), columns]
+                arrival = moved_ref.at[pl.ds(pl.multiple_of(from_z * rows, 16), rows), columns]
                 moves.append((copy, arrival, slot))
 
+    swaps = []
+    for at_pair, (ref, full_ref) in enumerate(zip(pair_refs, paired_refs)):
+        span = ref.shape[-1]
+        mine = full_ref.at[:, pl.ds(pl.multiple_of(x * span, LANES), span)]
+        copy = pltpu.make_async_remote_copy(
+            src_ref=ref,
+            dst_ref=mine,
+            send_sem=pair_sem.at[0, at_pair],
+            recv_sem=pair_sem.at[1, at_pair],
+            device_id=device(z, y, k, 1 - x),
+            device_id_type=MESH,
+        )
+        copy.start()
+        swaps.append(copy)
+        copy = pltpu.make_async_copy(ref, mine, pair_sem.at[2, at_pair])
+        copy.start()
+        swaps.append(copy)
     low = jnp.minimum(z, nd - 1 - z)
     places = []
     for step in range(nd):
@@ -172,8 +186,15 @@
                 piece = (step, 0, 0, 0, half)
                 send(piece, links[half][1])
                 send(piece, "k")
-            if own_count:
-                move((step + 1) % nd)
+            if step == 0:
+                move(0)
+            if step == 1:
+                for copy, put in kept:
+                    copy.wait()
+                    put.start()
+            if step == nd - 2:
+                for hop in [2, 1, 3] if nd == 4 else range(1, nd):
+                    move(hop)
         if 1 <= step < nd + 1:
             for half in range(2):
                 piece = (step - 1, half, 0, 1 - half, half)
@@ -191,8 +212,10 @@
             for dx in range(2):
                 for half in range(2):
                     arrived((step, dy, 1, dx, half))
-    for own_copy in own_copies + kept:
+    for own_copy in own_copies + [put for _, put in kept]:
         own_copy.wait()
+    for copy in swaps:
+        copy.wait()
     for copy, arrival, slot in moves:
         pltpu.make_async_remote_copy(
             src_ref=arrival,
@@ -210,47 +233,89 @@
             pl.when(condition)(copy.wait_send)
 
 
-def gather_rows(own, nd, collective_id, wide=False, weights=None, own_count=0):
+def gather_rows(own, weight, units, own_count, nd, collective_id, pairs=(), wide=False):
     rows, width = own.shape
     half = rows // 2
     shape = (nd, 2, 2, 2, half, 2 * width) if wide else (nd, 2, 2, 2, 2, half, width)
-    shapes = [jax.ShapeDtypeStruct(shape, own.dtype)]
-    operands = [own.reshape(2, half, width)]
-    semaphores = [
-        pltpu.SemaphoreType.DMA((2,)),
-        pltpu.SemaphoreType.DMA((nd * 18,)),
-        pltpu.SemaphoreType.DMA((nd * 16,)),
-    ]
-    if weights:
-        depth, count = (nd * weights[0].shape[1], 3 * own_count)
-        operands += list(weights)
-        units = weights[1].shape[2] // nd
-        for parts in (2, 1):
-            shapes.append(jax.ShapeDtypeStruct((depth, parts * own_count * units), own.dtype))
-        semaphores = [
-            pltpu.SemaphoreType.DMA((count,)),
+    depth, moved = (nd * weight.shape[1], own_count * weight.shape[2] // nd)
+    count = moved // units
+    vmem, anywhere = (pl.BlockSpec(memory_space=pltpu.VMEM), pl.BlockSpec(memory_space=pl.ANY))
+    out = pl.pallas_call(
+        functools.partial(gather_kernel, own_count, units, len(pairs)),
+        in_specs=[vmem, anywhere] + [vmem] * len(pairs),
+        out_specs=[anywhere] * (2 + len(pairs)),
+        out_shape=[
+            jax.ShapeDtypeStruct(shape, own.dtype),
+            jax.ShapeDtypeStruct((depth, moved), weight.dtype),
+        ]
+        + [jax.ShapeDtypeStruct((p.shape[0], 2 * p.shape[1]), p.dtype) for p in pairs],
+        scratch_shapes=[
+            pltpu.SemaphoreType.DMA((2,)),
+            pltpu.SemaphoreType.DMA((nd * 18,)),
+            pltpu.SemaphoreType.DMA((nd * 16,)),
+            pltpu.SemaphoreType.DMA((2, count)),
             pltpu.SemaphoreType.DMA(((nd - 1) * count,)),
             pltpu.SemaphoreType.DMA(((nd - 1) * count,)),
-        ] + semaphores
-    out = pl.pallas_call(
-        functools.partial(gather_kernel, own_count),
-        in_specs=[pl.BlockSpec(memory_space=pltpu.VMEM)]
-        + [pl.BlockSpec(memory_space=pl.ANY)] * (len(operands) - 1),
-        out_specs=[pl.BlockSpec(memory_space=pl.ANY)] * len(shapes),
-        out_shape=shapes,
-        scratch_shapes=semaphores,
+            pltpu.SemaphoreType.DMA((3, max(len(pairs), 1))),
+            pltpu.VMEM((count, weight.shape[1], units), weight.dtype),
+        ],
         compiler_params=pltpu.CompilerParams(collective_id=collective_id, has_side_effects=True),
         cost_estimate=COST,
         name="gather_rows",
-    )(*operands)
-    gathered = out[0].reshape(-1, shape[-1])
-    return (gathered, out[1], out[2]) if weights else gathered
-
-
-def reduce_kernel(count, *refs):
+    )(own.reshape(2, half, width), weight, *pairs)
+    return (out[0].reshape(-1, shape[-1]), *out[1:])
+
+
+def ctx_kernel(own_ref, out_ref, local_sem, send_sem, recv_sem):
+    z, y, k, x = place()
+    y_partner, core = (device(z, 1 - y, k, x), device(z, y, 1 - k, x))
+    greet([y_partner, core])
+    kept = pltpu.make_async_copy(own_ref, out_ref.at[y, k], local_sem)
+    kept.start()
+    copies = []
+    for at, (source, chip, target) in enumerate(
+        ((own_ref, y, y_partner), (own_ref, y, core), (out_ref.at[1 - y, k], 1 - y, core))
+    ):
+        if at == 2:
+            copies[0].wait_recv()
+        copy = pltpu.make_async_remote_copy(
+            src_ref=source,
+            dst_ref=out_ref.at[chip, k],
+            send_sem=send_sem.at[at],
+            recv_sem=recv_sem.at[at],
+            device_id=target,
+            device_id_type=MESH,
+        )
+        copy.start()
+        copies.append(copy)
+    kept.wait()
+    for copy in copies[1:]:
+        copy.wait_recv()
+    for copy in copies:
+        copy.wait_send()
+
+
+def gather_ctx(own, collective_id):
+    out = pl.pallas_call(
+        ctx_kernel,
+        in_specs=[pl.BlockSpec(memory_space=pltpu.VMEM)],
+        out_specs=pl.BlockSpec(memory_space=pl.ANY),
+        out_shape=jax.ShapeDtypeStruct((2, 2, *own.shape), own.dtype),
+        scratch_shapes=[
+            pltpu.SemaphoreType.DMA,
+            pltpu.SemaphoreType.DMA((3,)),
+            pltpu.SemaphoreType.DMA((3,)),
+        ],
+        compiler_params=pltpu.CompilerParams(collective_id=collective_id, has_side_effects=True),
+        name="gather_ctx",
+    )(own)
+    return out.reshape(-1, own.shape[1])
+
+
+def reduce_kernel(count, when, *refs):
     parts, moved_ref, out_ref, arrived_ref = (refs[:count], *refs[count : count + 3])
-    own, from_core, first, second, across, load_sem, send_sem, recv_sem = refs[count + 3 : -3]
-    move_local_sem, move_send_sem, move_recv_sem = refs[-3:]
+    own, from_core, first, second, across, load_sem, send_sem, recv_sem = refs[count + 3 : -4]
+    move_local_sem, move_send_sem, move_recv_sem, held = refs[-4:]
     nd = parts[0].shape[0]
     z, y, k, x = place()
     greet(partners_of(nd, z, y, k, x))
@@ -318,8 +383,9 @@
                     load.start()
                     loads.append(load)
     x_partner, y_partner = (device(z, y, k, 1 - x), device(z, 1 - y, k, x))
-    kept = pltpu.make_async_copy(moved_ref.at[z], arrived_ref.at[z], move_local_sem)
-    kept.start()
+    taken = pltpu.make_async_copy(moved_ref.at[z], held, move_local_sem.at[0])
+    taken.start()
+    kept = pltpu.make_async_copy(held, arrived_ref.at[z], move_local_sem.at[1])
     moves = []
 
     def move(hop):
@@ -336,8 +402,11 @@
         moves.append((copy, hop))
 
     for step in range(nd + 2):
-        if step == 0 or 3 <= step < nd + 1:
-            move(step - 1 if step else 1)
+        if step == 0 and step in when:
+            move(when[step])
+        if step == 1:
+            taken.wait()
+            kept.start()
         if step < nd:
             for at in range(4):
                 base = spot(step, 0, 0, 0) + at * 2
@@ -385,6 +454,8 @@
                     device((z + hop) % nd, y, k, x),
                     across_slot + slot,
                 )
+        if step and step in when:
+            move(when[step])
     for slot in range(nd - 1):
         arrived(across.at[slot], across_slot + slot)
     mine = spot(order.index(0), 0, 0, 0)
@@ -415,14 +486,14 @@
         copy.wait_send()
 
 
-def reduce_rows(parts, moved, nd, collective_id):
+def reduce_rows(parts, moved, when, nd, collective_id):
     moved = moved.reshape(nd, moved.shape[0] // nd, moved.shape[1])
     rows = parts[0].shape[0] // (nd * 8)
     width = sum(part.shape[1] for part in parts)
     half, count = (rows // 2, len(parts))
     sends = nd * (4 * count + 7)
     out = pl.pallas_call(
-        functools.partial(reduce_kernel, count),
+        functools.partial(reduce_kernel, count, when),
         in_specs=[pl.BlockSpec(memory_space=pl.ANY)] * (count + 1),
         out_specs=[pl.BlockSpec(memory_space=pltpu.VMEM), pl.BlockSpec(memory_space=pl.ANY)],
         out_shape=[
@@ -438,9 +509,10 @@
             pltpu.SemaphoreType.DMA((nd * 4 * count,)),
             pltpu.SemaphoreType.DMA((sends,)),
             pltpu.SemaphoreType.DMA((sends,)),
-            pltpu.SemaphoreType.DMA,
+            pltpu.SemaphoreType.DMA((2,)),
             pltpu.SemaphoreType.DMA((nd - 1,)),
             pltpu.SemaphoreType.DMA((nd - 1,)),
+            pltpu.VMEM(moved.shape[1:], moved.dtype),
         ],
         compiler_params=pltpu.CompilerParams(
             collective_id=collective_id, has_side_effects=True, vmem_limit_bytes=48 << 20
@@ -740,9 +812,6 @@
     local_count = w_expert_in.shape[1]
     capacity = n_rows * 3 // 8
 
-    gains = lax.all_gather(jnp.stack([gain_one, gain_two]), "tensor", axis=1, tiled=True)
-    gain_one_full, gain_two_full = (gains[0], gains[1])
-    tokens_full = lax.all_gather(tokens, "tensor", axis=1, tiled=True)
     packed = jnp.concatenate([w_query, w_key, w_value, w_router], axis=1)
     share = d_local // nc
     packed = lax.dynamic_slice_in_dim(packed, ctx_at * share, share, 0)
@@ -759,17 +828,21 @@
     own_count = local_count // nc if by_expert else local_count
     units = FF // nd if by_expert else FF // (nd * nc)
     width = own_count * units
+    gains = jnp.stack([gain_one, gain_two])
     if kernels:
-        natural = [jnp.transpose(w, (1, 0, 2)) for w in (w_expert_in, w_expert_out)]
-        cot_all, upper_w, lower_w = gather_rows(
-            cotangent, nd, 1, wide=True, weights=natural, own_count=own_count
+        w_expert_in, w_expert_out = [jnp.transpose(w, (1, 0, 2)) for w in (w_expert_in, w_expert_out)]
+        cot_all, lower_w, tokens_full, gains = gather_rows(
+            cotangent, w_expert_out, units, own_count, nd, 1, (tokens, gains), wide=True
         )
         cot_sub = lax.dynamic_slice_in_dim(
             cot_all, (dp_at * nc + ctx_at) * n_rows + tensor_at * sub, sub, 0
         )
     else:
+        tokens_full = lax.all_gather(tokens, "tensor", axis=1, tiled=True)
+        gains = lax.all_gather(gains, "tensor", axis=1, tiled=True)
         cot_sub = lax.all_to_all(cotangent, "tensor", 0, 1, tiled=True)
         cot_all = lax.all_gather(cot_sub, ALL, axis=0, tiled=True)
+    gain_one_full, gain_two_full = (gains[0], gains[1])
     tokens_sub = lax.dynamic_slice_in_dim(tokens_full, tensor_at * sub, sub, 0).astype(F32)
 
     first_expert = tensor_at * local_count + (ctx_at * own_count if by_expert else 0)
@@ -826,7 +899,10 @@
         ],
         axis=1,
     )
-    kv_all = lax.all_gather(kv_rows, "ctx", axis=0, tiled=True)
+    if kernels:
+        kv_all = gather_ctx(kv_rows, 7)
+    else:
+        kv_all = lax.all_gather(kv_rows, "ctx", axis=0, tiled=True)
     key_heads = kv_all[:, :kv_width].reshape(pack_len, kv_heads, HEAD_DIM)
     value_heads = kv_all[:, kv_width:].reshape(pack_len, kv_heads, HEAD_DIM)
     allowed = (local_segs[:, None] == segment_row[None, :]) & (
@@ -859,7 +935,7 @@
     extra = jnp.zeros((sub, LANES - 2 * EXPERTS), BF)
     h_ext = jnp.concatenate([h_two, gates_high, gates_low, extra], axis=1)
     if kernels:
-        h_all = gather_rows(h_ext, nd, 2)
+        h_all, upper_w = gather_rows(h_ext, w_expert_in, units, own_count, nd, 2)
     else:
         h_all = lax.all_gather(h_ext, ALL, axis=0, tiled=True)
     gates_all = (
@@ -867,6 +943,7 @@
     )
     total_rows = h_all.shape[0]
     gates_own = lax.dynamic_slice_in_dim(gates_all, first_expert, own_count, 1)
+    h_two_full = lax.dynamic_slice(h_all, ((dp_at * nc + ctx_at) * n_rows, 0), (n_rows, D))
     h_all = h_all[:, :D]
 
     gate_wide = jnp.broadcast_to(gates_own[:, :, None], (total_rows, own_count, units)).reshape(
@@ -897,9 +974,9 @@
     grad_lower = dot(cot_all, active_gated, ((0,), (0,))).astype(BF)
     if kernels:
         grad_in, grad_upper, grad_lower = lax.optimization_barrier((grad_in, grad_upper, grad_lower))
-        back_sub, grad_upper = reduce_rows([grad_in, grad_gates], grad_upper, nd, 3)
+        back_sub, grad_upper = reduce_rows([grad_in, grad_gates], grad_upper, {0: 1, 4: 2, 5: 3}, nd, 3)
         mixed, back_sub = lax.optimization_barrier((mixed, back_sub))
-        mixed_sub, grad_lower = reduce_rows([mixed], grad_lower, nd, 4)
+        mixed_sub, grad_lower = reduce_rows([mixed], grad_lower, {0: 2, 1: 1, 2: 3}, nd, 4)
         back_sub, mixed_sub = lax.optimization_barrier((back_sub, mixed_sub))
         grad_upper = lax.all_gather(grad_upper, "ctx", axis=0)
         grad_lower = lax.all_gather(grad_lower, "ctx", axis=0)
@@ -937,7 +1014,6 @@
     )
     logit_grads_full = grad_attn[:, D : D + EXPERTS]
     grad_attn = grad_attn[:, :D]
-    h_two_full = lax.dynamic_slice_in_dim(h_all, (dp_at * nc + ctx_at) * n_rows, n_rows, 0)
     grad_router = dot(h_two_full, logit_grads_full, ((0,), (0,)))
 
     grad_output_w = dot(grad_attn, attended, ((0,), (0,)))

time: 1060 us -> 935 us (0.88)
  waiting for transfers between devices: 86.2 us -> 14.8 us
  Pallas kernels: 622 us -> 591 us
  local copies, waits for them, and re-layouts: 83.8 us -> 66.4 us
  blocking collectives: 26.1 us -> 12.5 us
    all_gather x1 -> x0, waiting for transfers between devices: 41.9 us -> none  [on_device(): kv_all = lax.all_gather(kv_rows, 'ctx', axis=0, tiled=True)]
    pallas_call x4 -> x5, Pallas kernels: 492 us -> 452 us  [the longest x2 231 us: gather_rows(): pl.pallas_call(functools.partial(gather_kernel, own_count, units, len(pai...]
    all_gather x1, waiting for transfers between devices: 29.7 us -> 0.02 us  [on_device(): lax.all_gather(lax.dynamic_slice_in_dim(w_output, ctx_at * share, share,...]
    all_gather x2 -> x0, blocking collectives: 13.9 us -> none  [the longest x1 9.51 us: on_device(): tokens_full = lax.all_gather(tokens, 'tensor', axis=1, tiled=True)]
    slice x1 -> x0, local copies, waits for them, and re-layouts: 12 us -> none  [on_device(): h_all = h_all[:, :D]]
  transfers between devices with their start and end apart: 9 -> 8, of which waited for: 4 -> 2; matrix products, arithmetic and copies ran while one was open for 11% -> 12% of each run, Pallas kernels for 29% -> 26%
where the time goes in v4:
time: 935 us; the launch traced here: 925 us
  Pallas kernels  591 us (63%)
  matrix products  176 us (19%)
  local copies, waits for them, and re-layouts  66.4 us (7%)
  other arithmetic  37.7 us (4%)
  between operations  15 us (2%)
  waiting for transfers between devices  14.8 us (2%)
  blocking collectives  12.5 us (1%)
  starting transfers between devices  10.5 us (1%)
    pallas_call x2, Pallas kernels, gather_rows(): pl.pallas_call(functools.partial(gather_kernel, own_count, units, len(pai...  231 us
    pallas_call x2, Pallas kernels, reduce_rows(): pl.pallas_call(functools.partial(reduce_kernel, count, when), in_specs=[p...  210 us
    dot_general x16, matrix products, dot(): return lax.dot_general(a, b, (dims, ((), ())), preferred_element_type=F32)  154 us
    pallas_call x2, Pallas kernels, sum_blocks(): pl.pallas_call(functools.partial(sum_kernel, nd > 1), in_specs=[pl.BlockS...  114 us
    pallas_call x1, Pallas kernels, spread(): pl.pallas_call(spread_kernel, grid=(d_local // block,), in_specs=[pl.Bloc...  25.6 us
  transfers between devices with their start and end apart: 8, of which 2 were waited for; matrix products, arithmetic and copies ran while one was open for 12% of the time, Pallas kernels for 26%

profile of v4, /device:TPU:0, one launch (start us, length us, event | category | flops | bytes accessed | tf_op | source)
XLA Modules:
  0.0 924.8 jit_solution(15913657468312289375)
XLA Ops:
  8.2 1.6 fusion.43
  13.7 1.2 select_reduce_fusion
  17.4 114.5 %gather_rows.2 = (bf16[4,2,2,2,128,1536]{5,4,3,2,1,0:T(8,128)(2,1)}, bf16[1536,640]{1,0:T(8,128)(2,1)}, bf16[256,1536]{1,0:T(8,128)(2,1)}, f32[2,1536]{1,0:T(2,128)}) custom-call(bf16[2,128,768]{2,1,0:T(8,128)(2,1)} %bitcast.199, bf16[20,384,512]{2,1,0:T(8,128)(2,1)} %bitcast.168, bf16[256,768]{1,0:T(8,128)(2,1)} %refs_2_.1, f32[2,768]{1,0:T(2,128)} %pad_maximum_fusion.13.refs_3_), custom_call_target="tpu_custom_call" | custom-call | bytes 250000000 | tf_op jit(solution)/shard_map/gather_rows/pallas_call | solution.py:243
  131.9 1.4 fusion.18
  134.1 1.8 constant_dynamic-slice_fusion.4
  135.9 1.4 fusion.20
  138.2 3.3 fusion.16
  143.0 1.6 pad_maximum_fusion.10.own_ref
  144.6 11.4 %gather_ctx.1 = bf16[2,2,256,512]{3,2,1,0:T(8,128)(2,1)} custom-call(bf16[256,512]{1,0:T(8,128)(2,1)} %pad_maximum_fusion.10.own_ref), custom_call_target="tpu_custom_call" | custom-call | tf_op jit(solution)/shard_map/gather_ctx/pallas_call | solution.py:299
  156.0 1.3 fusion.68
  157.8 2.0 fusion.13
  159.8 2.6 fusion.3
  162.4 1.9 copy-done.5
  164.3 3.4 divide_convert_fusion
  167.8 2.6 copy-done.6
  171.6 2.6 fusion.70
  175.0 1.4 collective-permute-start
  176.6 10.0 %collective-permute-done = bf16[128,1536]{1,0:T(8,128)(2,1)S(1)} collective-permute-done((bf16[128,1536]{1,0:T(8,128)(2,1)}, bf16[128,1536]{1,0:T(8,128)(2,1)S(1)}, u32[]{:S(2)}, u32[]{:S(2)}) %collective-permute-start) | collective-permute-done | bytes 393248 | tf_op jit(solution)/shard_map/ppermute | solution.py:778
  188.4 1.3 fusion.69
  191.7 116.4 %gather_rows.3 = (bf16[4,2,2,2,2,64,1664]{6,5,4,3,2,1,0:T(8,128)(2,1)}, bf16[1536,1280]{1,0:T(8,128)(2,1)}) custom-call(bf16[2,64,1664]{2,1,0:T(8,128)(2,1)} %bitcast.189, bf16[20,384,1024]{2,1,0:T(8,128)(2,1)} %bitcast.161), custom_call_target="tpu_custom_call" | custom-call | bytes 250000000 | tf_op jit(solution)/shard_map/gather_rows/pallas_call | solution.py:243
  308.2 2.0 fusion.65
  311.4 22.7 %fusion.6 = f32[4096,1280]{0,1:T(8,128)} fusion(bf16[1536,1280]{1,0:T(8,128)(2,1)} %get-tuple-element.41, bf16[4096,1664]{1,0:T(8,128)(2,1)} %bitcast.195), kind=kOutput, calls=%fused_computation.17 | convolution fusion | flops 16106127360 | bytes 37486592 | tf_op jit(solution)/shard_map/dot_general | solution.py:745
  334.2 32.8 %multiply_convert_fusion.1 = (bf16[4096,640]{0,1:T(8,128)(2,1)}, bf16[4096,640]{0,1:T(8,128)(2,1)}, f32[4096,640]{0,1:T(8,128)}, bf16[4096,640]{0,1:T(8,128)(2,1)}) fusion(f32[4096,1280]{0,1:T(8,128)} %fusion.6, f32[4096,5]{0,1:T(8,128)S(1)} %copy.131, bf16[4096,1536]{1,0:T(8,128)(2,1)} %bitcast.164, bf16[1536,640]{1,0:T(8,128)(2,1)S(1)} %copy-done.31), kind=kOutput, calls=%fused_computation.22 | convolution fusion | flops 8100249600 | bytes 61816832 | tf_op jit(solution)/shard_map/dot_general | solution.py:745
  367.0 23.3 %fusion.10 = bf16[1536,1280]{1,0:T(8,128)(2,1)} fusion(bf16[4096,1664]{1,0:T(8,128)(2,1)} %bitcast.196, bf16[4096,640]{0,1:T(8,128)(2,1)} %get-tuple-element.76, bf16[4096,640]{0,1:T(8,128)(2,1)} %get-tuple-element.75), kind=kOutput, calls=%fused_computation.26 | convolution fusion | flops 16129064960 | bytes 27000832 | tf_op jit(solution)/shard_map/dot_general | solution.py:745
  390.4 23.9 %convolution_convert_fusion.1 = bf16[4096,1536]{1,0:T(8,128)(2,1)} fusion(bf16[1536,1280]{1,0:T(8,128)(2,1)} %get-tuple-element.41, bf16[4096,640]{0,1:T(8,128)(2,1)} %get-tuple-element.76, bf16[4096,640]{0,1:T(8,128)(2,1)} %get-tuple-element.75), kind=kOutput, calls=%fused_computation.3 | convolution fusion | flops 16133390336 | bytes 27000832 | tf_op jit(solution)/shard_map/dot_general | solution.py:745
  414.3 1.3 fusion.8
  415.6 14.1 %convolution_convert_fusion.3 = bf16[1536,640]{1,0:T(8,128)(2,1)} fusion(bf16[4096,1536]{1,0:T(8,128)(2,1)} %bitcast.165, bf16[4096,640]{0,1:T(8,128)(2,1)S(1)} %fusion.8), kind=kOutput, calls=%fused_computation.35 | convolution fusion | flops 8054046720 | bytes 19791872 | tf_op jit(solution)/shard_map/dot_general | solution.py:745
  429.7 13.3 %convolution_convert_fusion = bf16[4096,1536]{1,0:T(8,128)(2,1)} fusion(bf16[4096,640]{0,1:T(8,128)(2,1)S(1)} %fusion.8, bf16[1536,640]{1,0:T(8,128)(2,1)S(1)} %copy-done.31), kind=kOutput, calls=%fused_computation.2 | convolution fusion | flops 8059355136 | bytes 19791872 | tf_op jit(solution)/shard_map/dot_general | solution.py:745
  443.0 4.7 reduce_sum.132
  448.3 3.9 dynamic_update_slice.3
  452.2 118.3 %reduce_rows.2 = (f32[2,64,1664]{2,1,0:T(8,128)S(1)}, bf16[4,384,1280]{2,1,0:T(8,128)(2,1)S(1)}) custom-call(bf16[4,2,2,2,2,64,1536]{6,5,4,3,2,1,0:T(8,128)(2,1)} %bitcast.167, bf16[4,2,2,2,2,64,128]{6,5,4,3,2,1,0:T(8,128)(2,1)S(1)} %bitcast.150, bf16[4,384,1280]{2,1,0:T(8,128)(2,1)} %bitcast.178), custom_call_target="tpu_custom_call" | custom-call | bytes 250000000 | tf_op jit(solution)/shard_map/reduce_rows/pallas_call | solution.py:495
  570.5 1.9 copy-done.2
  572.4 91.7 %reduce_rows.3 = (f32[2,64,1536]{2,1,0:T(8,128)S(1)}, bf16[4,384,640]{2,1,0:T(8,128)(2,1)}) custom-call(bf16[4,2,2,2,2,64,1536]{6,5,4,3,2,1,0:T(8,128)(2,1)} %bitcast.166, bf16[4,384,640]{2,1,0:T(8,128)(2,1)S(1)} %bitcast.154), custom_call_target="tpu_custom_call" | custom-call | bytes 250000000 | tf_op jit(solution)/shard_map/reduce_rows/pallas_call | solution.py:495
  665.2 1.4 multiply_reduce_fusion
  667.9 12.5 %all_gather.23 = bf16[256,1664]{1,0:T(8,128)(2,1)S(1)} all-gather(bf16[128,1664]{1,0:T(8,128)(2,1)S(1)} %concatenate.59), channel_id=1, replica_groups=mesh['dp'=4,'ctx'=4,'tensor'=2] {'tensor'}, dimensions={0}, use_global_device_ids=true | all-gather | bytes 1277952 | tf_op jit(solution)/shard_map/all_gather | solution.py:1009
  681.3 3.7 convolution_convert_fusion.6
  685.0 1.2 copy.134
  686.2 5.6 fusion.25
  691.8 2.2 concatenate.61
  694.0 2.1 copy.139
  696.1 6.6 fusion
  702.7 6.7 fusion.2
  709.5 2.7 copy-done.7
  712.2 2.0 fusion.26
  716.2 15.3 %sum_blocks.2 = (f32[256,512]{1,0:T(8,128)S(1)}, f32[8,128]{1,0:T(8,128)}) custom-call(bf16[1,2,2,256,512]{4,3,2,1,0:T(8,128)(2,1)S(1)} %pad_maximum_fusion.3.part_ref, f32[8,128]{1,0:T(8,128)S(1)} %broadcast_in_dim.49.gain_ref), custom_call_target="tpu_custom_call" | custom-call | bytes 250000000 | tf_op jit(solution)/shard_map/sum_blocks/pallas_call | solution.py:661
  731.6 2.1 slice_bitcast_fusion
  733.7 2.4 copy.143
  736.1 1.5 convolution_convert_fusion.4
  738.8 4.9 convolution_multiply_fusion
  744.0 3.8 fusion.14
  748.6 1.9 collective-permute-start.1
  750.4 3.2 convolution_convert_fusion.2
  753.6 2.2 convolution_convert_fusion.5
  755.9 10.6 %concatenate.68.part_ref = bf16[4,2,2,96,2176]{4,3,2,1,0:T(8,128)(2,1)} concatenate(bf16[4,2,2,96,1280]{4,3,2,1,0:T(8,128)(2,1)} %bitcast.160, bf16[4,2,2,96,768]{4,3,2,1,0:T(8,128)(2,1)} %convolution_convert_fusion.5, bf16[4,2,2,96,40]{4,3,2,1,0:T(8,128)(2,1)} %bitcast.192, bf16[4,2,2,96,88]{4,3,2,1,0:T(8,128)(2,1)S(1)} %broadcast_in_dim.50), dimensions={4} | concatenate | bytes 13369344 | tf_op jit(solution)/shard_map/concatenate | solution.py:1073
  766.5 1.5 fusion.34
  768.1 2.0 fusion.32
  771.8 3.5 all-to-all-start
  775.3 98.4 %sum_blocks.3 = (f32[2,2,96,2176]{3,2,1,0:T(8,128)S(1)}, f32[2,1536]{1,0:T(2,128)S(1)}) custom-call(bf16[4,2,2,96,2176]{4,3,2,1,0:T(8,128)(2,1)} %concatenate.68.part_ref, f32[2,1536]{1,0:T(2,128)S(1)} %pad_maximum_fusion.12.gain_ref), custom_call_target="tpu_custom_call" | custom-call | bytes 250000000 | tf_op jit(solution)/shard_map/sum_blocks/pallas_call | solution.py:661
  873.8 1.7 copy-done.3
  875.5 3.5 all-to-all-start.1
  879.0 2.0 fusion.67
  883.5 3.2 fusion.66
  886.6 4.3 all-to-all-done.1
  890.9 25.6 %spread.1 = (f32[20,384,1024]{2,1,0:T(8,128)}, f32[20,384,512]{2,1,0:T(8,128)}) custom-call(bf16[4,4,384,1280]{3,2,1,0:T(8,128)(2,1)} %bitcast.162, bf16[4,4,384,640]{3,2,1,0:T(8,128)(2,1)} %bitcast.169), custom_call_target="tpu_custom_call" | custom-call | tf_op jit(solution)/shard_map/spread/pallas_call | solution.py:707
  (191 shorter events, 31.9 us)
Async XLA Ops:
  7.2 2.7 copy-start
  7.2 131.0 %all-gather.7.cloned.1.call-start = ((), (), s32[]{:S(2)}) async-start(), calls=%async_computation.2 | async-start | bytes 4595712 | tf_op jit(solution)/shard_map/all_gather | solution.py:818
  9.8 161.7 %all-gather.9.cloned.1.call-start = ((), (), s32[]{:S(2)}) async-start(), calls=%async_computation.3 | async-start | bytes 2506752 | tf_op jit(solution)/shard_map/all_gather | solution.py:820
  10.6 880.3 %all-gather.13.cloned.1.call-start = ((), (), s32[]{:S(2)}) async-start(), calls=%async_computation.5 | async-start | bytes 9830400 | tf_op jit(solution)/shard_map/all_gather | solution.py:982
  16.7 145.6 %copy-start.11 = (pred[256,1024]{0,1:T(8,128)(4,1)}, pred[256,1024]{0,1:T(8,128)(4,1)S(1)}, u32[]{:S(2)}) copy-start(pred[256,1024]{0,1:T(8,128)(4,1)S(1)} %fusion.28) | copy-start | bytes 786436
  134.1 8.6 copy-start.42
  134.1 53.3 %copy-start.38 = (f32[1536]{0:T(1024)}, f32[1536]{0:T(1024)S(1)}, u32[]{:S(2)}) copy-start(f32[1536]{0:T(1024)S(1)} %get-tuple-element.67) | copy-start | bytes 18436
  137.3 5.5 copy-start.18
  138.2 4.7 copy-start.34
  157.5 2.3 copy-start.20
  157.7 10.0 %copy-start.16 = (bf16[1024,256]{0,1:T(8,128)(2,1)}, bf16[1024,256]{0,1:T(8,128)(2,1)S(1)}, u32[]{:S(2)}) copy-start(bf16[1024,256]{0,1:T(8,128)(2,1)S(1)} %copy.125) | copy-start | bytes 1572868
  157.8 2.0 copy-start.22
  159.8 4.5 copy-start.5
  159.8 4.5 copy-start.36
  164.3 3.5 copy-start.40
  167.7 2.6 copy-start.6
  167.7 18.8 %copy-start.13 = (bf16[256,1536]{1,0:T(8,128)(2,1)S(1)}, bf16[256,1536]{1,0:T(8,128)(2,1)}, u32[]{:S(2)}) copy-start(bf16[256,1536]{1,0:T(8,128)(2,1)} %get-tuple-element.36) | copy-start | bytes 2359300
  171.5 136.6 %copy-start.24 = (bf16[4,64,3,256]{3,1,2,0:T(8,128)(2,1)}, bf16[4,64,3,256]{3,1,2,0:T(8,128)(2,1)S(1)}, u32[]{:S(2)}) copy-start(bf16[4,64,3,256]{3,1,2,0:T(8,128)(2,1)S(1)} %convolution_convert_fusion.7) | copy-start | bytes 1179652
  175.0 11.6 %collective-permute-start = (bf16[128,1536]{1,0:T(8,128)(2,1)}, bf16[128,1536]{1,0:T(8,128)(2,1)S(1)}, u32[]{:S(2)}, u32[]{:S(2)}) collective-permute-start(bf16[128,1536]{1,0:T(8,128)(2,1)} %dynamic-slice_convert_fusion.1), channel_id=1, source_target_pairs={{0,1},{1,0},{2,3},{3,2},{4,5},{5,4},{6,7},{7,6},{8,9},{9,8},{10,11... | collective-permute-start | bytes 1179656 | tf_op jit(solution)/shard_map/ppermute | solution.py:778
  187.4 0.9 copy-start.9
  187.4 0.9 copy-start.53
  187.4 120.7 %copy-start.46 = (f32[128]{0:T(128)}, f32[128]{0:T(128)S(1)}, u32[]{:S(2)}) copy-start(f32[128]{0:T(128)S(1)} %add_rsqrt_fusion.2) | copy-start | bytes 1540
  189.7 118.4 %copy-start.32 = (f32[128,40]{1,0:T(8,128)}, f32[128,40]{1,0:T(8,128)S(1)}, u32[]{:S(2)}) copy-start(f32[128,40]{1,0:T(8,128)S(1)} %get-tuple-element.102) | copy-start | bytes 61444
  189.7 118.4 %copy-start.48 = (f32[128]{0:T(128)}, f32[128]{0:T(128)S(1)}, u32[]{:S(2)}) copy-start(f32[128]{0:T(128)S(1)} %get-tuple-element.101) | copy-start | bytes 1540
  189.9 118.2 %copy-start.50 = (f32[128]{0:T(128)}, f32[128]{0:T(128)S(1)}, u32[]{:S(2)}) copy-start(f32[128]{0:T(128)S(1)} %fusion.50) | copy-start | bytes 1540
  311.4 22.7 %copy-start.31 = (bf16[1536,640]{1,0:T(8,128)(2,1)S(1)}, bf16[1536,640]{1,0:T(8,128)(2,1)}, u32[]{:S(2)}) copy-start(bf16[1536,640]{1,0:T(8,128)(2,1)} %get-tuple-element.42) | copy-start | bytes 5898244
  390.4 23.9 %copy-start.8 = (bf16[4096,640]{0,1:T(8,128)(2,1)S(1)}, bf16[4096,640]{0,1:T(8,128)(2,1)}, u32[]{:S(2)}) copy-start(bf16[4096,640]{0,1:T(8,128)(2,1)} %get-tuple-element.78) | copy-start | bytes 15728644
  452.2 120.2 %copy-start.4 = (bf16[1536,640]{1,0:T(8,128)(2,1)S(1)}, bf16[1536,640]{1,0:T(8,128)(2,1)}, u32[]{:S(2)}) copy-start(bf16[1536,640]{1,0:T(8,128)(2,1)} %convolution_convert_fusion.3) | copy-start | bytes 5898244
  570.5 1.9 copy-start.2
  572.4 92.4 %copy-start.37 = (f32[4,3,256]{2,1,0:T(4,128)S(1)}, f32[4,3,256]{2,1,0:T(4,128)}, u32[]{:S(2)}) copy-start(f32[4,3,256]{2,1,0:T(4,128)} %copy-done.36) | copy-start | bytes 36868
  572.4 92.4 %copy-start.41 = (f32[4,3,256]{2,1,0:T(4,128)S(1)}, f32[4,3,256]{2,1,0:T(4,128)}, u32[]{:S(2)}) copy-start(f32[4,3,256]{2,1,0:T(4,128)} %copy-done.40) | copy-start | bytes 36868
  572.4 92.4 %copy-start.33 = (f32[128,40]{1,0:T(8,128)S(1)}, f32[128,40]{1,0:T(8,128)}, u32[]{:S(2)}) copy-start(f32[128,40]{1,0:T(8,128)} %copy-done.32) | copy-start | bytes 61444
  572.4 92.4 %copy-start.45 = (pred[128,40]{1,0:T(8,128)(4,1)S(1)}, pred[128,40]{1,0:T(8,128)(4,1)}, u32[]{:S(2)}) copy-start(pred[128,40]{1,0:T(8,128)(4,1)} %get-tuple-element.103) | copy-start | bytes 15364
  572.4 92.4 %copy-start.49 = (f32[128]{0:T(128)S(1)}, f32[128]{0:T(128)}, u32[]{:S(2)}) copy-start(f32[128]{0:T(128)} %copy-done.48) | copy-start | bytes 1540
  572.4 92.4 %copy-start.51 = (f32[128]{0:T(128)S(1)}, f32[128]{0:T(128)}, u32[]{:S(2)}) copy-start(f32[128]{0:T(128)} %copy-done.50) | copy-start | bytes 1540
  664.1 1.1 copy-start.10
  664.1 1.1 copy-start.39
  664.1 1.1 copy-start.47
  664.1 2.6 copy-start.54
  664.1 3.4 copy-start.26
  664.1 226.8 %all-gather.11.cloned.1.call-start = ((), (), s32[]{:S(2)}) async-start(), calls=%async_computation.4 | async-start | bytes 19660800 | tf_op jit(solution)/shard_map/all_gather | solution.py:981
  666.7 0.9 copy-start.15
  680.4 0.9 copy-start.28
  681.3 14.8 %copy-start.12 = (pred[256,1024]{0,1:T(8,128)(4,1)S(1)}, pred[256,1024]{0,1:T(8,128)(4,1)}, u32[]{:S(2)}) copy-start(pred[256,1024]{0,1:T(8,128)(4,1)} %copy-done.11) | copy-start | bytes 786436
  681.3 14.8 %copy-start.17 = (bf16[1024,256]{0,1:T(8,128)(2,1)S(1)}, bf16[1024,256]{0,1:T(8,128)(2,1)}, u32[]{:S(2)}) copy-start(bf16[1024,256]{0,1:T(8,128)(2,1)} %copy-done.16) | copy-start | bytes 1572868
  702.7 9.4 %copy-start.23 = (bf16[256,12,64]{0,2,1:T(8,128)(2,1)S(1)}, bf16[256,12,64]{0,2,1:T(8,128)(2,1)}, u32[]{:S(2)}) copy-start(bf16[256,12,64]{0,2,1:T(8,128)(2,1)} %copy-done.22) | copy-start | bytes 1179652
  709.4 2.7 copy-start.7
  714.2 24.6 %copy-start.21 = (bf16[1024,256]{0,1:T(8,128)(2,1)S(1)}, bf16[1024,256]{0,1:T(8,128)(2,1)}, u32[]{:S(2)}) copy-start(bf16[1024,256]{0,1:T(8,128)(2,1)} %copy-done.20) | copy-start | bytes 1572868
  731.6 12.2 %copy-start.35 = (f32[256,32]{0,1:T(8,128)S(1)}, f32[256,32]{0,1:T(8,128)}, u32[]{:S(2)}) copy-start(f32[256,32]{0,1:T(8,128)} %copy-done.34) | copy-start | bytes 98308
  731.6 12.2 %copy-start.44 = (f32[256,32]{0,1:T(8,128)S(1)}, f32[256,32]{0,1:T(8,128)}, u32[]{:S(2)}) copy-start(f32[256,32]{0,1:T(8,128)} %get-tuple-element.96) | copy-start | bytes 98308
  743.7 6.7 copy-start.19
  747.7 8.1 copy-start.30
  747.8 5.8 copy-start.25
  747.8 5.8 copy-start.29
  748.6 17.9 %collective-permute-start.1 = (bf16[128,1536]{1,0:T(8,128)(2,1)}, bf16[128,1536]{1,0:T(8,128)(2,1)}, u32[]{:S(2)}, u32[]{:S(2)}) collective-permute-start(bf16[128,1536]{1,0:T(8,128)(2,1)} %dynamic-slice_convert_fusion), channel_id=1, source_target_pairs={{0,1},{1,0},{2,3},{3,2},{4,5},{5,4},{6,7},{7,6},{8,9},{9,8},{10,11... | collective-permute-start | bytes 1179656 | tf_op jit(solution)/shard_map/ppermute | solution.py:778
  755.9 10.6 %copy-start.52 = (f32[128]{0:T(128)S(1)}, f32[128]{0:T(128)}, u32[]{:S(2)}) copy-start(f32[128]{0:T(128)} %get-tuple-element.93) | copy-start | bytes 1540
  755.9 10.6 %copy-start.14 = (bf16[256,1536]{1,0:T(8,128)(2,1)S(1)}, bf16[256,1536]{1,0:T(8,128)(2,1)}, u32[]{:S(2)}) copy-start(bf16[256,1536]{1,0:T(8,128)(2,1)} %get-tuple-element.36) | copy-start | bytes 2359300
  755.9 10.6 %copy-start.43 = (f32[1536]{0:T(1024)S(1)}, f32[1536]{0:T(1024)}, u32[]{:S(2)}) copy-start(f32[1536]{0:T(1024)} %copy-done.42) | copy-start | bytes 18436
  755.9 12.2 %copy-start.27 = (bf16[128,1536]{1,0:T(8,128)(2,1)S(1)}, bf16[128,1536]{1,0:T(8,128)(2,1)}, u32[]{:S(2)}) copy-start(bf16[128,1536]{1,0:T(8,128)(2,1)} %constant_dynamic-slice_fusion.4) | copy-start | bytes 1179652
  771.8 103.7 %all-to-all-start = ((bf16[128,2,768]{2,0,1:T(8,128)(2,1)}), bf16[128,2,768]{2,0,1:T(8,128)(2,1)S(1)}, u32[]{:S(2)}, u32[]{:S(2)}) async-start(bf16[128,2,768]{2,0,1:T(8,128)(2,1)} %bitcast.149), calls=%async_computation | async-start | bytes 786432 | tf_op jit(solution)/shard_map/all_to_all | solution.py:999
  873.8 1.7 copy-start.3
  875.5 15.4 %all-to-all-start.1 = ((f32[128,2,768]{2,0,1:T(8,128)}), f32[128,2,768]{2,0,1:T(8,128)S(1)}, u32[]{:S(2)}, u32[]{:S(2)}) async-start(f32[128,2,768]{2,0,1:T(8,128)} %bitcast.148), calls=%async_computation.1 | async-start | bytes 1572864 | tf_op jit(solution)/shard_map/all_to_all | solution.py:1068
  890.9 27.2 %copy-start.1 = (bf16[384,768]{1,0:T(8,128)(2,1)S(1)}, bf16[384,768]{1,0:T(8,128)(2,1)}, u32[]{:S(2)}) copy-start(bf16[384,768]{1,0:T(8,128)(2,1)} %param.22) | copy-start | bytes 1769476
Sparse Core Ops, SparseCore 0:
  10.9 94.6 all-gather.6
  108.4 41.7 all-gather.8
  664.3 62.1 all-gather.12
  727.9 130.6 all-gather.10

commit v5 on v4

--- a/solution.py
+++ b/solution.py
@@ -523,9 +523,16 @@
     return (out[0].reshape(rows, width), out[1])
 
 
-def sum_kernel(across_dp, part_ref, gain_ref, out_ref, total_ref, *scratch):
-    own, from_core, from_chip, across, result, gains, load_sem, send_sem, recv_sem, gain_sems = scratch
-    nd = part_ref.shape[0]
+def sum_kernel(across_dp, count, *refs):
+    parts, gain_ref, out_ref, total_ref = (refs[:count], *refs[count : count + 3])
+    own, from_core, from_chip, across, result, gains, load_sem, send_sem, recv_sem, gain_sems = refs[
+        count + 3 :
+    ]
+    spans, start = ([], 0)
+    for ref in parts:
+        spans.append(pl.ds(start, ref.shape[-1]))
+        start += ref.shape[-1]
+    nd = parts[0].shape[0]
     z, y, k, x = place()
     y_partner, core = (device(z, 1 - y, k, x), device(z, y, 1 - k, x))
     x_partner = device(z, y, k, 1 - x)
@@ -548,7 +555,7 @@
     gain_copy(0, core)
     order = ([2, 1, 3] if nd == 4 else list(range(1, nd))) + [0]
     sends, loads = ([], [])
-    core_slot, chip_slot, across_slot, result_slot = (0, nd * 2, nd * 3, nd * 4)
+    chip_slot, across_slot, result_slot, core_slot = (0, nd, nd * 2, nd * 2 + 3)
 
     def send(source, there, target, slot):
         copy = pltpu.make_async_remote_copy(
@@ -584,11 +591,14 @@
     for step, dz in enumerate(order):
         for dy in (1, 0):
             at = step * 2 + dy
-            block = part_ref.at[(z + dz) % nd, (y + dy) % 2]
-            send(block.at[1 - k], from_core.at[at], core, core_slot + at)
-            load = pltpu.make_async_copy(block.at[k], own.at[at], load_sem.at[at])
-            load.start()
-            loads.append(load)
+            for ref, span in zip(parts, spans):
+                block = ref.at[(z + dz) % nd, (y + dy) % 2]
+                send(block.at[1 - k], from_core.at[at, :, span], core, core_slot + len(loads))
+                load = pltpu.make_async_copy(
+                    block.at[k], own.at[at, :, span], load_sem.at[len(loads)]
+                )
+                load.start()
+                loads.append(load)
     stages = [y_partner, x_partner]
     if nd > 1:
         stages += [device(z + 1 - z % 2 * 2, y, k, x), device((z + 2) % nd, y, k, x)]
@@ -602,8 +612,10 @@
         if step < nd:
             for dy in (1, 0):
                 at = step * 2 + dy
-                loads[step * 2 + 1 - dy].wait()
-                arrived(from_core.at[at], core_slot + at)
+                for which, span in enumerate(spans):
+                    slot = (step * 2 + 1 - dy) * count + which
+                    loads[slot].wait()
+                    arrived(from_core.at[at, :, span], core_slot + slot)
                 add(at, from_core, at)
                 if dy:
                     send(own.at[at], from_chip.at[step], y_partner, chip_slot + step)
@@ -655,12 +667,15 @@
         copy.wait_send()
 
 
-def sum_blocks(part, gain, nd, collective_id):
-    rows, width = (part.shape[0] // (nd * 4), part.shape[1])
+def sum_blocks(parts, gain, nd, collective_id):
+    rows, width = (parts[0].shape[0] // (nd * 4), sum(part.shape[1] for part in parts))
+    count = len(parts)
+    sends = nd * (2 * count + 2) + 3
     shape = (2, 2, rows, width) if nd > 1 else (rows, width)
     out = pl.pallas_call(
-        functools.partial(sum_kernel, nd > 1),
-        in_specs=[pl.BlockSpec(memory_space=pl.ANY), pl.BlockSpec(memory_space=pltpu.VMEM)],
+        functools.partial(sum_kernel, nd > 1, count),
+        in_specs=[pl.BlockSpec(memory_space=pl.ANY)] * count
+        + [pl.BlockSpec(memory_space=pltpu.VMEM)],
         out_specs=[pl.BlockSpec(memory_space=pltpu.VMEM)] * 2,
         out_shape=[jax.ShapeDtypeStruct(shape, F32), jax.ShapeDtypeStruct(gain.shape, F32)],
         scratch_shapes=[
@@ -670,9 +685,9 @@
             pltpu.VMEM((max(nd - 1, 1), rows, width), BF),
             pltpu.VMEM((2, 2, rows, width) if nd > 1 else (1, 1, 16, LANES), BF),
             pltpu.VMEM((2, 6, *gain.shape), F32),
-            pltpu.SemaphoreType.DMA((nd * 2,)),
-            pltpu.SemaphoreType.DMA((nd * 4 + 3,)),
-            pltpu.SemaphoreType.DMA((nd * 4 + 3,)),
+            pltpu.SemaphoreType.DMA((nd * 2 * count,)),
+            pltpu.SemaphoreType.DMA((sends,)),
+            pltpu.SemaphoreType.DMA((sends,)),
             pltpu.SemaphoreType.DMA((2, 5)),
         ],
         compiler_params=pltpu.CompilerParams(
@@ -680,7 +695,7 @@
         ),
         cost_estimate=COST,
         name="sum_blocks",
-    )(part.reshape(nd, 2, 2, rows, width), gain)
+    )(*[part.reshape(nd, 2, 2, rows, part.shape[1]) for part in parts], gain)
     return (out[0].reshape(-1, width), out[1])
 
 
@@ -975,12 +990,7 @@
     if kernels:
         grad_in, grad_upper, grad_lower = lax.optimization_barrier((grad_in, grad_upper, grad_lower))
         back_sub, grad_upper = reduce_rows([grad_in, grad_gates], grad_upper, {0: 1, 4: 2, 5: 3}, nd, 3)
-        mixed, back_sub = lax.optimization_barrier((mixed, back_sub))
-        mixed_sub, grad_lower = reduce_rows([mixed], grad_lower, {0: 2, 1: 1, 2: 3}, nd, 4)
-        back_sub, mixed_sub = lax.optimization_barrier((back_sub, mixed_sub))
         grad_upper = lax.all_gather(grad_upper, "ctx", axis=0)
-        grad_lower = lax.all_gather(grad_lower, "ctx", axis=0)
-        grad_expert_in, grad_expert_out = spread(grad_upper, grad_lower, own_count)
     else:
         back = jnp.concatenate([grad_in, grad_gates], axis=1)
         back_sub = lax.psum_scatter(back, ALL, scatter_dimension=0, tiled=True).astype(F32)
@@ -996,8 +1006,6 @@
         grad_expert_in = grad_up.reshape(d_local, local_count, 2 * FF).astype(F32)
         grad_expert_out = grad_low.reshape(d_local, local_count, FF).astype(F32)
 
-    result = lax.all_to_all((middle + mixed_sub).astype(BF), "tensor", 1, 0, tiled=True)
-
     gate_grads = back_sub[:, D : D + EXPERTS] * kept
     logit_grads = (
         gates * (gate_grads - jnp.sum(gates * gate_grads, axis=1, keepdims=True))
@@ -1041,9 +1049,15 @@
         [grad_keys.reshape(pack_len, kv_width), grad_values.reshape(pack_len, kv_width)], axis=1
     ).astype(BF)
     if kernels:
-        grad_kv, _ = sum_blocks(grad_kv, jnp.zeros((8, LANES), F32), 1, 5)
+        grad_kv, _ = sum_blocks([grad_kv], jnp.zeros((8, LANES), F32), 1, 5)
+        mixed, _ = lax.optimization_barrier((mixed, grad_kv))
+        mixed_sub, grad_lower = reduce_rows([mixed], grad_lower, {0: 2, 1: 1, 2: 3}, nd, 4)
+        grad_lower, grad_upper = lax.optimization_barrier((grad_lower, grad_upper))
+        grad_lower = lax.all_gather(grad_lower, "ctx", axis=0)
+        grad_expert_in, grad_expert_out = spread(grad_upper, grad_lower, own_count)
     else:
         grad_kv = lax.psum_scatter(grad_kv, "ctx", scatter_dimension=0, tiled=True).astype(F32)
+    result = lax.all_to_all((middle + mixed_sub).astype(BF), "tensor", 1, 0, tiled=True)
     grad_turned = jnp.concatenate(
         [
             grad_queries.reshape(n_rows, q_heads, HEAD_DIM),
@@ -1069,13 +1083,14 @@
 
     grad_qkv_w = dot(h_one, grad_qkv, ((0,), (0,)))
     gain_grads = jnp.stack([grad_gain_one, grad_gain_two])
-    extra = jnp.zeros((D, LANES - EXPERTS), F32)
-    weight_grads = jnp.concatenate([grad_qkv_w, grad_output_w, grad_router, extra], axis=1).astype(BF)
+    grad_router = jnp.pad(grad_router, ((0, 0), (0, LANES - EXPERTS)))
+    weight_grads = [w.astype(BF) for w in (grad_qkv_w, grad_output_w, grad_router)]
     if kernels:
+        gain_grads, _ = lax.optimization_barrier((gain_grads, mixed_sub))
         weight_grads, gain_grads = sum_blocks(weight_grads, gain_grads, nd, 6)
     else:
         weight_grads = lax.psum_scatter(
-            weight_grads, ("dp", "ctx"), scatter_dimension=0, tiled=True
+            jnp.concatenate(weight_grads, axis=1), ("dp", "ctx"), scatter_dimension=0, tiled=True
         )
         weight_grads = lax.all_gather(weight_grads, "ctx", axis=0, tiled=True).astype(F32)
         gain_grads = jnp.sum(lax.all_gather(gain_grads, ALL, axis=0), axis=0)

time: 935 us -> 924 us (0.988)
  local copies, waits for them, and re-layouts: 66.4 us -> 48.2 us
    pallas_call x2, Pallas kernels: 210 us -> 224 us  [reduce_rows(): pl.pallas_call(functools.partial(reduce_kernel, count, when), in_specs=[p...]
    concatenate x1 -> x0, local copies, waits for them, and re-layouts: 10.6 us -> none  [on_device(): jnp.concatenate([grad_qkv_w, grad_output_w, grad_router, extra], axis=1)]
  transfers between devices with their start and end apart: 8 -> 8, of which waited for: 2 -> 2; matrix products, arithmetic and copies ran while one was open for 12% -> 12% of each run, Pallas kernels for 26% -> 37%
where the time goes in v5:
time: 924 us; the launch traced here: 915 us
  Pallas kernels  600 us (65%)
  matrix products  185 us (20%)
  local copies, waits for them, and re-layouts  48.2 us (5%)
  other arithmetic  33 us (4%)
  between operations  15.2 us (2%)
  waiting for transfers between devices  14.3 us (2%)
  starting transfers between devices  10.1 us (1%)
  blocking collectives  9.44 us (1%)
    pallas_call x2, Pallas kernels, gather_rows(): pl.pallas_call(functools.partial(gather_kernel, own_count, units, len(pai...  230 us
    pallas_call x2, Pallas kernels, reduce_rows(): pl.pallas_call(functools.partial(reduce_kernel, count, when), in_specs=[p...  224 us
    dot_general x16, matrix products, dot(): return lax.dot_general(a, b, (dims, ((), ())), preferred_element_type=F32)  160 us
    pallas_call x2, Pallas kernels, sum_blocks(): pl.pallas_call(functools.partial(sum_kernel, nd > 1, count), in_specs=[pl...  108 us
    pallas_call x1, Pallas kernels, spread(): pl.pallas_call(spread_kernel, grid=(d_local // block,), in_specs=[pl.Bloc...  25.6 us
  transfers between devices with their start and end apart: 8, of which 2 were waited for; matrix products, arithmetic and copies ran while one was open for 12% of the time, Pallas kernels for 37%

profile of v5, /device:TPU:0, one launch (start us, length us, event | category | flops | bytes accessed | tf_op | source)
XLA Modules:
  0.0 914.9 jit_solution(5269926996886832303)
XLA Ops:
  7.2 0.9 copy.114
  8.2 1.6 fusion.44
  12.7 113.9 %gather_rows.2 = (bf16[4,2,2,2,128,1536]{5,4,3,2,1,0:T(8,128)(2,1)}, bf16[1536,640]{1,0:T(8,128)(2,1)}, bf16[256,1536]{1,0:T(8,128)(2,1)}, f32[2,1536]{1,0:T(2,128)}) custom-call(bf16[2,128,768]{2,1,0:T(8,128)(2,1)} %bitcast.198, bf16[20,384,512]{2,1,0:T(8,128)(2,1)} %bitcast.167, bf16[256,768]{1,0:T(8,128)(2,1)} %refs_2_.1, f32[2,768]{1,0:T(2,128)} %pad_maximum_fusion.13.refs_3_), custom_call_target="tpu_custom_call" | custom-call | bytes 250000000 | tf_op jit(solution)/shard_map/gather_rows/pallas_call | solution.py:243
  126.6 1.4 fusion.18
  128.9 1.8 constant_dynamic-slice_fusion.4
  130.6 1.4 fusion.20
  134.1 3.3 fusion.16
  138.9 1.6 pad_maximum_fusion.10.own_ref
  140.5 11.4 %gather_ctx.1 = bf16[2,2,256,512]{3,2,1,0:T(8,128)(2,1)} custom-call(bf16[256,512]{1,0:T(8,128)(2,1)} %pad_maximum_fusion.10.own_ref), custom_call_target="tpu_custom_call" | custom-call | tf_op jit(solution)/shard_map/gather_ctx/pallas_call | solution.py:299
  151.9 1.3 fusion.69
  153.6 2.0 fusion.13
  155.6 2.6 fusion.3
  158.2 1.9 copy-done.6
  160.1 3.2 divide_convert_fusion
  163.4 2.6 copy-done.7
  166.0 1.2 convolution_convert_fusion.7
  167.1 2.6 fusion.71
  170.6 1.5 collective-permute-start
  172.3 9.9 %collective-permute-done = bf16[128,1536]{1,0:T(8,128)(2,1)S(1)} collective-permute-done((bf16[128,1536]{1,0:T(8,128)(2,1)}, bf16[128,1536]{1,0:T(8,128)(2,1)S(1)}, u32[]{:S(2)}, u32[]{:S(2)}) %collective-permute-start) | collective-permute-done | bytes 393248 | tf_op jit(solution)/shard_map/ppermute | solution.py:793
  184.0 1.3 fusion.70
  187.3 116.5 %gather_rows.3 = (bf16[4,2,2,2,2,64,1664]{6,5,4,3,2,1,0:T(8,128)(2,1)}, bf16[1536,1280]{1,0:T(8,128)(2,1)}) custom-call(bf16[2,64,1664]{2,1,0:T(8,128)(2,1)} %bitcast.188, bf16[20,384,1024]{2,1,0:T(8,128)(2,1)} %bitcast.160), custom_call_target="tpu_custom_call" | custom-call | bytes 250000000 | tf_op jit(solution)/shard_map/gather_rows/pallas_call | solution.py:243
  303.9 2.1 fusion.66
  307.2 22.7 %fusion.6 = f32[4096,1280]{0,1:T(8,128)} fusion(bf16[1536,1280]{1,0:T(8,128)(2,1)} %get-tuple-element.41, bf16[4096,1664]{1,0:T(8,128)(2,1)} %bitcast.194), kind=kOutput, calls=%fused_computation.17 | convolution fusion | flops 16106127360 | bytes 37486592 | tf_op jit(solution)/shard_map/dot_general | solution.py:760
  330.0 33.2 %multiply_convert_fusion.1 = (bf16[4096,640]{0,1:T(8,128)(2,1)}, bf16[4096,640]{0,1:T(8,128)(2,1)}, f32[4096,640]{0,1:T(8,128)}, bf16[4096,640]{0,1:T(8,128)(2,1)}) fusion(f32[4096,1280]{0,1:T(8,128)} %fusion.6, f32[4096,5]{0,1:T(8,128)S(1)} %copy.123, bf16[4096,1536]{1,0:T(8,128)(2,1)} %bitcast.163, bf16[1536,640]{1,0:T(8,128)(2,1)S(1)} %copy-done.31), kind=kOutput, calls=%fused_computation.22 | convolution fusion | flops 8100249600 | bytes 61816832 | tf_op jit(solution)/shard_map/dot_general | solution.py:760
  363.2 23.2 %fusion.10 = bf16[1536,1280]{1,0:T(8,128)(2,1)} fusion(bf16[4096,1664]{1,0:T(8,128)(2,1)} %bitcast.195, bf16[4096,640]{0,1:T(8,128)(2,1)} %get-tuple-element.76, bf16[4096,640]{0,1:T(8,128)(2,1)} %get-tuple-element.75), kind=kOutput, calls=%fused_computation.26 | convolution fusion | flops 16129064960 | bytes 27000832 | tf_op jit(solution)/shard_map/dot_general | solution.py:760
  386.4 23.9 %convolution_convert_fusion.1 = bf16[4096,1536]{1,0:T(8,128)(2,1)} fusion(bf16[1536,1280]{1,0:T(8,128)(2,1)} %get-tuple-element.41, bf16[4096,640]{0,1:T(8,128)(2,1)} %get-tuple-element.76, bf16[4096,640]{0,1:T(8,128)(2,1)} %get-tuple-element.75), kind=kOutput, calls=%fused_computation.3 | convolution fusion | flops 16133390336 | bytes 27000832 | tf_op jit(solution)/shard_map/dot_general | solution.py:760
  410.3 1.6 fusion.8
  411.9 16.3 %convolution_convert_fusion.4 = bf16[1536,640]{1,0:T(8,128)(2,1)} fusion(bf16[4096,1536]{1,0:T(8,128)(2,1)} %bitcast.164, bf16[4096,640]{0,1:T(8,128)(2,1)S(1)} %fusion.8), kind=kOutput, calls=%fused_computation.36 | convolution fusion | flops 8054046720 | bytes 19791872 | tf_op jit(solution)/shard_map/dot_general | solution.py:760
  428.2 4.7 reduce_sum.132
  433.6 3.9 dynamic_update_slice.3
  437.6 118.2 %reduce_rows.2 = (f32[2,64,1664]{2,1,0:T(8,128)S(1)}, bf16[4,384,1280]{2,1,0:T(8,128)(2,1)S(1)}) custom-call(bf16[4,2,2,2,2,64,1536]{6,5,4,3,2,1,0:T(8,128)(2,1)} %bitcast.166, bf16[4,2,2,2,2,64,128]{6,5,4,3,2,1,0:T(8,128)(2,1)S(1)} %bitcast.147, bf16[4,384,1280]{2,1,0:T(8,128)(2,1)} %bitcast.177), custom_call_target="tpu_custom_call" | custom-call | bytes 250000000 | tf_op jit(solution)/shard_map/reduce_rows/pallas_call | solution.py:495
  555.8 1.9 copy-done.2
  558.2 1.5 multiply_reduce_fusion
  560.7 9.4 %all_gather.23 = bf16[256,1664]{1,0:T(8,128)(2,1)S(1)} all-gather(bf16[128,1664]{1,0:T(8,128)(2,1)S(1)} %concatenate.50), channel_id=1, replica_groups=mesh['dp'=4,'ctx'=4,'tensor'=2] {'tensor'}, dimensions={0}, use_global_device_ids=true | all-gather | bytes 1277952 | tf_op jit(solution)/shard_map/all_gather | solution.py:1017
  570.1 2.7 convolution_convert_fusion.6
  573.1 6.7 fusion
  580.2 1.2 slice-done.2
  581.4 4.8 fusion.2
  586.2 5.9 fusion.26
  593.0 5.2 fusion.25
  599.3 21.8 %sum_blocks.2 = (f32[256,512]{1,0:T(8,128)S(1)}, f32[8,128]{1,0:T(8,128)}) custom-call(bf16[1,2,2,256,512]{4,3,2,1,0:T(8,128)(2,1)S(1)} %pad_maximum_fusion.3.refs_0_, f32[8,128]{1,0:T(8,128)S(1)} %broadcast_in_dim.47.refs_1_), custom_call_target="tpu_custom_call" | custom-call | bytes 250000000 | tf_op jit(solution)/shard_map/sum_blocks/pallas_call | solution.py:675
  621.1 16.0 %convolution_convert_fusion = bf16[4096,1536]{1,0:T(8,128)(2,1)} fusion(bf16[4096,640]{0,1:T(8,128)(2,1)} %copy-done.18, bf16[1536,640]{1,0:T(8,128)(2,1)} %get-tuple-element.42), kind=kOutput, calls=%fused_computation.2 | convolution fusion | flops 8059355136 | bytes 19791872 | tf_op jit(solution)/shard_map/dot_general | solution.py:760
  637.1 105.8 %reduce_rows.3 = (f32[2,64,1536]{2,1,0:T(8,128)S(1)}, bf16[4,384,640]{2,1,0:T(8,128)(2,1)}) custom-call(bf16[4,2,2,2,2,64,1536]{6,5,4,3,2,1,0:T(8,128)(2,1)} %bitcast.165, bf16[4,384,640]{2,1,0:T(8,128)(2,1)S(1)} %bitcast.151), custom_call_target="tpu_custom_call" | custom-call | bytes 250000000 | tf_op jit(solution)/shard_map/reduce_rows/pallas_call | solution.py:495
  742.9 0.9 copy-done.5
  744.2 4.0 convolution_multiply_fusion
  748.4 3.6 fusion.14
  752.8 1.4 collective-permute-start.1
  754.3 2.1 convolution_convert_fusion.5
  756.4 2.1 convolution_convert_fusion.3
  758.6 1.9 copy.149
  760.4 1.2 pad.5.clone
  761.7 4.5 convolution_convert_fusion.2
  766.2 1.4 fusion.34
  767.6 3.2 fusion.32
  771.6 3.5 all-to-all-start
  775.1 2.1 copy.154
  777.2 86.6 %sum_blocks.3 = (f32[2,2,96,2176]{3,2,1,0:T(8,128)S(1)}, f32[2,1536]{1,0:T(2,128)S(1)}) custom-call(bf16[4,2,2,96,1280]{4,3,2,1,0:T(8,128)(2,1)} %bitcast.159, bf16[4,2,2,96,768]{4,3,2,1,0:T(8,128)(2,1)S(1)} %bitcast.146, bf16[4,2,2,96,128]{4,3,2,1,0:T(8,128)(2,1)S(1)} %bitcast.152, f32[2,1536]{1,0:T(2,128)S(1)} %pad_maximum_fusion.12.refs_3_), custom_call_target="tpu_custom_call" | custom-call | bytes 250000000 | tf_op jit(solution)/shard_map/sum_blocks/pallas_call | solution.py:675
  863.8 1.7 copy-done.3
  865.6 3.5 all-to-all-start.1
  869.1 2.0 fusion.68
  871.2 0.9 slice.154
  873.5 3.2 fusion.67
  876.7 4.3 all-to-all-done.1
  881.0 25.6 %spread.1 = (f32[20,384,1024]{2,1,0:T(8,128)}, f32[20,384,512]{2,1,0:T(8,128)}) custom-call(bf16[4,4,384,1280]{3,2,1,0:T(8,128)(2,1)} %bitcast.161, bf16[4,4,384,640]{3,2,1,0:T(8,128)(2,1)} %bitcast.168), custom_call_target="tpu_custom_call" | custom-call | tf_op jit(solution)/shard_map/spread/pallas_call | solution.py:722
  (201 shorter events, 23.3 us)
Async XLA Ops:
  7.2 2.7 copy-start
  7.2 126.9 %all-gather.7.cloned.1.call-start = ((), (), s32[]{:S(2)}) async-start(), calls=%async_computation.2 | async-start | bytes 4595712 | tf_op jit(solution)/shard_map/all_gather | solution.py:833
  9.8 122.2 %copy-start.47 = (s32[1,1024]{1,0:T(1,128)S(1)}, s32[1,1024]{1,0:T(1,128)}, u32[]{:S(2)}) copy-start(s32[1,1024]{1,0:T(1,128)} %param.15) | copy-start | bytes 12292
  9.8 122.7 %copy-start.46 = (s32[1024,8]{0,1:T(8,128)S(1)}, s32[1024,8]{0,1:T(8,128)}, u32[]{:S(2)}) copy-start(s32[1024,8]{0,1:T(8,128)} %param.17) | copy-start | bytes 98308
  9.9 157.3 %all-gather.9.cloned.1.call-start = ((), (), s32[]{:S(2)}) async-start(), calls=%async_computation.3 | async-start | bytes 2506752 | tf_op jit(solution)/shard_map/all_gather | solution.py:835
  10.6 122.1 %copy-start.57 = (s32[1,1024]{1,0:T(1,128)S(1)}, s32[1,1024]{1,0:T(1,128)}, u32[]{:S(2)}) copy-start(s32[1,1024]{1,0:T(1,128)} %param.16) | copy-start | bytes 12292
  10.6 733.2 %all-gather.11.cloned.1.call-start = ((), (), s32[]{:S(2)}) async-start(), calls=%async_computation.4 | async-start | bytes 19660800 | tf_op jit(solution)/shard_map/all_gather | solution.py:993
  128.8 8.7 copy-start.42
  128.9 54.1 %copy-start.38 = (f32[1536]{0:T(1024)}, f32[1536]{0:T(1024)S(1)}, u32[]{:S(2)}) copy-start(f32[1536]{0:T(1024)S(1)} %get-tuple-element.67) | copy-start | bytes 18436
  132.0 6.5 copy-start.17
  132.6 25.7 %copy-start.11 = (pred[256,1024]{0,1:T(8,128)(4,1)}, pred[256,1024]{0,1:T(8,128)(4,1)S(1)}, u32[]{:S(2)}) copy-start(pred[256,1024]{0,1:T(8,128)(4,1)S(1)} %fusion.28) | copy-start | bytes 786436
  134.1 4.7 copy-start.34
  153.3 2.3 copy-start.19
  153.6 9.8 %copy-start.15 = (bf16[1024,256]{0,1:T(8,128)(2,1)}, bf16[1024,256]{0,1:T(8,128)(2,1)S(1)}, u32[]{:S(2)}) copy-start(bf16[1024,256]{0,1:T(8,128)(2,1)S(1)} %copy.117) | copy-start | bytes 1572868
  153.6 2.0 copy-start.21
  155.6 4.5 copy-start.6
  155.6 4.5 copy-start.36
  160.1 3.2 copy-start.40
  163.3 2.6 copy-start.7
  163.3 18.8 %copy-start.13 = (bf16[256,1536]{1,0:T(8,128)(2,1)S(1)}, bf16[256,1536]{1,0:T(8,128)(2,1)}, u32[]{:S(2)}) copy-start(bf16[256,1536]{1,0:T(8,128)(2,1)} %get-tuple-element.36) | copy-start | bytes 2359300
  167.1 136.7 %copy-start.23 = (bf16[4,64,3,256]{3,1,2,0:T(8,128)(2,1)}, bf16[4,64,3,256]{3,1,2,0:T(8,128)(2,1)S(1)}, u32[]{:S(2)}) copy-start(bf16[4,64,3,256]{3,1,2,0:T(8,128)(2,1)S(1)} %convolution_convert_fusion.7) | copy-start | bytes 1179652
  170.6 11.6 %collective-permute-start = (bf16[128,1536]{1,0:T(8,128)(2,1)}, bf16[128,1536]{1,0:T(8,128)(2,1)S(1)}, u32[]{:S(2)}, u32[]{:S(2)}) collective-permute-start(bf16[128,1536]{1,0:T(8,128)(2,1)} %dynamic-slice_convert_fusion.1), channel_id=1, source_target_pairs={{0,1},{1,0},{2,3},{3,2},{4,5},{5,4},{6,7},{7,6},{8,9},{9,8},{10,11... | collective-permute-start | bytes 1179656 | tf_op jit(solution)/shard_map/ppermute | solution.py:793
  183.0 120.9 %copy-start.48 = (f32[128]{0:T(128)}, f32[128]{0:T(128)S(1)}, u32[]{:S(2)}) copy-start(f32[128]{0:T(128)S(1)} %add_rsqrt_fusion.2) | copy-start | bytes 1540
  185.3 118.5 %copy-start.32 = (f32[128,40]{1,0:T(8,128)}, f32[128,40]{1,0:T(8,128)S(1)}, u32[]{:S(2)}) copy-start(f32[128,40]{1,0:T(8,128)S(1)} %get-tuple-element.102) | copy-start | bytes 61444
  185.3 118.5 %copy-start.50 = (f32[128]{0:T(128)}, f32[128]{0:T(128)S(1)}, u32[]{:S(2)}) copy-start(f32[128]{0:T(128)S(1)} %get-tuple-element.101) | copy-start | bytes 1540
  185.5 118.3 %copy-start.52 = (f32[128]{0:T(128)}, f32[128]{0:T(128)S(1)}, u32[]{:S(2)}) copy-start(f32[128]{0:T(128)S(1)} %fusion.51) | copy-start | bytes 1540
  307.2 22.7 %copy-start.31 = (bf16[1536,640]{1,0:T(8,128)(2,1)S(1)}, bf16[1536,640]{1,0:T(8,128)(2,1)}, u32[]{:S(2)}) copy-start(bf16[1536,640]{1,0:T(8,128)(2,1)} %get-tuple-element.42) | copy-start | bytes 5898244
  386.4 23.9 %copy-start.8 = (bf16[4096,640]{0,1:T(8,128)(2,1)S(1)}, bf16[4096,640]{0,1:T(8,128)(2,1)}, u32[]{:S(2)}) copy-start(bf16[4096,640]{0,1:T(8,128)(2,1)} %get-tuple-element.78) | copy-start | bytes 15728644
  411.9 16.3 %copy-start.18 = (bf16[4096,640]{0,1:T(8,128)(2,1)}, bf16[4096,640]{0,1:T(8,128)(2,1)S(1)}, u32[]{:S(2)}) copy-start(bf16[4096,640]{0,1:T(8,128)(2,1)S(1)} %fusion.8) | copy-start | bytes 15728644
  437.5 120.3 %copy-start.37 = (f32[4,3,256]{2,1,0:T(4,128)S(1)}, f32[4,3,256]{2,1,0:T(4,128)}, u32[]{:S(2)}) copy-start(f32[4,3,256]{2,1,0:T(4,128)} %copy-done.36) | copy-start | bytes 36868
  437.5 120.3 %copy-start.41 = (f32[4,3,256]{2,1,0:T(4,128)S(1)}, f32[4,3,256]{2,1,0:T(4,128)}, u32[]{:S(2)}) copy-start(f32[4,3,256]{2,1,0:T(4,128)} %copy-done.40) | copy-start | bytes 36868
  437.5 120.3 %copy-start.33 = (f32[128,40]{1,0:T(8,128)S(1)}, f32[128,40]{1,0:T(8,128)}, u32[]{:S(2)}) copy-start(f32[128,40]{1,0:T(8,128)} %copy-done.32) | copy-start | bytes 61444
  437.5 120.3 %copy-start.45 = (pred[128,40]{1,0:T(8,128)(4,1)S(1)}, pred[128,40]{1,0:T(8,128)(4,1)}, u32[]{:S(2)}) copy-start(pred[128,40]{1,0:T(8,128)(4,1)} %get-tuple-element.103) | copy-start | bytes 15364
  437.5 120.3 %copy-start.51 = (f32[128]{0:T(128)S(1)}, f32[128]{0:T(128)}, u32[]{:S(2)}) copy-start(f32[128]{0:T(128)} %copy-done.50) | copy-start | bytes 1540
  437.5 120.3 %copy-start.53 = (f32[128]{0:T(128)S(1)}, f32[128]{0:T(128)}, u32[]{:S(2)}) copy-start(f32[128]{0:T(128)} %copy-done.52) | copy-start | bytes 1540
  437.5 120.7 %copy-start.10 = (f32[128,1536]{1,0:T(8,128)S(1)}, f32[128,1536]{1,0:T(8,128)}, u32[]{:S(2)}) copy-start(f32[128,1536]{1,0:T(8,128)} %copy-done.9) | copy-start | bytes 2359300
  437.5 120.6 %copy-start.39 = (f32[1536]{0:T(1024)S(1)}, f32[1536]{0:T(1024)}, u32[]{:S(2)}) copy-start(f32[1536]{0:T(1024)} %copy-done.38) | copy-start | bytes 18436
  437.5 120.6 %copy-start.49 = (f32[128]{0:T(128)S(1)}, f32[128]{0:T(128)}, u32[]{:S(2)}) copy-start(f32[128]{0:T(128)} %copy-done.48) | copy-start | bytes 1540
  555.8 1.9 copy-start.2
  557.7 2.0 copy-start.56
  557.7 2.1 copy-start.25
  557.7 323.3 %all-gather.13.cloned.1.call-start = ((), (), s32[]{:S(2)}) async-start(), calls=%async_computation.5 | async-start | bytes 9830400 | tf_op jit(solution)/shard_map/all_gather | solution.py:1056
  558.0 15.1 %copy-start.12 = (pred[256,1024]{0,1:T(8,128)(4,1)S(1)}, pred[256,1024]{0,1:T(8,128)(4,1)}, u32[]{:S(2)}) copy-start(pred[256,1024]{0,1:T(8,128)(4,1)} %copy-done.11) | copy-start | bytes 786436
  558.0 15.1 %copy-start.16 = (bf16[1024,256]{0,1:T(8,128)(2,1)S(1)}, bf16[1024,256]{0,1:T(8,128)(2,1)}, u32[]{:S(2)}) copy-start(bf16[1024,256]{0,1:T(8,128)(2,1)} %copy-done.15) | copy-start | bytes 1572868
  570.1 184.1 %copy-start.27 = (bf16[256,1664]{1,0:T(8,128)(2,1)}, bf16[256,1664]{1,0:T(8,128)(2,1)S(1)}, u32[]{:S(2)}) copy-start(bf16[256,1664]{1,0:T(8,128)(2,1)S(1)} %all_gather.23) | copy-start | bytes 2555908
  573.1 6.7 slice-start
  573.1 7.0 slice-start.1
  573.1 8.2 slice-start.2
  581.4 4.8 copy-start.22
  621.1 16.0 %copy-start.4 = (bf16[1536,640]{1,0:T(8,128)(2,1)S(1)}, bf16[1536,640]{1,0:T(8,128)(2,1)}, u32[]{:S(2)}) copy-start(bf16[1536,640]{1,0:T(8,128)(2,1)} %convolution_convert_fusion.4) | copy-start | bytes 5898244
  637.0 107.1 %copy-start.20 = (bf16[1024,256]{0,1:T(8,128)(2,1)S(1)}, bf16[1024,256]{0,1:T(8,128)(2,1)}, u32[]{:S(2)}) copy-start(bf16[1024,256]{0,1:T(8,128)(2,1)} %copy-done.19) | copy-start | bytes 1572868
  743.8 4.3 copy-start.35
  743.8 4.3 copy-start.44
  748.1 8.2 copy-start.24
  748.3 10.1 %copy-start.30 = (bf16[256,16,64]{0,2,1:T(8,128)(2,1)}, bf16[256,16,64]{0,2,1:T(8,128)(2,1)S(1)}, u32[]{:S(2)}) copy-start(bf16[256,16,64]{0,2,1:T(8,128)(2,1)S(1)} %pad_maximum_fusion.6) | copy-start | bytes 1572868
  748.4 10.2 %copy-start.54 = (f32[128]{0:T(128)S(1)}, f32[128]{0:T(128)}, u32[]{:S(2)}) copy-start(f32[128]{0:T(128)} %get-tuple-element.93) | copy-start | bytes 1540
  751.9 6.6 copy-start.28
  752.8 13.4 %collective-permute-start.1 = (bf16[128,1536]{1,0:T(8,128)(2,1)}, bf16[128,1536]{1,0:T(8,128)(2,1)}, u32[]{:S(2)}, u32[]{:S(2)}) collective-permute-start(bf16[128,1536]{1,0:T(8,128)(2,1)} %dynamic-slice_convert_fusion), channel_id=1, source_target_pairs={{0,1},{1,0},{2,3},{3,2},{4,5},{5,4},{6,7},{7,6},{8,9},{9,8},{10,11... | collective-permute-start | bytes 1179656 | tf_op jit(solution)/shard_map/ppermute | solution.py:793
  756.4 9.8 %copy-start.43 = (f32[1536]{0:T(1024)S(1)}, f32[1536]{0:T(1024)}, u32[]{:S(2)}) copy-start(f32[1536]{0:T(1024)} %copy-done.42) | copy-start | bytes 18436
  758.5 9.1 copy-start.26
  760.4 5.7 copy-start.29
  771.6 93.9 %all-to-all-start = ((bf16[128,2,768]{2,0,1:T(8,128)(2,1)}), bf16[128,2,768]{2,0,1:T(8,128)(2,1)S(1)}, u32[]{:S(2)}, u32[]{:S(2)}) async-start(bf16[128,2,768]{2,0,1:T(8,128)(2,1)} %bitcast.190), calls=%async_computation | async-start | bytes 786432 | tf_op jit(solution)/shard_map/all_to_all | solution.py:1060
  865.6 15.4 %all-to-all-start.1 = ((f32[128,2,768]{2,0,1:T(8,128)}), f32[128,2,768]{2,0,1:T(8,128)S(1)}, u32[]{:S(2)}, u32[]{:S(2)}) async-start(f32[128,2,768]{2,0,1:T(8,128)} %bitcast.184), calls=%async_computation.1 | async-start | bytes 1572864 | tf_op jit(solution)/shard_map/all_to_all | solution.py:1082
  881.0 27.2 %copy-start.1 = (bf16[384,768]{1,0:T(8,128)(2,1)S(1)}, bf16[384,768]{1,0:T(8,128)(2,1)}, u32[]{:S(2)}) copy-start(bf16[384,768]{1,0:T(8,128)(2,1)} %param.22) | copy-start | bytes 1769476
  (5 other events, 5.3 us)
Sparse Core Ops, SparseCore 0:
  10.9 88.7 all-gather.6
  102.5 42.9 all-gather.8
  557.8 138.3 all-gather.10
  744.0 64.2 all-gather.12

commit v6 on v5

--- a/solution.py
+++ b/solution.py
@@ -1086,7 +1086,7 @@
     grad_router = jnp.pad(grad_router, ((0, 0), (0, LANES - EXPERTS)))
     weight_grads = [w.astype(BF) for w in (grad_qkv_w, grad_output_w, grad_router)]
     if kernels:
-        gain_grads, _ = lax.optimization_barrier((gain_grads, mixed_sub))
+        gain_grads, grad_tokens, _ = lax.optimization_barrier((gain_grads, grad_tokens, mixed_sub))
         weight_grads, gain_grads = sum_blocks(weight_grads, gain_grads, nd, 6)
     else:
         weight_grads = lax.psum_scatter(

time: 924 us -> 922 us (level)
  Pallas kernels: 600 us -> 582 us
  waiting for transfers between devices: 14.3 us -> 24.9 us
    pallas_call x2, Pallas kernels: 108 us -> 97.8 us  [sum_blocks(): pl.pallas_call(functools.partial(sum_kernel, nd > 1, count), in_specs=[pl...]
    unnamed x128 -> x122, local copies, waits for them, and re-layouts: 17.5 us -> 20.1 us
  transfers between devices with their start and end apart: 8 -> 8, of which waited for: 2 -> 4; matrix products, arithmetic and copies ran while one was open for 12% -> 12% of each run, Pallas kernels for 37% -> 35%
where the time goes in v6:
time: 922 us; the launch traced here: 912 us
  Pallas kernels  582 us (63%)
  matrix products  179 us (19%)
  local copies, waits for them, and re-layouts  53.4 us (6%)
  other arithmetic  37.4 us (4%)
  waiting for transfers between devices  24.9 us (3%)
  between operations  15.4 us (2%)
  starting transfers between devices  11.1 us (1%)
  blocking collectives  9.44 us (1%)
    pallas_call x2, Pallas kernels, gather_rows(): pl.pallas_call(functools.partial(gather_kernel, own_count, units, len(pai...  230 us
    pallas_call x2, Pallas kernels, reduce_rows(): pl.pallas_call(functools.partial(reduce_kernel, count, when), in_specs=[p...  217 us
    dot_general x16, matrix products, dot(): return lax.dot_general(a, b, (dims, ((), ())), preferred_element_type=F32)  155 us
    pallas_call x2, Pallas kernels, sum_blocks(): pl.pallas_call(functools.partial(sum_kernel, nd > 1, count), in_specs=[pl...  97.8 us
    pallas_call x1, Pallas kernels, spread(): pl.pallas_call(spread_kernel, grid=(d_local // block,), in_specs=[pl.Bloc...  25.6 us
    unnamed x122, local copies, waits for them, and re-layouts  20.1 us
  transfers between devices with their start and end apart: 8, of which 4 were waited for; matrix products, arithmetic and copies ran while one was open for 12% of the time, Pallas kernels for 35%

profile of v6, /device:TPU:0, one launch (start us, length us, event | category | flops | bytes accessed | tf_op | source)
XLA Modules:
  0.0 912.4 jit_solution(2378114476127582892)
XLA Ops:
  8.2 1.6 fusion.44
  12.7 113.9 %gather_rows.2 = (bf16[4,2,2,2,128,1536]{5,4,3,2,1,0:T(8,128)(2,1)}, bf16[1536,640]{1,0:T(8,128)(2,1)}, bf16[256,1536]{1,0:T(8,128)(2,1)}, f32[2,1536]{1,0:T(2,128)}) custom-call(bf16[2,128,768]{2,1,0:T(8,128)(2,1)} %bitcast.193, bf16[20,384,512]{2,1,0:T(8,128)(2,1)} %bitcast.165, bf16[256,768]{1,0:T(8,128)(2,1)} %refs_2_.1, f32[2,768]{1,0:T(2,128)} %pad_maximum_fusion.13.refs_3_), custom_call_target="tpu_custom_call" | custom-call | bytes 250000000 | tf_op jit(solution)/shard_map/gather_rows/pallas_call | solution.py:243
  127.5 1.6 fusion.18
  129.1 1.4 fusion.20
  130.5 2.1 constant_dynamic-slice_fusion.4
  134.5 3.3 fusion.16
  139.3 1.6 pad_maximum_fusion.10.own_ref
  140.9 11.4 %gather_ctx.1 = bf16[2,2,256,512]{3,2,1,0:T(8,128)(2,1)} custom-call(bf16[256,512]{1,0:T(8,128)(2,1)} %pad_maximum_fusion.10.own_ref), custom_call_target="tpu_custom_call" | custom-call | tf_op jit(solution)/shard_map/gather_ctx/pallas_call | solution.py:299
  152.3 1.3 fusion.69
  154.0 2.0 fusion.13
  156.1 2.6 fusion.3
  158.6 1.9 copy-done.5
  160.6 3.2 divide_convert_fusion
  163.8 2.6 copy-done.6
  166.4 1.2 convolution_convert_fusion.7
  167.6 2.6 fusion.71
  171.0 1.5 collective-permute-start
  172.7 9.8 %collective-permute-done = bf16[128,1536]{1,0:T(8,128)(2,1)S(1)} collective-permute-done((bf16[128,1536]{1,0:T(8,128)(2,1)}, bf16[128,1536]{1,0:T(8,128)(2,1)S(1)}, u32[]{:S(2)}, u32[]{:S(2)}) %collective-permute-start) | collective-permute-done | bytes 393248 | tf_op jit(solution)/shard_map/ppermute | solution.py:793
  184.4 1.3 fusion.70
  187.7 116.3 %gather_rows.3 = (bf16[4,2,2,2,2,64,1664]{6,5,4,3,2,1,0:T(8,128)(2,1)}, bf16[1536,1280]{1,0:T(8,128)(2,1)}) custom-call(bf16[2,64,1664]{2,1,0:T(8,128)(2,1)} %bitcast.184, bf16[20,384,1024]{2,1,0:T(8,128)(2,1)} %bitcast.158), custom_call_target="tpu_custom_call" | custom-call | bytes 250000000 | tf_op jit(solution)/shard_map/gather_rows/pallas_call | solution.py:243
  304.1 2.1 fusion.66
  306.1 22.6 %fusion.6 = f32[4096,1280]{0,1:T(8,128)} fusion(bf16[1536,1280]{1,0:T(8,128)(2,1)} %get-tuple-element.42, bf16[4096,1664]{1,0:T(8,128)(2,1)} %bitcast.189), kind=kOutput, calls=%fused_computation.17 | convolution fusion | flops 16106127360 | bytes 37486592 | tf_op jit(solution)/shard_map/dot_general | solution.py:760
  330.0 28.7 %multiply_convert_fusion.1 = (bf16[4096,640]{0,1:T(8,128)(2,1)}, bf16[4096,640]{0,1:T(8,128)(2,1)}, f32[4096,640]{0,1:T(8,128)}, bf16[4096,640]{0,1:T(8,128)(2,1)}) fusion(f32[4096,1280]{0,1:T(8,128)} %fusion.6, f32[4096,5]{0,1:T(8,128)S(1)} %copy.123, bf16[4096,1536]{1,0:T(8,128)(2,1)} %bitcast.161, bf16[1536,640]{1,0:T(8,128)(2,1)} %get-tuple-element.43), kind=kOutput, calls=%fused_computation.22 | convolution fusion | flops 8100249600 | bytes 61816832 | tf_op jit(solution)/shard_map/dot_general | solution.py:760
  358.7 23.6 %convolution_convert_fusion.1 = bf16[4096,1536]{1,0:T(8,128)(2,1)} fusion(bf16[1536,1280]{1,0:T(8,128)(2,1)} %get-tuple-element.42, bf16[4096,640]{0,1:T(8,128)(2,1)} %get-tuple-element.78, bf16[4096,640]{0,1:T(8,128)(2,1)} %get-tuple-element.77), kind=kOutput, calls=%fused_computation.3 | convolution fusion | flops 16133390336 | bytes 27000832 | tf_op jit(solution)/shard_map/dot_general | solution.py:760
  382.2 23.6 %fusion.10 = bf16[1536,1280]{1,0:T(8,128)(2,1)} fusion(bf16[4096,1664]{1,0:T(8,128)(2,1)} %bitcast.190, bf16[4096,640]{0,1:T(8,128)(2,1)} %get-tuple-element.78, bf16[4096,640]{0,1:T(8,128)(2,1)} %get-tuple-element.77), kind=kOutput, calls=%fused_computation.26 | convolution fusion | flops 16129064960 | bytes 27000832 | tf_op jit(solution)/shard_map/dot_general | solution.py:760
  405.9 3.8 fusion.8
  409.7 16.0 %convolution_convert_fusion.4 = bf16[1536,640]{1,0:T(8,128)(2,1)} fusion(bf16[4096,1536]{1,0:T(8,128)(2,1)} %bitcast.162, bf16[4096,640]{0,1:T(8,128)(2,1)S(1)} %fusion.8), kind=kOutput, calls=%fused_computation.36 | convolution fusion | flops 8054046720 | bytes 19791872 | tf_op jit(solution)/shard_map/dot_general | solution.py:760
  425.7 4.7 reduce_sum.132
  431.1 3.9 dynamic_update_slice.3
  435.0 118.3 %reduce_rows.2 = (f32[2,64,1664]{2,1,0:T(8,128)S(1)}, bf16[4,384,1280]{2,1,0:T(8,128)(2,1)S(1)}) custom-call(bf16[4,2,2,2,2,64,1536]{6,5,4,3,2,1,0:T(8,128)(2,1)} %bitcast.164, bf16[4,2,2,2,2,64,128]{6,5,4,3,2,1,0:T(8,128)(2,1)S(1)} %bitcast.147, bf16[4,384,1280]{2,1,0:T(8,128)(2,1)} %bitcast.175), custom_call_target="tpu_custom_call" | custom-call | bytes 250000000 | tf_op jit(solution)/shard_map/reduce_rows/pallas_call | solution.py:495
  553.4 1.9 copy-done.2
  555.8 1.4 multiply_reduce_fusion
  557.6 9.4 %all_gather.23 = bf16[256,1664]{1,0:T(8,128)(2,1)S(1)} all-gather(bf16[128,1664]{1,0:T(8,128)(2,1)S(1)} %concatenate.50), channel_id=1, replica_groups=mesh['dp'=4,'ctx'=4,'tensor'=2] {'tensor'}, dimensions={0}, use_global_device_ids=true | all-gather | bytes 1277952 | tf_op jit(solution)/shard_map/all_gather | solution.py:1017
  567.9 3.3 convolution_convert_fusion.6
  571.2 1.9 copy.125
  573.1 5.7 fusion.25
  578.8 2.2 concatenate.52
  581.1 1.5 copy.129
  582.6 8.9 fusion
  591.5 7.0 fusion.2
  598.5 2.7 copy-done.7
  601.2 2.0 fusion.26
  604.2 21.6 %sum_blocks.2 = (f32[256,512]{1,0:T(8,128)S(1)}, f32[8,128]{1,0:T(8,128)}) custom-call(bf16[1,2,2,256,512]{4,3,2,1,0:T(8,128)(2,1)S(1)} %pad_maximum_fusion.3.refs_0_, f32[8,128]{1,0:T(8,128)S(1)} %broadcast_in_dim.47.refs_1_), custom_call_target="tpu_custom_call" | custom-call | bytes 250000000 | tf_op jit(solution)/shard_map/sum_blocks/pallas_call | solution.py:675
  625.9 16.1 %convolution_convert_fusion = bf16[4096,1536]{1,0:T(8,128)(2,1)} fusion(bf16[4096,640]{0,1:T(8,128)(2,1)} %copy-done.18, bf16[1536,640]{1,0:T(8,128)(2,1)} %get-tuple-element.43), kind=kOutput, calls=%fused_computation.2 | convolution fusion | flops 8059355136 | bytes 19791872 | tf_op jit(solution)/shard_map/dot_general | solution.py:760
  642.0 98.8 %reduce_rows.3 = (f32[2,64,1536]{2,1,0:T(8,128)S(1)}, bf16[4,384,640]{2,1,0:T(8,128)(2,1)}) custom-call(bf16[4,2,2,2,2,64,1536]{6,5,4,3,2,1,0:T(8,128)(2,1)} %bitcast.163, bf16[4,384,640]{2,1,0:T(8,128)(2,1)S(1)} %bitcast.151), custom_call_target="tpu_custom_call" | custom-call | bytes 250000000 | tf_op jit(solution)/shard_map/reduce_rows/pallas_call | solution.py:495
  741.2 4.0 convolution_multiply_fusion
  745.5 3.6 fusion.14
  749.1 1.1 copy-done.28
  751.0 1.5 collective-permute-start.1
  752.5 1.5 convolution_convert_fusion.5
  756.1 6.3 collective-permute-done.1
  762.4 1.5 fusion.32
  763.9 3.1 fusion.34
  767.8 3.6 all-to-all-start
  771.4 4.4 convolution_convert_fusion.2
  778.4 4.3 all-to-all-start.1
  782.7 2.0 convolution_convert_fusion.3
  784.7 7.8 all-to-all-done.1
  792.5 76.1 %sum_blocks.3 = (f32[2,2,96,2176]{3,2,1,0:T(8,128)S(1)}, f32[2,1536]{1,0:T(2,128)S(1)}) custom-call(bf16[4,2,2,96,1280]{4,3,2,1,0:T(8,128)(2,1)} %bitcast.157, bf16[4,2,2,96,768]{4,3,2,1,0:T(8,128)(2,1)S(1)} %bitcast.146, bf16[4,2,2,96,128]{4,3,2,1,0:T(8,128)(2,1)S(1)} %bitcast.152, f32[2,1536]{1,0:T(2,128)S(1)} %pad_maximum_fusion.12.refs_3_), custom_call_target="tpu_custom_call" | custom-call | bytes 250000000 | tf_op jit(solution)/shard_map/sum_blocks/pallas_call | solution.py:675
  868.6 1.7 copy-done.3
  871.8 2.0 fusion.68
  873.8 3.2 fusion.67
  877.0 25.6 %spread.1 = (f32[20,384,1024]{2,1,0:T(8,128)}, f32[20,384,512]{2,1,0:T(8,128)}) custom-call(bf16[4,4,384,1280]{3,2,1,0:T(8,128)(2,1)} %bitcast.159, bf16[4,4,384,640]{3,2,1,0:T(8,128)(2,1)} %bitcast.166), custom_call_target="tpu_custom_call" | custom-call | tf_op jit(solution)/shard_map/spread/pallas_call | solution.py:722
  903.3 2.1 copy.162
  (194 shorter events, 26.7 us)
Async XLA Ops:
  7.2 2.7 copy-start
  7.2 127.3 %all-gather.7.cloned.1.call-start = ((), (), s32[]{:S(2)}) async-start(), calls=%async_computation.2 | async-start | bytes 4595712 | tf_op jit(solution)/shard_map/all_gather | solution.py:833
  9.8 122.7 %copy-start.47 = (s32[1,1024]{1,0:T(1,128)S(1)}, s32[1,1024]{1,0:T(1,128)}, u32[]{:S(2)}) copy-start(s32[1,1024]{1,0:T(1,128)} %param.15) | copy-start | bytes 12292
  9.8 123.2 %copy-start.46 = (s32[1024,8]{0,1:T(8,128)S(1)}, s32[1024,8]{0,1:T(8,128)}, u32[]{:S(2)}) copy-start(s32[1024,8]{0,1:T(8,128)} %param.17) | copy-start | bytes 98308
  9.9 157.7 %all-gather.9.cloned.1.call-start = ((), (), s32[]{:S(2)}) async-start(), calls=%async_computation.3 | async-start | bytes 2506752 | tf_op jit(solution)/shard_map/all_gather | solution.py:835
  10.6 122.6 %copy-start.57 = (s32[1,1024]{1,0:T(1,128)S(1)}, s32[1,1024]{1,0:T(1,128)}, u32[]{:S(2)}) copy-start(s32[1,1024]{1,0:T(1,128)} %param.16) | copy-start | bytes 12292
  10.6 730.3 %all-gather.11.cloned.1.call-start = ((), (), s32[]{:S(2)}) async-start(), calls=%async_computation.4 | async-start | bytes 19660800 | tf_op jit(solution)/shard_map/all_gather | solution.py:993
  127.5 11.2 %copy-start.42 = (f32[1536]{0:T(1024)}, f32[1536]{0:T(1024)S(1)}, u32[]{:S(2)}) copy-start(f32[1536]{0:T(1024)S(1)} %get-tuple-element.70) | copy-start | bytes 18436
  127.5 55.9 %copy-start.38 = (f32[1536]{0:T(1024)}, f32[1536]{0:T(1024)S(1)}, u32[]{:S(2)}) copy-start(f32[1536]{0:T(1024)S(1)} %get-tuple-element.69) | copy-start | bytes 18436
  130.4 8.5 copy-start.17
  133.0 25.6 %copy-start.10 = (pred[256,1024]{0,1:T(8,128)(4,1)}, pred[256,1024]{0,1:T(8,128)(4,1)S(1)}, u32[]{:S(2)}) copy-start(pred[256,1024]{0,1:T(8,128)(4,1)S(1)} %fusion.28) | copy-start | bytes 786436
  134.5 4.6 copy-start.34
  153.8 10.0 %copy-start.15 = (bf16[1024,256]{0,1:T(8,128)(2,1)}, bf16[1024,256]{0,1:T(8,128)(2,1)S(1)}, u32[]{:S(2)}) copy-start(bf16[1024,256]{0,1:T(8,128)(2,1)S(1)} %copy.117) | copy-start | bytes 1572868
  154.0 2.0 copy-start.19
  154.0 2.0 copy-start.21
  156.0 4.5 copy-start.5
  156.1 4.5 copy-start.36
  160.6 3.2 copy-start.40
  163.7 2.6 copy-start.6
  163.7 18.9 %copy-start.12 = (bf16[256,1536]{1,0:T(8,128)(2,1)S(1)}, bf16[256,1536]{1,0:T(8,128)(2,1)}, u32[]{:S(2)}) copy-start(bf16[256,1536]{1,0:T(8,128)(2,1)} %get-tuple-element.37) | copy-start | bytes 2359300
  167.5 136.5 %copy-start.23 = (bf16[4,64,3,256]{3,1,2,0:T(8,128)(2,1)}, bf16[4,64,3,256]{3,1,2,0:T(8,128)(2,1)S(1)}, u32[]{:S(2)}) copy-start(bf16[4,64,3,256]{3,1,2,0:T(8,128)(2,1)S(1)} %convolution_convert_fusion.7) | copy-start | bytes 1179652
  171.0 11.6 %collective-permute-start = (bf16[128,1536]{1,0:T(8,128)(2,1)}, bf16[128,1536]{1,0:T(8,128)(2,1)S(1)}, u32[]{:S(2)}, u32[]{:S(2)}) collective-permute-start(bf16[128,1536]{1,0:T(8,128)(2,1)} %dynamic-slice_convert_fusion.1), channel_id=1, source_target_pairs={{0,1},{1,0},{2,3},{3,2},{4,5},{5,4},{6,7},{7,6},{8,9},{9,8},{10,11... | collective-permute-start | bytes 1179656 | tf_op jit(solution)/shard_map/ppermute | solution.py:793
  183.4 0.9 copy-start.55
  183.4 120.6 %copy-start.48 = (f32[128]{0:T(128)}, f32[128]{0:T(128)S(1)}, u32[]{:S(2)}) copy-start(f32[128]{0:T(128)S(1)} %add_rsqrt_fusion.2) | copy-start | bytes 1540
  185.7 118.3 %copy-start.32 = (f32[128,40]{1,0:T(8,128)}, f32[128,40]{1,0:T(8,128)S(1)}, u32[]{:S(2)}) copy-start(f32[128,40]{1,0:T(8,128)S(1)} %get-tuple-element.104) | copy-start | bytes 61444
  185.7 118.3 %copy-start.50 = (f32[128]{0:T(128)}, f32[128]{0:T(128)S(1)}, u32[]{:S(2)}) copy-start(f32[128]{0:T(128)S(1)} %get-tuple-element.103) | copy-start | bytes 1540
  185.9 118.1 %copy-start.52 = (f32[128]{0:T(128)}, f32[128]{0:T(128)S(1)}, u32[]{:S(2)}) copy-start(f32[128]{0:T(128)S(1)} %fusion.51) | copy-start | bytes 1540
  409.6 16.0 %copy-start.18 = (bf16[4096,640]{0,1:T(8,128)(2,1)}, bf16[4096,640]{0,1:T(8,128)(2,1)S(1)}, u32[]{:S(2)}) copy-start(bf16[4096,640]{0,1:T(8,128)(2,1)S(1)} %fusion.8) | copy-start | bytes 15728644
  434.9 120.4 %copy-start.37 = (f32[4,3,256]{2,1,0:T(4,128)S(1)}, f32[4,3,256]{2,1,0:T(4,128)}, u32[]{:S(2)}) copy-start(f32[4,3,256]{2,1,0:T(4,128)} %copy-done.36) | copy-start | bytes 36868
  435.0 120.4 %copy-start.41 = (f32[4,3,256]{2,1,0:T(4,128)S(1)}, f32[4,3,256]{2,1,0:T(4,128)}, u32[]{:S(2)}) copy-start(f32[4,3,256]{2,1,0:T(4,128)} %copy-done.40) | copy-start | bytes 36868
  435.0 120.4 %copy-start.33 = (f32[128,40]{1,0:T(8,128)S(1)}, f32[128,40]{1,0:T(8,128)}, u32[]{:S(2)}) copy-start(f32[128,40]{1,0:T(8,128)} %copy-done.32) | copy-start | bytes 61444
  435.0 120.4 %copy-start.45 = (pred[128,40]{1,0:T(8,128)(4,1)S(1)}, pred[128,40]{1,0:T(8,128)(4,1)}, u32[]{:S(2)}) copy-start(pred[128,40]{1,0:T(8,128)(4,1)} %get-tuple-element.105) | copy-start | bytes 15364
  435.0 120.4 %copy-start.51 = (f32[128]{0:T(128)S(1)}, f32[128]{0:T(128)}, u32[]{:S(2)}) copy-start(f32[128]{0:T(128)} %copy-done.50) | copy-start | bytes 1540
  435.0 120.4 %copy-start.53 = (f32[128]{0:T(128)S(1)}, f32[128]{0:T(128)}, u32[]{:S(2)}) copy-start(f32[128]{0:T(128)} %copy-done.52) | copy-start | bytes 1540
  435.0 120.7 %copy-start.9 = (f32[128,1536]{1,0:T(8,128)S(1)}, f32[128,1536]{1,0:T(8,128)}, u32[]{:S(2)}) copy-start(f32[128,1536]{1,0:T(8,128)} %copy-done.8) | copy-start | bytes 2359300
  435.0 120.7 %copy-start.39 = (f32[1536]{0:T(1024)S(1)}, f32[1536]{0:T(1024)}, u32[]{:S(2)}) copy-start(f32[1536]{0:T(1024)} %copy-done.38) | copy-start | bytes 18436
  435.0 120.7 %copy-start.49 = (f32[128]{0:T(128)S(1)}, f32[128]{0:T(128)}, u32[]{:S(2)}) copy-start(f32[128]{0:T(128)} %copy-done.48) | copy-start | bytes 1540
  553.4 1.9 copy-start.2
  555.2 2.0 copy-start.56
  555.2 2.0 copy-start.25
  555.3 321.7 %all-gather.13.cloned.1.call-start = ((), (), s32[]{:S(2)}) async-start(), calls=%async_computation.5 | async-start | bytes 9830400 | tf_op jit(solution)/shard_map/all_gather | solution.py:1056
  557.2 21.6 %copy-start.14 = (f32[128,1536]{1,0:T(8,128)}, f32[128,1536]{1,0:T(8,128)S(1)}, u32[]{:S(2)}) copy-start(f32[128,1536]{1,0:T(8,128)S(1)} %get-tuple-element.106) | copy-start | bytes 2359300
  567.0 0.9 copy-start.26
  567.9 14.6 %copy-start.11 = (pred[256,1024]{0,1:T(8,128)(4,1)S(1)}, pred[256,1024]{0,1:T(8,128)(4,1)}, u32[]{:S(2)}) copy-start(pred[256,1024]{0,1:T(8,128)(4,1)} %copy-done.10) | copy-start | bytes 786436
  567.9 14.7 %copy-start.16 = (bf16[1024,256]{0,1:T(8,128)(2,1)S(1)}, bf16[1024,256]{0,1:T(8,128)(2,1)}, u32[]{:S(2)}) copy-start(bf16[1024,256]{0,1:T(8,128)(2,1)} %copy-done.15) | copy-start | bytes 1572868
  591.5 9.7 %copy-start.22 = (bf16[256,12,64]{0,2,1:T(8,128)(2,1)S(1)}, bf16[256,12,64]{0,2,1:T(8,128)(2,1)}, u32[]{:S(2)}) copy-start(bf16[256,12,64]{0,2,1:T(8,128)(2,1)} %copy-done.21) | copy-start | bytes 1179652
  598.4 2.7 copy-start.7
  625.8 16.1 %copy-start.4 = (bf16[1536,640]{1,0:T(8,128)(2,1)S(1)}, bf16[1536,640]{1,0:T(8,128)(2,1)}, u32[]{:S(2)}) copy-start(bf16[1536,640]{1,0:T(8,128)(2,1)} %convolution_convert_fusion.4) | copy-start | bytes 5898244
  642.0 99.2 %copy-start.20 = (bf16[1024,256]{0,1:T(8,128)(2,1)S(1)}, bf16[1024,256]{0,1:T(8,128)(2,1)}, u32[]{:S(2)}) copy-start(bf16[1024,256]{0,1:T(8,128)(2,1)} %copy-done.19) | copy-start | bytes 1572868
  740.8 4.3 copy-start.35
  740.8 4.3 copy-start.44
  745.4 10.7 %copy-start.54 = (f32[128]{0:T(128)S(1)}, f32[128]{0:T(128)}, u32[]{:S(2)}) copy-start(f32[128]{0:T(128)} %get-tuple-element.95) | copy-start | bytes 1540
  745.4 17.0 %copy-start.13 = (bf16[256,1536]{1,0:T(8,128)(2,1)S(1)}, bf16[256,1536]{1,0:T(8,128)(2,1)}, u32[]{:S(2)}) copy-start(bf16[256,1536]{1,0:T(8,128)(2,1)} %get-tuple-element.37) | copy-start | bytes 2359300
  745.4 17.0 %copy-start.43 = (f32[1536]{0:T(1024)S(1)}, f32[1536]{0:T(1024)}, u32[]{:S(2)}) copy-start(f32[1536]{0:T(1024)} %copy-done.42) | copy-start | bytes 18436
  745.4 8.6 copy-start.29
  749.0 1.1 copy-start.28
  751.0 11.4 %collective-permute-start.1 = (bf16[128,1536]{1,0:T(8,128)(2,1)}, bf16[128,1536]{1,0:T(8,128)(2,1)}, u32[]{:S(2)}, u32[]{:S(2)}) collective-permute-start(bf16[128,1536]{1,0:T(8,128)(2,1)} %dynamic-slice_convert_fusion), channel_id=1, source_target_pairs={{0,1},{1,0},{2,3},{3,2},{4,5},{5,4},{6,7},{7,6},{8,9},{9,8},{10,11... | collective-permute-start | bytes 1179656 | tf_op jit(solution)/shard_map/ppermute | solution.py:793
  767.0 8.8 copy-start.27
  767.8 14.9 %copy-start.24 = (bf16[4,64,3,256]{3,1,2,0:T(8,128)(2,1)S(1)}, bf16[4,64,3,256]{3,1,2,0:T(8,128)(2,1)}, u32[]{:S(2)}) copy-start(bf16[4,64,3,256]{3,1,2,0:T(8,128)(2,1)} %copy-done.23) | copy-start | bytes 1179652
  767.8 9.8 %all-to-all-start = ((bf16[128,2,768]{2,0,1:T(8,128)(2,1)}), bf16[128,2,768]{2,0,1:T(8,128)(2,1)S(1)}, u32[]{:S(2)}, u32[]{:S(2)}) async-start(bf16[128,2,768]{2,0,1:T(8,128)(2,1)} %bitcast.145), calls=%async_computation | async-start | bytes 786432 | tf_op jit(solution)/shard_map/all_to_all | solution.py:1060
  778.4 14.1 %all-to-all-start.1 = ((f32[128,2,768]{2,0,1:T(8,128)}), f32[128,2,768]{2,0,1:T(8,128)}, u32[]{:S(2)}, u32[]{:S(2)}) async-start(f32[128,2,768]{2,0,1:T(8,128)} %bitcast.144), calls=%async_computation.1 | async-start | bytes 1572864 | tf_op jit(solution)/shard_map/all_to_all | solution.py:1082
  868.6 1.7 copy-start.3
  877.0 25.6 %copy-start.31 = (bf16[128,2,768]{2,0,1:T(8,128)(2,1)S(1)}, bf16[128,2,768]{2,0,1:T(8,128)(2,1)}, u32[]{:S(2)}) copy-start(bf16[128,2,768]{2,0,1:T(8,128)(2,1)} %copy-done.30) | copy-start | bytes 1179652
  877.0 28.4 %copy-start.1 = (bf16[384,768]{1,0:T(8,128)(2,1)S(1)}, bf16[384,768]{1,0:T(8,128)(2,1)}, u32[]{:S(2)}) copy-start(bf16[384,768]{1,0:T(8,128)(2,1)} %param.22) | copy-start | bytes 1769476
  (2 other events, 1.6 us)
Sparse Core Ops, SparseCore 0:
  10.9 88.7 all-gather.6
  102.5 42.9 all-gather.8
  555.4 132.0 all-gather.10
  741.0 60.9 all-gather.12
